TPU v7x, 32 devices: a whole 2x2x4 slice. The times are simulated.
32 devices in a mesh: dp: 8 (over z, x), mp: 4 (over y, core).
Axes of the slice: x: 2, y: 2, z: 4, core: 2. Of those that a mesh axis runs over, the one named last changes fastest.
Arguments:
- tokens: bfloat16 [2, 2, 8192, 768], P(None, None, ('dp', 'mp')), may hold values from -6 to 6
- cotangent: bfloat16 [2, 2, 8192, 768], P(None, None, ('dp', 'mp')), may hold values from -6 to 6
- lengths: int32 [2, 8, 3], P(None, 'dp'), may hold values from 1 to 768, 1024 in all within a row
- norm1_gain: bfloat16 [2, 768], replicated, may hold values from 0.5 to 1.5
- norm1_shift: bfloat16 [2, 768], replicated, may hold values from -1.25 to 1.25
- query_key_value_weight: bfloat16 [2, 768, 3, 768], P(None, 'dp', None, 'mp'), may hold values from -0.21875 to 0.21875
- query_key_value_bias: bfloat16 [2, 3, 768], P(None, None, 'mp'), may hold values from -1.25 to 1.25
- out_weight: bfloat16 [2, 768, 768], P(None, 'mp', 'dp'), may hold values from -1.5 to 1.5
- out_bias: bfloat16 [2, 768], replicated, may hold values from -1.25 to 1.25
- norm2_gain: bfloat16 [2, 768], replicated, may hold values from 0.5 to 1.5
- norm2_shift: bfloat16 [2, 768], replicated, may hold values from -1.25 to 1.25
- normy_gain: bfloat16 [2, 768], replicated, may hold values from 0.5 to 1.5
- normy_shift: bfloat16 [2, 768], replicated, may hold values from -1.25 to 1.25
- cross_q_weight: bfloat16 [2, 768, 768], P(None, 'dp', 'mp'), may hold values from -0.21875 to 0.21875
- cross_q_bias: bfloat16 [2, 768], P(None, 'mp'), may hold values from -1.25 to 1.25
- cross_key_value_weight: bfloat16 [2, 768, 2, 768], P(None, 'dp', None, 'mp'), may hold values from -0.21875 to 0.21875
- cross_key_value_bias: bfloat16 [2, 2, 768], P(None, None, 'mp'), may hold values from -1.25 to 1.25
- cross_out_weight: bfloat16 [2, 768, 768], P(None, 'mp', 'dp'), may hold values from -1.5 to 1.5
- cross_out_bias: bfloat16 [2, 768], replicated, may hold values from -1.25 to 1.25
- norm3_gain: bfloat16 [2, 768], replicated, may hold values from 0.5 to 1.5
- norm3_shift: bfloat16 [2, 768], replicated, may hold values from -1.25 to 1.25
- up_weight: bfloat16 [2, 768, 3072], P(None, 'dp', 'mp'), may hold values from -0.21875 to 0.21875
- up_bias: bfloat16 [2, 3072], P(None, 'mp'), may hold values from -1.25 to 1.25
- down_weight: bfloat16 [2, 3072, 768], P(None, 'mp', 'dp'), may hold values from -0.109375 to 0.109375
- down_bias: bfloat16 [2, 768], replicated, may hold values from -1.25 to 1.25
Outputs:
- block_output: bfloat16 [2, 2, 8192, 768], P(None, None, ('dp', 'mp'))
- input_grad: float32 [2, 2, 8192, 768], P(None, None, ('dp', 'mp'))
- norm1_gain_grad: float32 [2, 768], replicated
- norm1_shift_grad: float32 [2, 768], replicated
- qkv_weight_grad: float32 [2, 768, 3, 768], P(None, 'dp', None, 'mp')
- qkv_bias_grad: float32 [2, 3, 768], P(None, None, 'mp')
- out_weight_grad: float32 [2, 768, 768], P(None, 'mp', 'dp')
- out_bias_grad: float32 [2, 768], replicated
- norm2_gain_grad: float32 [2, 768], replicated
- norm2_shift_grad: float32 [2, 768], replicated
- normy_gain_grad: float32 [2, 768], replicated
- normy_shift_grad: float32 [2, 768], replicated
- cross_q_weight_grad: float32 [2, 768, 768], P(None, 'dp', 'mp')
- cross_q_bias_grad: float32 [2, 768], P(None, 'mp')
- cross_kv_weight_grad: float32 [2, 768, 2, 768], P(None, 'dp', None, 'mp')
- cross_kv_bias_grad: float32 [2, 2, 768], P(None, None, 'mp')
- cross_out_weight_grad: float32 [2, 768, 768], P(None, 'mp', 'dp')
- cross_out_bias_grad: float32 [2, 768], replicated
- norm3_gain_grad: float32 [2, 768], replicated
- norm3_shift_grad: float32 [2, 768], replicated
- up_weight_grad: float32 [2, 768, 3072], P(None, 'dp', 'mp')
- up_bias_grad: float32 [2, 3072], P(None, 'mp')
- down_weight_grad: float32 [2, 3072, 768], P(None, 'mp', 'dp')
- down_bias_grad: float32 [2, 768], replicated
Inputs may be any that keep to these rules, and one draw needn't show every extreme that they name: In every buffer the 3 image lengths sum to 1024 and the longest is exactly 768.
All inputs are finite; a program needn't handle non-finite values.
Results may differ from a plain program's by a relative error of at most 0.015.
Values may be sent and summed in bfloat16 or wider, within the bound.
No kernel may reach another device: no remote copies, remote signals or barrier semaphores. Data moves between devices by JAX's collectives and lax.ppermute only.
A program may use at most 448 MiB of HBM per device.

v0:
```python
import jax
import jax.numpy as jnp
from jax import lax
from jax.sharding import PartitionSpec as P

HEAD_DIM = 64


norm_epsilon = 1e-06


def split_up(shard, dim, length):
    dims = shard.shape
    parts = shard.reshape(*dims[:dim], length, dims[dim] // length, *dims[dim + 1 :])
    return jnp.moveaxis(parts, dim, 0)


def sum_at_owner(shard, axis, dim):
    parts = split_up(shard, dim, lax.axis_size(axis))
    arrived = lax.all_to_all(parts, axis, split_axis=0, concat_axis=0, tiled=True)
    return arrived.astype(jnp.float32).sum(axis=0)


def in_one_piece(arrays, axis, dim, along):
    widths = [a.shape[along] for a in arrays]
    both = jnp.concatenate(arrays, axis=along)
    whole = sum_at_owner(both, axis, dim)
    return tuple(jnp.split(whole, [sum(widths[:k]) for k in range(1, len(widths))], axis=along))


def layer_norm(rows, gain, shift):
    centre = jnp.mean(rows, -1, keepdims=True)
    centred = rows - centre
    spread = jnp.mean(centred * centred, -1, keepdims=True)
    return centred * lax.rsqrt(spread + norm_epsilon) * gain + shift


def rope_turn(vectors, cosine, sine):
    half = vectors.shape[-1] // 2
    first = vectors[..., :half]
    second = vectors[..., half:]
    return jnp.concatenate([first * cosine - second * sine, second * cosine + first * sine], -1)


def tables(image_sizes, count, half):
    places = jnp.arange(count, dtype=jnp.int32)
    ends = jnp.cumsum(image_sizes)
    passed = places[:, None] >= ends[None, :]
    segment = jnp.sum(passed.astype(jnp.int32), -1)
    start = jnp.sum(jnp.where(passed, image_sizes[None, :], 0), -1)
    place = (places - start).astype(jnp.float32)
    freqs = 100.0 ** (-(jnp.arange(half, dtype=jnp.float32) / half))
    angles = place[:, None] * freqs[None, :]
    return (segment, jnp.cos(angles)[:, None, :], jnp.sin(angles)[:, None, :])


def gelu_exact(values):
    return jax.nn.gelu(values, approximate=False)


def fetch(matrices):
    (
        query_key_value_weight,
        cross_q_weight,
        cross_key_value_weight,
        up_weight,
        out_weight,
        cross_out_weight,
        down_weight,
        query_key_value_bias,
        cross_q_bias,
        cross_key_value_bias,
        up_bias,
    ) = matrices
    query_key_value_weight, cross_q_weight, cross_key_value_weight, up_weight = (
        lax.all_gather(query_key_value_weight, "dp", axis=1, tiled=True),
        lax.all_gather(cross_q_weight, "dp", axis=1, tiled=True),
        lax.all_gather(cross_key_value_weight, "dp", axis=1, tiled=True),
        lax.all_gather(up_weight, "dp", axis=1, tiled=True),
    )
    out_weight, cross_out_weight, down_weight = (
        lax.all_gather(out_weight, "dp", axis=2, tiled=True),
        lax.all_gather(cross_out_weight, "dp", axis=2, tiled=True),
        lax.all_gather(down_weight, "dp", axis=2, tiled=True),
    )
    return (
        query_key_value_weight,
        cross_q_weight,
        cross_key_value_weight,
        up_weight,
        out_weight,
        cross_out_weight,
        down_weight,
        query_key_value_bias,
        cross_q_bias,
        cross_key_value_bias,
        up_bias,
    )


def settle(grads):
    (
        grad_qkv,
        grad_query,
        grad_pair,
        grad_up,
        grad_out,
        grad_cross,
        grad_down,
        bias_qkv,
        bias_query,
        bias_pair,
        bias_up,
    ) = grads
    grad_qkv, grad_query, grad_pair, grad_up = (
        lax.psum_scatter(grad_qkv, "dp", scatter_dimension=1, tiled=True),
        lax.psum_scatter(grad_query, "dp", scatter_dimension=1, tiled=True),
        lax.psum_scatter(grad_pair, "dp", scatter_dimension=1, tiled=True),
        lax.psum_scatter(grad_up, "dp", scatter_dimension=1, tiled=True),
    )
    grad_out, grad_cross, grad_down = in_one_piece(
        (
            grad_out.astype(jnp.bfloat16),
            grad_cross.astype(jnp.bfloat16),
            grad_down.astype(jnp.bfloat16),
        ),
        "dp",
        2,
        1,
    )
    return (
        grad_qkv,
        grad_query,
        grad_pair,
        grad_up,
        grad_out,
        grad_cross,
        grad_down,
        bias_qkv,
        bias_query,
        bias_pair,
        bias_up,
    )


def widen(rows):
    wide = lax.all_gather(rows, "mp", axis=0, tiled=True)
    return wide


def narrow(terms):
    total = lax.psum_scatter(terms, "mp", scatter_dimension=0, tiled=True)
    return total


def widen_grad(rows):
    wide = lax.all_gather(rows, "mp", axis=0, tiled=True)
    return wide


def narrow_grad(terms):
    total = lax.psum_scatter(terms, "mp", scatter_dimension=0, tiled=True)
    return total


def share_pair(keys, values):
    shared = (keys, values)
    return shared


def settle_pair(key_grad, value_grad):
    settled = (key_grad, value_grad)
    return settled


def block_scores(query_block, segment_block, keys, key_segment, scale):
    scores = (
        jnp.einsum("qhc,khc->hqk", query_block, keys, preferred_element_type=jnp.float32) * scale
    )
    same = segment_block[:, None] == key_segment[None, :]
    return jnp.where(same[None], scores, -1e30)


def attend(queries, keys, values, query_segment, key_segment):
    query_rows, heads, depth = queries.shape
    block_rows = min(512, query_rows)
    blocks = query_rows // block_rows
    scale = depth ** (-0.5)
    query_blocks = queries.reshape(blocks, block_rows, heads, depth)
    segment_blocks = query_segment.reshape(blocks, block_rows)

    def one_block(item):
        query_block, segment_block = item
        scores = block_scores(query_block, segment_block, keys, key_segment, scale)
        top = jnp.max(scores, -1, keepdims=True)
        raised = jnp.exp(scores - top)
        total = jnp.sum(raised, -1, keepdims=True)
        probs = (raised / total).astype(jnp.bfloat16)
        result = jnp.einsum("hqk,khc->qhc", probs, values, preferred_element_type=jnp.float32)
        return (result, (top + jnp.log(total))[..., 0])

    results, log_totals = lax.map(one_block, (query_blocks, segment_blocks))
    return (results.reshape(query_rows, heads * depth), log_totals)


def attend_back(queries, keys, values, query_segment, key_segment, log_totals, attended_grad):
    query_rows, heads, depth = queries.shape
    block_rows = min(512, query_rows)
    blocks = query_rows // block_rows
    scale = depth ** (-0.5)
    query_blocks = queries.reshape(blocks, block_rows, heads, depth)
    segment_blocks = query_segment.reshape(blocks, block_rows)
    grad_blocks = attended_grad.reshape(blocks, block_rows, heads, depth)

    def back_block(carry, item):
        key_acc, value_acc = carry
        query_block, segment_block, log_block, grad_block = item
        scores = block_scores(query_block, segment_block, keys, key_segment, scale)
        probs = jnp.exp(scores - log_block[..., None])
        value_acc = value_acc + jnp.einsum(
            "hqk,qhc->khc",
            probs.astype(jnp.bfloat16),
            grad_block,
            preferred_element_type=jnp.float32,
        )
        prob_grad = jnp.einsum(
            "qhc,khc->hqk", grad_block, values, preferred_element_type=jnp.float32
        )
        inner = jnp.sum(prob_grad * probs, -1, keepdims=True)
        score_grad = (probs * (prob_grad - inner)).astype(jnp.bfloat16)
        query_grad = (
            jnp.einsum("hqk,khc->qhc", score_grad, keys, preferred_element_type=jnp.float32) * scale
        )
        key_acc = (
            key_acc
            + jnp.einsum(
                "hqk,qhc->khc", score_grad, query_block, preferred_element_type=jnp.float32
            )
            * scale
        )
        return ((key_acc, value_acc), query_grad)

    empty = jnp.zeros(keys.shape, jnp.float32)
    (key_grad, value_grad), query_grads = lax.scan(
        back_block, (empty, empty), (query_blocks, segment_blocks, log_totals, grad_blocks)
    )
    return (query_grads.reshape(query_rows, heads, depth), key_grad, value_grad)


def view_pass(rows, other_rows, cot_rows, fetched, norms, view, layout):
    (
        qkv_all,
        query_all,
        pair_all,
        up_all,
        out_all,
        cross_all,
        down_all,
        qkv_bias_all,
        query_bias_all,
        pair_bias_all,
        up_bias_all,
    ) = fetched
    query_key_value_gathered = qkv_all[view]
    cross_q_full = query_all[view]
    cross_key_value_gathered = pair_all[view]
    up_full = up_all[view]
    out_full = out_all[view]
    cross_out_full = cross_all[view]
    down_full = down_all[view]
    qkv_shift = qkv_bias_all[view].astype(jnp.float32)
    cross_q_shift = query_bias_all[view].astype(jnp.float32)
    cross_kv_shift = pair_bias_all[view].astype(jnp.float32)
    up_shift = up_bias_all[view].astype(jnp.float32)
    (
        gain_one,
        shift_one,
        out_shift,
        gain_two,
        shift_two,
        gain_side,
        shift_side,
        cross_shift,
        gain_three,
        shift_three,
        down_shift,
    ) = tuple((entry[view] for entry in norms))
    segment, row_segment, row_cosine, row_sine = layout
    buffer_rows = segment.shape[0]
    heads_here = query_key_value_gathered.shape[2] // HEAD_DIM

    def turn(vectors):
        return rope_turn(vectors, row_cosine, row_sine)

    normalized_rows, pull_one = jax.vjp(layer_norm, rows, gain_one, shift_one)
    normalized_rows_wide = widen(normalized_rows.astype(jnp.bfloat16))
    span = normalized_rows_wide.shape[0]
    blended_output = (
        jnp.einsum(
            "rj,jqw->rqw",
            normalized_rows_wide,
            query_key_value_gathered,
            preferred_element_type=jnp.float32,
        )
        + qkv_shift
    )
    query_f, pull_query = jax.vjp(turn, blended_output[:, 0].reshape(span, heads_here, HEAD_DIM))
    key_f, pull_key = jax.vjp(turn, blended_output[:, 1].reshape(span, heads_here, HEAD_DIM))
    queries = query_f.astype(jnp.bfloat16)
    keys_all, values_all = share_pair(
        key_f.astype(jnp.bfloat16).reshape(span, -1), blended_output[:, 2].astype(jnp.bfloat16)
    )
    keys_turned = keys_all.reshape(buffer_rows, heads_here, HEAD_DIM)
    values = values_all.reshape(buffer_rows, heads_here, HEAD_DIM)
    attended_f, log_self = attend(queries, keys_turned, values, row_segment, segment)
    attended = attended_f.astype(jnp.bfloat16)
    middle = (
        rows + narrow(jnp.dot(attended, out_full, preferred_element_type=jnp.float32)) + out_shift
    )
    normed_two, pull_two = jax.vjp(layer_norm, middle, gain_two, shift_two)
    normed_two_wide = widen(normed_two.astype(jnp.bfloat16))
    source_tokens, pull_side = jax.vjp(layer_norm, other_rows, gain_side, shift_side)
    source_tokens_wide = widen(source_tokens.astype(jnp.bfloat16))
    cross_query = (
        jnp.dot(normed_two_wide, cross_q_full, preferred_element_type=jnp.float32) + cross_q_shift
    )
    cross_query_f, pull_cross_query = jax.vjp(turn, cross_query.reshape(span, heads_here, HEAD_DIM))
    cross_queries = cross_query_f.astype(jnp.bfloat16)
    cross_blended = (
        jnp.einsum(
            "rj,jqw->rqw",
            source_tokens_wide,
            cross_key_value_gathered,
            preferred_element_type=jnp.float32,
        )
        + cross_kv_shift
    )
    cross_key_f, pull_cross_key = jax.vjp(
        turn, cross_blended[:, 0].reshape(span, heads_here, HEAD_DIM)
    )
    cross_keys_all, cross_values_all = share_pair(
        cross_key_f.astype(jnp.bfloat16).reshape(span, -1), cross_blended[:, 1].astype(jnp.bfloat16)
    )
    cross_keys = cross_keys_all.reshape(buffer_rows, heads_here, HEAD_DIM)
    cross_values = cross_values_all.reshape(buffer_rows, heads_here, HEAD_DIM)
    cross_f, log_cross = attend(cross_queries, cross_keys, cross_values, row_segment, segment)
    cross_attended = cross_f.astype(jnp.bfloat16)
    middle_two = (
        middle
        + narrow(jnp.dot(cross_attended, cross_out_full, preferred_element_type=jnp.float32))
        + cross_shift
    )
    normed_three, pull_three = jax.vjp(layer_norm, middle_two, gain_three, shift_three)
    normed_three_wide = widen(normed_three.astype(jnp.bfloat16))
    hidden_in = jnp.dot(normed_three_wide, up_full, preferred_element_type=jnp.float32) + up_shift
    hidden_f, pull_gelu = jax.vjp(gelu_exact, hidden_in)
    hidden = hidden_f.astype(jnp.bfloat16)
    output = (
        middle_two
        + narrow(jnp.dot(hidden, down_full, preferred_element_type=jnp.float32))
        + down_shift
    ).astype(jnp.bfloat16)
    cot_wide = widen_grad(cot_rows)
    down_grad = jnp.einsum("tf,td->fd", hidden, cot_wide, preferred_element_type=jnp.float32)
    hidden_grad = jnp.einsum("td,fd->tf", cot_wide, down_full, preferred_element_type=jnp.float32)
    hidden_in_grad = pull_gelu(hidden_grad)[0].astype(jnp.bfloat16)
    up_bias_grad = jnp.sum(hidden_in_grad.astype(jnp.float32), 0)
    up_grad = jnp.einsum(
        "td,tf->df", normed_three_wide, hidden_in_grad, preferred_element_type=jnp.float32
    )
    three_terms = jnp.einsum(
        "tf,df->td", hidden_in_grad, up_full, preferred_element_type=jnp.float32
    )
    middle_two_part, gain_three_grad, shift_three_grad = pull_three(narrow_grad(three_terms))
    cot_float = cot_rows.astype(jnp.float32)
    middle_two_grad = cot_float + middle_two_part
    cross_grad = middle_two_grad.astype(jnp.bfloat16)
    cross_wide = widen_grad(cross_grad)
    cross_out_grad = jnp.einsum(
        "te,td->ed", cross_attended, cross_wide, preferred_element_type=jnp.float32
    )
    cross_attended_grad = jnp.einsum(
        "td,ed->te", cross_wide, cross_out_full, preferred_element_type=jnp.float32
    ).astype(jnp.bfloat16)
    cross_query_grads, cross_key_grad, cross_value_grad = attend_back(
        cross_queries,
        cross_keys,
        cross_values,
        row_segment,
        segment,
        log_cross,
        cross_attended_grad.reshape(span, heads_here, HEAD_DIM),
    )
    cross_key_grad, cross_value_grad = settle_pair(
        cross_key_grad.reshape(buffer_rows, -1), cross_value_grad.reshape(buffer_rows, -1)
    )
    cross_query_grad = pull_cross_query(cross_query_grads)[0].reshape(span, -1).astype(jnp.bfloat16)
    cross_key_back = pull_cross_key(cross_key_grad.reshape(span, heads_here, HEAD_DIM))[0].reshape(
        span, -1
    )
    cross_blended_gradient = jnp.stack([cross_key_back, cross_value_grad], 1).astype(jnp.bfloat16)
    cross_q_bias_grad = jnp.sum(cross_query_grad.astype(jnp.float32), 0)
    cross_kv_bias_grad = jnp.sum(cross_blended_gradient.astype(jnp.float32), 0)
    cross_q_grad = jnp.einsum(
        "td,te->de", normed_two_wide, cross_query_grad, preferred_element_type=jnp.float32
    )
    cross_kv_grad = jnp.einsum(
        "vi,vaw->iaw",
        source_tokens_wide,
        cross_blended_gradient,
        preferred_element_type=jnp.float32,
    )
    two_terms = jnp.einsum(
        "te,de->td", cross_query_grad, cross_q_full, preferred_element_type=jnp.float32
    )
    side_terms = jnp.einsum(
        "jim,qim->jq",
        cross_blended_gradient,
        cross_key_value_gathered,
        preferred_element_type=jnp.float32,
    )
    both_totals = narrow_grad(jnp.stack([two_terms, side_terms], 1))
    middle_part, gain_two_grad, shift_two_grad = pull_two(both_totals[:, 0])
    side_grad, gain_side_grad, shift_side_grad = pull_side(both_totals[:, 1])
    middle_grad = middle_two_grad + middle_part
    branch_grad = middle_grad.astype(jnp.bfloat16)
    branch_wide = widen_grad(branch_grad)
    out_grad = jnp.einsum("te,td->ed", attended, branch_wide, preferred_element_type=jnp.float32)
    attended_grad = jnp.einsum(
        "td,ed->te", branch_wide, out_full, preferred_element_type=jnp.float32
    ).astype(jnp.bfloat16)
    query_grads, key_grad, value_grad = attend_back(
        queries,
        keys_turned,
        values,
        row_segment,
        segment,
        log_self,
        attended_grad.reshape(span, heads_here, HEAD_DIM),
    )
    key_grad, value_grad = settle_pair(
        key_grad.reshape(buffer_rows, -1), value_grad.reshape(buffer_rows, -1)
    )
    query_back = pull_query(query_grads)[0].reshape(span, -1)
    key_back = pull_key(key_grad.reshape(span, heads_here, HEAD_DIM))[0].reshape(span, -1)
    blended_gradient = jnp.stack([query_back, key_back, value_grad], 1).astype(jnp.bfloat16)
    qkv_bias_grad = jnp.sum(blended_gradient.astype(jnp.float32), 0)
    qkv_grad = jnp.einsum(
        "vi,vaw->iaw", normalized_rows_wide, blended_gradient, preferred_element_type=jnp.float32
    )
    first_gain_terms = jnp.einsum(
        "jim,qim->jq",
        blended_gradient,
        query_key_value_gathered,
        preferred_element_type=jnp.float32,
    )
    rows_part, gain_one_grad, shift_one_grad = pull_one(narrow_grad(first_gain_terms))
    own_grad = middle_grad + rows_part
    small = (
        gain_one_grad,
        shift_one_grad,
        jnp.sum(branch_grad.astype(jnp.float32), 0),
        gain_two_grad,
        shift_two_grad,
        gain_side_grad,
        shift_side_grad,
        jnp.sum(cross_grad.astype(jnp.float32), 0),
        gain_three_grad,
        shift_three_grad,
        jnp.sum(cot_float, 0),
    )
    large = (
        qkv_grad,
        cross_q_grad,
        cross_kv_grad,
        up_grad,
        out_grad,
        cross_out_grad,
        down_grad,
        qkv_bias_grad,
        cross_q_bias_grad,
        cross_kv_bias_grad,
        up_bias_grad,
    )
    return (output, own_grad, side_grad, small, large)


def body(
    tokens,
    cotangent,
    lengths,
    norm1_gain,
    norm1_shift,
    query_key_value_weight,
    query_key_value_bias,
    out_weight,
    out_bias,
    norm2_gain,
    norm2_shift,
    normy_gain,
    normy_shift,
    cross_q_weight,
    cross_q_bias,
    cross_key_value_weight,
    cross_key_value_bias,
    cross_out_weight,
    cross_out_bias,
    norm3_gain,
    norm3_shift,
    up_weight,
    up_bias,
    down_weight,
    down_bias,
):
    batches = tokens.shape[0]
    local_rows = tokens.shape[2]
    buffer_rows = local_rows * lax.axis_size("mp")
    norms = tuple(
        (
            entry.astype(jnp.float32)
            for entry in (
                norm1_gain,
                norm1_shift,
                out_bias,
                norm2_gain,
                norm2_shift,
                normy_gain,
                normy_shift,
                cross_out_bias,
                norm3_gain,
                norm3_shift,
                down_bias,
            )
        )
    )
    matrices = (
        query_key_value_weight,
        cross_q_weight,
        cross_key_value_weight,
        up_weight,
        out_weight,
        cross_out_weight,
        down_weight,
        query_key_value_bias,
        cross_q_bias,
        cross_key_value_bias,
        up_bias,
    )
    fetched = None
    held = None
    small_sums = None
    outputs = []
    row_grads = []
    for index in range(batches):
        fetched = fetch(matrices)
        segment, cosine, sine = tables(lengths[index, 0], buffer_rows, HEAD_DIM // 2)
        layout = (segment, segment, cosine, sine)
        views = (tokens[index, 0].astype(jnp.float32), tokens[index, 1].astype(jnp.float32))
        first = view_pass(views[0], views[1], cotangent[index, 0], fetched, norms, 0, layout)
        second = view_pass(views[1], views[0], cotangent[index, 1], fetched, norms, 1, layout)
        outputs.append(jnp.stack([first[0], second[0]], 0))
        row_grads.append(jnp.stack([first[1] + second[2], second[1] + first[2]], 0))
        fresh_small = tuple(
            (jnp.stack([left, right], 0) for left, right in zip(first[3], second[3]))
        )
        if small_sums is None:
            small_sums = fresh_small
        else:
            small_sums = tuple((left + right for left, right in zip(small_sums, fresh_small)))
        grads = tuple((jnp.stack([left, right], 0) for left, right in zip(first[4], second[4])))
        grads = settle(grads)
        held = grads if held is None else tuple((left + right for left, right in zip(held, grads)))
    (
        gain_one_sum,
        shift_one_sum,
        out_bias_sum,
        gain_two_sum,
        shift_two_sum,
        gain_side_sum,
        shift_side_sum,
        cross_bias_sum,
        gain_three_sum,
        shift_three_sum,
        down_bias_sum,
    ) = small_sums
    small_total = lax.psum(
        (
            gain_one_sum,
            shift_one_sum,
            out_bias_sum,
            gain_two_sum,
            shift_two_sum,
            gain_side_sum,
            shift_side_sum,
            cross_bias_sum,
            gain_three_sum,
            shift_three_sum,
            down_bias_sum,
        ),
        ("dp", "mp"),
    )
    head_total = lax.psum((held[7], held[8], held[9], held[10]), "dp")
    block_output = jnp.stack(outputs, 0)
    input_grad = jnp.stack(row_grads, 0)
    return (
        block_output,
        input_grad,
        small_total[0],
        small_total[1],
        held[0],
        head_total[0],
        held[4],
        small_total[2],
        small_total[3],
        small_total[4],
        small_total[5],
        small_total[6],
        held[1],
        head_total[1],
        held[2],
        head_total[2],
        held[5],
        small_total[7],
        small_total[8],
        small_total[9],
        held[3],
        head_total[3],
        held[6],
        small_total[10],
    )


def solution(mesh):
    in_specs = (
        P(None, None, ("dp", "mp"), None),
        P(None, None, ("dp", "mp"), None),
        P(None, "dp", None),
        P(),
        P(),
        P(None, "dp", None, "mp"),
        P(None, None, "mp"),
        P(None, "mp", "dp"),
        P(),
        P(),
        P(),
        P(),
        P(),
        P(None, "dp", "mp"),
        P(None, "mp"),
        P(None, "dp", None, "mp"),
        P(None, None, "mp"),
        P(None, "mp", "dp"),
        P(),
        P(),
        P(),
        P(None, "dp", "mp"),
        P(None, "mp"),
        P(None, "mp", "dp"),
        P(),
    )
    out_specs = (
        P(None, None, ("dp", "mp"), None),
        P(None, None, ("dp", "mp"), None),
        P(),
        P(),
        P(None, "dp", None, "mp"),
        P(None, None, "mp"),
        P(None, "mp", "dp"),
        P(),
        P(),
        P(),
        P(),
        P(),
        P(None, "dp", "mp"),
        P(None, "mp"),
        P(None, "dp", None, "mp"),
        P(None, None, "mp"),
        P(None, "mp", "dp"),
        P(),
        P(),
        P(),
        P(None, "dp", "mp"),
        P(None, "mp"),
        P(None, "mp", "dp"),
        P(),
    )
    return jax.shard_map(body, mesh=mesh, in_specs=in_specs, out_specs=out_specs, check_vma=False)
```

profile of v0, /device:TPU:0, one launch (start us, length us, event | category | flops | bytes accessed | tf_op | source)
XLA Modules:
  0.0 2557.9 jit_solution(17473485651461324039)
XLA Ops:
  23.3 35.1 %all_gather.114 = bf16[2,192,768]{1,0,2:T(2,128)(2,1)S(1)} all-gather(bf16[2,192,96]{1,0,2:T(2,128)(2,1)S(1)} %copy.299), channel_id=1, replica_groups=mesh['dp'=8,'mp'=4] {'dp'}, dimensions={2}, use_global_device_ids=true | all-gather | bytes 663552 | tf_op jit(solution)/shard_map/all_gather | solution.py:82
  68.5 17.2 all-gather.73.cloned.1.call-done
  87.9 19.6 all-gather.57.cloned.1.call-done
  113.2 49.1 %all-gather.39.cloned.1.call-done = bf16[2,768,3,192]{3,0,2,1:T(2,128)(2,1)} async-done(((bf16[2,96,3,192]{3,0,2,1:T(2,128)(2,1)}), bf16[2,768,3,192]{3,0,2,1:T(2,128)(2,1)}) %all-gather.39.cloned.1.call-update) | async-done | bytes 1769488 | tf_op jit(solution)/shard_map/all_gather | solution.py:76
  185.3 18.9 all-gather.37.cloned.1.call-done
  210.1 12.0 while.220
  227.8 11.6 while.216
  243.5 19.7 reduce-scatter.47.cloned.1.call-done
  263.2 41.3 %reduce-scatter.35.cloned.1.call-done = f32[256,768]{1,0:T(8,128)} async-done(((f32[1024,768]{1,0:T(8,128)}), f32[256,768]{1,0:T(8,128)}) %reduce-scatter.35.cloned.1.call-update) | async-done | bytes 786448 | tf_op jit(solution)/shard_map/reduce_scatter | solution.py:152
  314.5 32.2 %all_gather.116 = bf16[2,768,192]{2,1,0:T(8,128)(2,1)S(1)} all-gather(bf16[2,96,192]{2,1,0:T(8,128)(2,1)S(1)} %copy-done.298), channel_id=1, replica_groups=mesh['dp'=8,'mp'=4] {'dp'}, dimensions={1}, use_global_device_ids=true | all-gather | bytes 663552 | tf_op jit(solution)/shard_map/all_gather | solution.py:77
  375.4 16.9 all-gather.69.cloned.1.call-done
  397.9 15.6 all-gather.63.cloned.1.call-done
  417.3 11.6 while.222
  434.7 11.8 while.218
  449.9 22.4 reduce-scatter.53.cloned.1.call-done
  472.3 41.1 %reduce-scatter.41.cloned.1.call-done = f32[256,768]{1,0:T(8,128)} async-done(((f32[1024,768]{1,0:T(8,128)}), f32[256,768]{1,0:T(8,128)}) %reduce-scatter.41.cloned.1.call-update) | async-done | bytes 786448 | tf_op jit(solution)/shard_map/reduce_scatter | solution.py:152
  517.9 32.3 %all_gather.119 = bf16[2,192,768]{1,0,2:T(2,128)(2,1)S(1)} all-gather(bf16[2,192,96]{1,0,2:T(2,128)(2,1)S(1)} %copy.306), channel_id=1, replica_groups=mesh['dp'=8,'mp'=4] {'dp'}, dimensions={2}, use_global_device_ids=true | all-gather | bytes 663552 | tf_op jit(solution)/shard_map/all_gather | solution.py:83
  564.1 14.8 while.219
  588.2 11.6 while.223
  607.3 15.6 reduce-scatter.43.cloned.1.call-done
  622.8 40.7 %reduce-scatter.55.cloned.1.call-done = f32[256,768]{1,0:T(8,128)} async-done(((f32[1024,768]{1,0:T(8,128)}), f32[256,768]{1,0:T(8,128)}) %reduce-scatter.55.cloned.1.call-update) | async-done | bytes 786448 | tf_op jit(solution)/shard_map/reduce_scatter | solution.py:152
  671.9 45.6 %all-gather.49.cloned.1.call-done = bf16[2,768,768]{2,1,0:T(8,128)(2,1)} async-done(((bf16[2,96,768]{2,1,0:T(8,128)(2,1)}), bf16[2,768,768]{2,1,0:T(8,128)(2,1)}) %all-gather.49.cloned.1.call-update) | async-done | bytes 2359312 | tf_op jit(solution)/shard_map/all_gather | solution.py:79
  717.5 20.4 all-gather.75.cloned.1.call-done
  742.7 17.0 all-gather.59.cloned.1.call-done
  759.7 18.0 multiply_convert_fusion.10
  781.0 54.2 %all-gather.51.cloned.1.call-done = bf16[2,768,768]{1,2,0:T(8,128)(2,1)} async-done(((bf16[2,768,96]{1,2,0:T(8,128)(2,1)}), bf16[2,768,768]{1,2,0:T(8,128)(2,1)}) %all-gather.51.cloned.1.call-update) | async-done | bytes 2359312 | tf_op jit(solution)/shard_map/all_gather | solution.py:84
  845.1 9.8 all-gather.99.cloned.1.call-done
  884.1 11.2 reduce-scatter.65.cloned.1.call-done
  895.3 41.1 %reduce-scatter.77.cloned.1.call-done = f32[256,768]{1,0:T(8,128)} async-done(((f32[1024,768]{1,0:T(8,128)}), f32[256,768]{1,0:T(8,128)}) %reduce-scatter.77.cloned.1.call-update) | async-done | bytes 786448 | tf_op jit(solution)/shard_map/reduce_scatter | solution.py:162
  941.9 35.1 %reduce-scatter.45.cloned.1.call-done = f32[256,768]{1,0:T(8,128)} async-done(((f32[1024,768]{1,0:T(8,128)}), f32[256,768]{1,0:T(8,128)}) %reduce-scatter.45.cloned.1.call-update) | async-done | bytes 786448 | tf_op jit(solution)/shard_map/reduce_scatter | solution.py:152
  976.9 40.7 %reduce-scatter.57.cloned.1.call-done = f32[256,768]{1,0:T(8,128)} async-done(((f32[1024,768]{1,0:T(8,128)}), f32[256,768]{1,0:T(8,128)}) %reduce-scatter.57.cloned.1.call-update) | async-done | bytes 786448 | tf_op jit(solution)/shard_map/reduce_scatter | solution.py:152
  1025.4 14.3 while.221
  1049.6 10.3 all-gather.81.cloned.1.call-done
  1064.3 36.9 %while.226 = (s32[]{:T(128)}, f32[1024,3,64]{0,2,1:T(8,128)S(1)}, f32[1024,3,64]{0,2,1:T(8,128)}, f32[2,512,3,64]{1,0,3,2:T(2,128)}, bf16[2,512,3,64]{1,3,2,0:T(...) while((s32[]{:T(128)}, f32[1024,3,64]{0,2,1:T(8,128)S(1)}, ...), condition=%wide.region_94.95_spmd.clone, body=%wide.region_92.94_spmd.clone.sunk | while | flops 1031830016 | bytes 64282876 | solution.py:244
  1074.6 8.1 dynamic_update_slice.140
  1093.1 8.1 dynamic_update_slice.140
  1106.0 11.8 while.217
  1121.0 38.0 %reduce-scatter.37.cloned.1.call-done = f32[256,768]{1,0:T(8,128)} async-done(((f32[1024,768]{1,0:T(8,128)}), f32[256,768]{1,0:T(8,128)}) %reduce-scatter.37.cloned.1.call-update) | async-done | bytes 786448 | tf_op jit(solution)/shard_map/reduce_scatter | solution.py:152
  1173.6 9.7 all-gather.67.cloned.1.call-done
  1188.2 16.5 all-gather.47.cloned.1.call-done
  1204.6 18.2 multiply_convert_fusion.11
  1235.4 11.4 all-gather.93.cloned.1.call-done
  1269.3 38.5 %reduce-scatter.67.cloned.1.call-done = f32[256,2,768]{2,0,1:T(8,128)} async-done(((f32[1024,2,768]{2,0,1:T(8,128)}), f32[256,2,768]{2,0,1:T(8,128)}) %reduce-scatter.67.cloned.1.call-update) | async-done | bytes 1572880 | tf_op jit(solution)/shard_map/reduce_scatter | solution.py:162
  1311.3 37.5 %reduce-scatter.71.cloned.1.call-done = f32[256,768]{1,0:T(8,128)} async-done(((f32[1024,768]{1,0:T(8,128)}), f32[256,768]{1,0:T(8,128)}) %reduce-scatter.71.cloned.1.call-update) | async-done | bytes 786448 | tf_op jit(solution)/shard_map/reduce_scatter | solution.py:162
  1348.8 40.5 %reduce-scatter.59.cloned.1.call-done = f32[256,768]{1,0:T(8,128)} async-done(((f32[1024,768]{1,0:T(8,128)}), f32[256,768]{1,0:T(8,128)}) %reduce-scatter.59.cloned.1.call-update) | async-done | bytes 786448 | tf_op jit(solution)/shard_map/reduce_scatter | solution.py:162
  1392.0 38.0 %reduce-scatter.51.cloned.1.call-done = f32[256,768]{1,0:T(8,128)} async-done(((f32[1024,768]{1,0:T(8,128)}), f32[256,768]{1,0:T(8,128)}) %reduce-scatter.51.cloned.1.call-update) | async-done | bytes 786448 | tf_op jit(solution)/shard_map/reduce_scatter | solution.py:152
  1430.0 40.5 %reduce-scatter.39.cloned.1.call-done = f32[256,768]{1,0:T(8,128)} async-done(((f32[1024,768]{1,0:T(8,128)}), f32[256,768]{1,0:T(8,128)}) %reduce-scatter.39.cloned.1.call-update) | async-done | bytes 786448 | tf_op jit(solution)/shard_map/reduce_scatter | solution.py:152
  1478.9 17.9 all-gather.89.cloned.1.call-done
  1502.1 40.3 %while.230 = (s32[]{:T(128)}, f32[1024,3,64]{0,2,1:T(8,128)S(1)}, f32[1024,3,64]{0,2,1:T(8,128)}, f32[2,512,3,64]{1,0,3,2:T(2,128)}, bf16[2,512,3,64]{1,3,2,0:T(...) while((s32[]{:T(128)}, f32[1024,3,64]{0,2,1:T(8,128)S(1)}, ...), condition=%wide.region_128.129_spmd.clone, body=%wide.region_126.128_spmd.clone.sunk | while | flops 1031830016 | bytes 56418472 | solution.py:244
  1546.0 40.5 %while.228 = (s32[]{:T(128)}, f32[1024,3,64]{0,2,1:T(8,128)S(1)}, f32[1024,3,64]{0,2,1:T(8,128)}, f32[2,512,3,64]{1,0,3,2:T(2,128)}, bf16[2,512,3,64]{1,3,2,0:T(...) while((s32[]{:T(128)}, f32[1024,3,64]{0,2,1:T(8,128)S(1)}, ...), condition=%wide.region_113.114_spmd.clone, body=%wide.region_111.113_spmd.clone.sunk | while | flops 1031830016 | bytes 56418472 | solution.py:244
  1606.0 39.2 %while.224 = (s32[]{:T(128)}, f32[1024,3,64]{0,2,1:T(8,128)S(1)}, f32[1024,3,64]{0,2,1:T(8,128)}, f32[2,512,3,64]{1,0,3,2:T(2,128)}, bf16[2,512,3,64]{1,3,2,0:T(...) while((s32[]{:T(128)}, f32[1024,3,64]{0,2,1:T(8,128)S(1)}, ...), condition=%wide.region_79.80_spmd.clone, body=%wide.region_77.79_spmd.clone.sunk | while | flops 1031830016 | bytes 56418472 | solution.py:244
  1656.1 42.6 %while.227 = (s32[]{:T(128)}, f32[1024,3,64]{0,2,1:T(8,128)S(1)}, f32[1024,3,64]{0,2,1:T(8,128)}, f32[2,512,3,64]{1,0,3,2:T(2,128)}, bf16[2,512,3,64]{1,3,2,0:T(...) while((s32[]{:T(128)}, f32[1024,3,64]{0,2,1:T(8,128)S(1)}, ...), condition=%wide.region_102.103_spmd.clone, body=%wide.region_100.102_spmd.clone.sunk | while | flops 1031830016 | bytes 56414376 | solution.py:244
  1669.4 8.1 dynamic_update_slice.141
  1690.6 8.1 dynamic_update_slice.141
  1717.4 50.8 %reduce-scatter.61.cloned.1.call-done = f32[256,2,768]{2,0,1:T(8,128)} async-done(((f32[1024,2,768]{2,0,1:T(8,128)}), f32[256,2,768]{2,0,1:T(8,128)}) %reduce-scatter.61.cloned.1.call-update) | async-done | bytes 1572880 | tf_op jit(solution)/shard_map/reduce_scatter | solution.py:162
  1773.9 55.3 %reduce-scatter.79.cloned.1.call-done = f32[256,2,768]{2,0,1:T(8,128)} async-done(((f32[1024,2,768]{2,0,1:T(8,128)}), f32[256,2,768]{2,0,1:T(8,128)}) %reduce-scatter.79.cloned.1.call-update) | async-done | bytes 1572880 | tf_op jit(solution)/shard_map/reduce_scatter | solution.py:162
  1874.6 40.3 %while.231 = (s32[]{:T(128)}, f32[1024,3,64]{0,2,1:T(8,128)S(1)}, f32[1024,3,64]{0,2,1:T(8,128)}, f32[2,512,3,64]{1,0,3,2:T(2,128)}, bf16[2,512,3,64]{1,3,2,0:T(...) while((s32[]{:T(128)}, f32[1024,3,64]{0,2,1:T(8,128)S(1)}, ...), condition=%wide.region_136.137_spmd.clone, body=%wide.region_134.136_spmd.clone.sunk | while | flops 1031830016 | bytes 56418472 | solution.py:244
  1921.5 40.6 %while.225 = (s32[]{:T(128)}, f32[1024,3,64]{0,2,1:T(8,128)S(1)}, f32[1024,3,64]{0,2,1:T(8,128)}, f32[2,512,3,64]{1,0,3,2:T(2,128)}, bf16[2,512,3,64]{1,3,2,0:T(...) while((s32[]{:T(128)}, f32[1024,3,64]{0,2,1:T(8,128)S(1)}, ...), condition=%wide.region_85.86_spmd.clone, body=%wide.region_83.85_spmd.clone.sunk | while | flops 1031830016 | bytes 56418472 | solution.py:244
  1974.6 39.1 %while.229 = (s32[]{:T(128)}, f32[1024,3,64]{0,2,1:T(8,128)S(1)}, f32[1024,3,64]{0,2,1:T(8,128)}, f32[2,512,3,64]{1,0,3,2:T(2,128)}, bf16[2,512,3,64]{1,3,2,0:T(...) while((s32[]{:T(128)}, f32[1024,3,64]{0,2,1:T(8,128)S(1)}, ...), condition=%wide.region_119.120_spmd.clone, body=%wide.region_117.119_spmd.clone.sunk | while | flops 1031830016 | bytes 56418472 | solution.py:244
  2093.4 8.1 reshape.1772
  2144.6 10.2 all-to-all-done
  2218.9 73.5 %all-reduce.33 = (f32[2,3,192]{2,1,0:T(4,128)S(1)}, f32[2,192]{1,0:T(2,128)}, f32[2,2,192]{2,1,0:T(2,128)}, f32[2,768]{1,0:T(2,128)}) all-reduce(f32[2,3,192]{2,1,0:T(4,128)S(1)} %maximum_add_fusion.4, f32[2,192]{1,0:T(2,128)} %maximum_add_fusion.18, f32[2,2,192]{2,1,0:T(2,128)S(1)} %copy-done.363, ...), channel_id=1, replica_groups=mesh['dp'=8,'mp'=4] {'dp'}, use_global_device_ids=true, to_apply=%region_158.159 | all-reduce | flops 3840 | bytes 30720 | tf_op jit(solution)/shard_map/psum | solution.py:602
  2328.7 74.9 %reduce-scatter.83.cloned.1.call-done = f32[2,96,768]{2,1,0:T(8,128)} async-done(((f32[2,768,768]{2,1,0:T(8,128)}), f32[2,96,768]{2,1,0:T(8,128)}) %reduce-scatter.83.cloned.1.call-update) | async-done | bytes 589840 | tf_op jit(solution)/shard_map/reduce_scatter | solution.py:119
  2403.6 132.9 %all-reduce.36.cloned.1.call-done = (f32[2,768]{1,0:T(2,128)}, f32[2,768]{1,0:T(2,128)}, f32[2,768]{1,0:T(2,128)}, f32[2,768]{1,0:T(2,128)}, f32[2,768]{1,0:T(2,...) async-done(((f32[2,768]{1,0:T(2,128)}, f32[2,768]{1,0:T(2,128)}, ...) | async-done | bytes 67600 | tf_op jit(solution)/shard_map/psum | solution.py:586
  (1914 shorter events, 1066.6 us)
Async XLA Ops:
  7.2 57.3 %all-gather.45.cloned.1.call-start = ((), (), s32[]{:S(2)}) async-start(), calls=%async_computation.35 | async-start | bytes 1769472 | tf_op jit(solution)/shard_map/all_gather | solution.py:78
  9.1 76.6 %all-gather.73.cloned.1.call-start = ((), (), s32[]{:S(2)}) async-start(), calls=%async_computation.58 | async-start | bytes 1966080 | tf_op jit(solution)/shard_map/all_gather | solution.py:147
  18.4 89.2 %all-gather.57.cloned.1.call-start = ((), (), s32[]{:S(2)}) async-start(), calls=%async_computation.44 | async-start | bytes 1966080 | tf_op jit(solution)/shard_map/all_gather | solution.py:147
  19.1 143.2 %all-gather.39.cloned.1.call-start = ((), (), s32[]{:S(2)}) async-start(), calls=%async_computation.31 | async-start | bytes 2654208 | tf_op jit(solution)/shard_map/all_gather | solution.py:76
  20.2 162.3 %all-gather.61.cloned.1.call-start = ((), (), s32[]{:S(2)}) async-start(), calls=%async_computation.48 | async-start | bytes 1966080 | tf_op jit(solution)/shard_map/all_gather | solution.py:147
  20.8 183.4 %all-gather.37.cloned.1.call-start = ((), (), s32[]{:S(2)}) async-start(), calls=%async_computation.30 | async-start | bytes 1966080 | tf_op jit(solution)/shard_map/all_gather | solution.py:147
  21.4 241.8 %reduce-scatter.47.cloned.1.call-start = ((), (), s32[]{:S(2)}) async-start(), calls=%async_computation.49 | async-start | bytes 3932160 | tf_op jit(solution)/shard_map/reduce_scatter | solution.py:152
  225.1 79.3 %reduce-scatter.35.cloned.1.call-start = ((), (), s32[]{:S(2)}) async-start(), calls=%async_computation.32 | async-start | bytes 3932160 | tf_op jit(solution)/shard_map/reduce_scatter | solution.py:152
  242.8 114.4 %all-gather.65.cloned.1.call-start = ((), (), s32[]{:S(2)}) async-start(), calls=%async_computation.51 | async-start | bytes 1966080 | tf_op jit(solution)/shard_map/all_gather | solution.py:147
  307.8 51.8 %all-gather.43.cloned.1.call-start = ((), (), s32[]{:S(2)}) async-start(), calls=%async_computation.34 | async-start | bytes 1966080 | tf_op jit(solution)/shard_map/all_gather | solution.py:147
  308.4 62.8 %all-gather.53.cloned.1.call-start = ((), (), s32[]{:S(2)}) async-start(), calls=%async_computation.41 | async-start | bytes 1966080 | tf_op jit(solution)/shard_map/all_gather | solution.py:147
  309.1 83.1 %all-gather.69.cloned.1.call-start = ((), (), s32[]{:S(2)}) async-start(), calls=%async_computation.55 | async-start | bytes 1966080 | tf_op jit(solution)/shard_map/all_gather | solution.py:147
  309.7 103.8 %all-gather.63.cloned.1.call-start = ((), (), s32[]{:S(2)}) async-start(), calls=%async_computation.50 | async-start | bytes 1966080 | tf_op jit(solution)/shard_map/all_gather | solution.py:147
  357.1 115.2 %reduce-scatter.53.cloned.1.call-start = ((), (), s32[]{:S(2)}) async-start(), calls=%async_computation.56 | async-start | bytes 3932160 | tf_op jit(solution)/shard_map/reduce_scatter | solution.py:152
  434.2 79.2 %reduce-scatter.41.cloned.1.call-start = ((), (), s32[]{:S(2)}) async-start(), calls=%async_computation.42 | async-start | bytes 3932160 | tf_op jit(solution)/shard_map/reduce_scatter | solution.py:152
  449.9 110.6 %all-gather.55.cloned.1.call-start = ((), (), s32[]{:S(2)}) async-start(), calls=%async_computation.43 | async-start | bytes 1966080 | tf_op jit(solution)/shard_map/all_gather | solution.py:147
  517.6 67.2 %all-gather.71.cloned.1.call-start = ((), (), s32[]{:S(2)}) async-start(), calls=%async_computation.57 | async-start | bytes 1966080 | tf_op jit(solution)/shard_map/all_gather | solution.py:147
  560.4 62.5 %reduce-scatter.43.cloned.1.call-start = ((), (), s32[]{:S(2)}) async-start(), calls=%async_computation.45 | async-start | bytes 3932160 | tf_op jit(solution)/shard_map/reduce_scatter | solution.py:152
  584.7 78.8 %reduce-scatter.55.cloned.1.call-start = ((), (), s32[]{:S(2)}) async-start(), calls=%async_computation.59 | async-start | bytes 3932160 | tf_op jit(solution)/shard_map/reduce_scatter | solution.py:152
  604.7 112.8 %all-gather.49.cloned.1.call-start = ((), (), s32[]{:S(2)}) async-start(), calls=%async_computation.38 | async-start | bytes 2654208 | tf_op jit(solution)/shard_map/all_gather | solution.py:79
  605.3 132.6 %all-gather.75.cloned.1.call-start = ((), (), s32[]{:S(2)}) async-start(), calls=%async_computation.60 | async-start | bytes 1966080 | tf_op jit(solution)/shard_map/all_gather | solution.py:147
  667.7 92.0 %all-gather.59.cloned.1.call-start = ((), (), s32[]{:S(2)}) async-start(), calls=%async_computation.46 | async-start | bytes 1966080 | tf_op jit(solution)/shard_map/all_gather | solution.py:147
  668.5 112.5 %all-gather.95.cloned.1.call-start = ((), (), s32[]{:S(2)}) async-start(), calls=%async_computation.83 | async-start | bytes 1966080 | tf_op jit(solution)/shard_map/all_gather | solution.py:157
  669.8 165.4 %all-gather.51.cloned.1.call-start = ((), (), s32[]{:S(2)}) async-start(), calls=%async_computation.39 | async-start | bytes 2654208 | tf_op jit(solution)/shard_map/all_gather | solution.py:84
  670.4 184.6 %all-gather.99.cloned.1.call-start = ((), (), s32[]{:S(2)}) async-start(), calls=%async_computation.85 | async-start | bytes 1966080 | tf_op jit(solution)/shard_map/all_gather | solution.py:157
  671.1 224.2 %reduce-scatter.65.cloned.1.call-start = ((), (), s32[]{:S(2)}) async-start(), calls=%async_computation.67 | async-start | bytes 3932160 | tf_op jit(solution)/shard_map/reduce_scatter | solution.py:162
  844.9 91.5 %reduce-scatter.77.cloned.1.call-start = ((), (), s32[]{:S(2)}) async-start(), calls=%async_computation.77 | async-start | bytes 3932160 | tf_op jit(solution)/shard_map/reduce_scatter | solution.py:162
  864.6 112.3 %reduce-scatter.45.cloned.1.call-start = ((), (), s32[]{:S(2)}) async-start(), calls=%async_computation.47 | async-start | bytes 3932160 | tf_op jit(solution)/shard_map/reduce_scatter | solution.py:152
  870.9 146.7 %reduce-scatter.57.cloned.1.call-start = ((), (), s32[]{:S(2)}) async-start(), calls=%async_computation.61 | async-start | bytes 3932160 | tf_op jit(solution)/shard_map/reduce_scatter | solution.py:152
  876.6 170.0 %all-gather.41.cloned.1.call-start = ((), (), s32[]{:S(2)}) async-start(), calls=%async_computation.33 | async-start | bytes 1966080 | tf_op jit(solution)/shard_map/all_gather | solution.py:147
  877.2 182.8 %all-gather.81.cloned.1.call-start = ((), (), s32[]{:S(2)}) async-start(), calls=%async_computation.68 | async-start | bytes 1966080 | tf_op jit(solution)/shard_map/all_gather | solution.py:157
  1023.9 97.1 %reduce-scatter.49.cloned.1.call-start = ((), (), s32[]{:S(2)}) async-start(), calls=%async_computation.52 | async-start | bytes 3932160 | tf_op jit(solution)/shard_map/reduce_scatter | solution.py:152
  1046.1 112.9 %reduce-scatter.37.cloned.1.call-start = ((), (), s32[]{:S(2)}) async-start(), calls=%async_computation.36 | async-start | bytes 3932160 | tf_op jit(solution)/shard_map/reduce_scatter | solution.py:152
  1120.9 62.5 %all-gather.67.cloned.1.call-start = ((), (), s32[]{:S(2)}) async-start(), calls=%async_computation.53 | async-start | bytes 1966080 | tf_op jit(solution)/shard_map/all_gather | solution.py:147
  1163.5 41.1 %all-gather.47.cloned.1.call-start = ((), (), s32[]{:S(2)}) async-start(), calls=%async_computation.37 | async-start | bytes 1966080 | tf_op jit(solution)/shard_map/all_gather | solution.py:147
  1164.3 61.4 %all-gather.97.cloned.1.call-start = ((), (), s32[]{:S(2)}) async-start(), calls=%async_computation.84 | async-start | bytes 1966080 | tf_op jit(solution)/shard_map/all_gather | solution.py:157
  1164.9 82.0 %all-gather.93.cloned.1.call-start = ((), (), s32[]{:S(2)}) async-start(), calls=%async_computation.82 | async-start | bytes 1966080 | tf_op jit(solution)/shard_map/all_gather | solution.py:157
  1165.5 142.3 %reduce-scatter.67.cloned.1.call-start = ((), (), s32[]{:S(2)}) async-start(), calls=%async_computation.69 | async-start | bytes 7864320 | tf_op jit(solution)/shard_map/reduce_scatter | solution.py:162
  1173.6 175.2 %reduce-scatter.71.cloned.1.call-start = ((), (), s32[]{:S(2)}) async-start(), calls=%async_computation.72 | async-start | bytes 3932160 | tf_op jit(solution)/shard_map/reduce_scatter | solution.py:162
  1235.4 153.9 %reduce-scatter.59.cloned.1.call-start = ((), (), s32[]{:S(2)}) async-start(), calls=%async_computation.62 | async-start | bytes 3932160 | tf_op jit(solution)/shard_map/reduce_scatter | solution.py:162
  1256.5 173.5 %reduce-scatter.51.cloned.1.call-start = ((), (), s32[]{:S(2)}) async-start(), calls=%async_computation.54 | async-start | bytes 3932160 | tf_op jit(solution)/shard_map/reduce_scatter | solution.py:152
  1262.9 207.6 %reduce-scatter.39.cloned.1.call-start = ((), (), s32[]{:S(2)}) async-start(), calls=%async_computation.40 | async-start | bytes 3932160 | tf_op jit(solution)/shard_map/reduce_scatter | solution.py:152
  1268.7 228.1 %all-gather.89.cloned.1.call-start = ((), (), s32[]{:S(2)}) async-start(), calls=%async_computation.78 | async-start | bytes 1966080 | tf_op jit(solution)/shard_map/all_gather | solution.py:157
  1269.3 204.6 %copy-start.334 = (f32[256]{0:T(256)}, f32[256]{0:T(256)S(1)}, u32[]{:S(2)}) copy-start(f32[256]{0:T(256)S(1)} %negate_multiply_fusion.8) | copy-start | bytes 3076
  1477.0 65.4 %all-gather.85.cloned.1.call-start = ((), (), s32[]{:S(2)}) async-start(), calls=%async_computation.73 | async-start | bytes 1966080 | tf_op jit(solution)/shard_map/all_gather | solution.py:157
  1477.7 114.3 %all-gather.77.cloned.1.call-start = ((), (), s32[]{:S(2)}) async-start(), calls=%async_computation.63 | async-start | bytes 1966080 | tf_op jit(solution)/shard_map/all_gather | solution.py:157
  1478.3 171.8 %all-gather.83.cloned.1.call-start = ((), (), s32[]{:S(2)}) async-start(), calls=%async_computation.70 | async-start | bytes 1966080 | tf_op jit(solution)/shard_map/all_gather | solution.py:157
  1478.9 238.6 %reduce-scatter.73.cloned.1.call-start = ((), (), s32[]{:S(2)}) async-start(), calls=%async_computation.74 | async-start | bytes 7864320 | tf_op jit(solution)/shard_map/reduce_scatter | solution.py:162
  1604.3 163.9 %reduce-scatter.61.cloned.1.call-start = ((), (), s32[]{:S(2)}) async-start(), calls=%async_computation.64 | async-start | bytes 7864320 | tf_op jit(solution)/shard_map/reduce_scatter | solution.py:162
  1709.5 119.6 %reduce-scatter.79.cloned.1.call-start = ((), (), s32[]{:S(2)}) async-start(), calls=%async_computation.79 | async-start | bytes 7864320 | tf_op jit(solution)/shard_map/reduce_scatter | solution.py:162
  1717.4 153.2 %all-gather.91.cloned.1.call-start = ((), (), s32[]{:S(2)}) async-start(), calls=%async_computation.80 | async-start | bytes 1966080 | tf_op jit(solution)/shard_map/all_gather | solution.py:157
  1836.8 81.1 %all-gather.79.cloned.1.call-start = ((), (), s32[]{:S(2)}) async-start(), calls=%async_computation.65 | async-start | bytes 1966080 | tf_op jit(solution)/shard_map/all_gather | solution.py:157
  1837.4 126.5 %all-gather.87.cloned.1.call-start = ((), (), s32[]{:S(2)}) async-start(), calls=%async_computation.75 | async-start | bytes 1966080 | tf_op jit(solution)/shard_map/all_gather | solution.py:157
  1838.1 372.3 %reduce-scatter.87.cloned.1.call-start = ((), (), s32[]{:S(2)}) async-start(), calls=%async_computation.88 | async-start | bytes 1327104
  1846.2 366.0 %reduce-scatter.89.cloned.1.call-start = ((), (), s32[]{:S(2)}) async-start(), calls=%async_computation.89 | async-start | bytes 2654208
  1863.4 441.9 %reduce-scatter.69.cloned.1.call-start = ((), (), s32[]{:S(2)}) async-start(), calls=%async_computation.71 | async-start | bytes 3932160 | tf_op jit(solution)/shard_map/reduce_scatter | solution.py:162
  1870.1 435.2 %reduce-scatter.63.cloned.1.call-start = ((), (), s32[]{:S(2)}) async-start(), calls=%async_computation.66 | async-start | bytes 3932160 | tf_op jit(solution)/shard_map/reduce_scatter | solution.py:162
  1972.9 332.4 %reduce-scatter.75.cloned.1.call-start = ((), (), s32[]{:S(2)}) async-start(), calls=%async_computation.76 | async-start | bytes 3932160 | tf_op jit(solution)/shard_map/reduce_scatter | solution.py:162
  2025.3 280.0 %reduce-scatter.81.cloned.1.call-start = ((), (), s32[]{:S(2)}) async-start(), calls=%async_computation.81 | async-start | bytes 3932160 | tf_op jit(solution)/shard_map/reduce_scatter | solution.py:162
  2070.8 84.1 %all-to-all-start = ((bf16[8,2,1152,96]{2,3,1,0:T(8,128)(2,1)}), bf16[8,2,1152,96]{2,3,1,0:T(8,128)(2,1)S(1)}, u32[]{:S(2)}, u32[]{:S(2)}) async-start(bf16[8,2,1152,96]{2,3,1,0:T(8,128)(2,1)} %bitcast.208), calls=%async_computation.24 | async-start | bytes 7077888 | tf_op jit(solution)/shard_map/all_to_all | solution.py:20
  2075.9 250.2 %reduce-scatter.85.cloned.1.call-start = ((), (), s32[]{:S(2)}) async-start(), calls=%async_computation.87 | async-start | bytes 3981312
  2156.7 140.0 %all-to-all-start.1 = ((bf16[8,2,1152,96]{2,3,1,0:T(8,128)(2,1)}), bf16[8,2,1152,96]{2,3,1,0:T(8,128)(2,1)}, u32[]{:S(2)}, u32[]{:S(2)}) async-start(bf16[8,2,1152,96]{2,3,1,0:T(8,128)(2,1)} %bitcast.1728), calls=%async_computation.25 | async-start | bytes 7077888 | tf_op jit(solution)/shard_map/all_to_all | solution.py:20
  2161.5 242.2 %reduce-scatter.83.cloned.1.call-start = ((), (), s32[]{:S(2)}) async-start(), calls=%async_computation.86 | async-start | bytes 5308416 | tf_op jit(solution)/shard_map/reduce_scatter | solution.py:119
  2185.8 350.7 %all-reduce.36.cloned.1.call-start = ((), (), s32[]{:S(2)}) async-start(), calls=%async_computation.90 | async-start | bytes 135168 | tf_op jit(solution)/shard_map/psum | solution.py:586
  (475 other events, 6489.6 us)
Sparse Core Ops, SparseCore 0:
  10.8 53.7 all-gather.44
  66.7 18.9 all-gather.72
  87.9 19.6 all-gather.56
  110.2 52.0 all-gather.38
  164.3 18.2 all-gather.60
  184.5 19.6 all-gather.36
  225.2 37.9 reduce-scatter.46
  266.4 37.9 reduce-scatter.34
  307.9 19.6 all-gather.64
  329.6 19.6 all-gather.42
  351.5 19.6 all-gather.52
  372.6 19.6 all-gather.68
  393.8 19.6 all-gather.62
  434.3 37.9 reduce-scatter.52
  475.4 37.9 reduce-scatter.40
  517.7 19.6 all-gather.54
  560.5 19.6 all-gather.70
  584.8 37.9 reduce-scatter.42
  625.5 37.9 reduce-scatter.54
  665.6 51.9 all-gather.48
  719.7 18.1 all-gather.74
  740.0 19.6 all-gather.58
  761.3 19.6 all-gather.94
  783.0 52.0 all-gather.50
  836.7 18.1 all-gather.98
  857.3 37.9 reduce-scatter.64
  898.4 37.9 reduce-scatter.76
  938.9 37.9 reduce-scatter.44
  979.6 37.9 reduce-scatter.56
  1019.0 19.6 all-gather.40
  1040.3 19.6 all-gather.80
  1062.5 37.9 reduce-scatter.48
  1121.0 37.9 reduce-scatter.36
  1163.7 19.6 all-gather.66
  1184.9 19.6 all-gather.46
  1206.0 19.6 all-gather.96
  1227.1 19.6 all-gather.92
  1249.4 58.3 reduce-scatter.66
  1310.9 37.9 reduce-scatter.70
  1351.4 37.9 reduce-scatter.58
  1392.0 37.9 reduce-scatter.50
  1432.5 37.9 reduce-scatter.38
  1477.1 19.6 all-gather.88
  1498.4 19.6 all-gather.84
  1519.6 19.6 all-gather.76
  1540.8 19.6 all-gather.82
  1604.5 58.3 reduce-scatter.72
  1709.6 58.5 reduce-scatter.60
  1770.8 58.3 reduce-scatter.78
  1836.9 19.6 all-gather.90
  1858.6 19.6 all-gather.78
  1880.5 19.6 all-gather.86
  1903.4 63.9 reduce-scatter.86
  1970.9 68.0 reduce-scatter.88
  2041.6 36.9 reduce-scatter.68
  2081.3 37.9 reduce-scatter.62
  2121.8 37.9 reduce-scatter.74
  2163.0 37.9 reduce-scatter.80
  2204.4 99.9 reduce-scatter.84
  2308.6 94.9 reduce-scatter.82
  2411.8 124.6 all-reduce.35
where the time goes:
time: 2580 us; the launch traced here: 2560 us
  waiting for transfers between devices  1250 us (48%)
  matrix products  446 us (17%)
  local copies, waits for them, and re-layouts  405 us (16%)
  other arithmetic  243 us (9%)
  blocking collectives  173 us (7%)
    reduce_scatter x12, waiting for transfers between devices, narrow(): total = lax.psum_scatter(terms, 'mp', scatter_dimension=0, tiled=True)  373 us
    reduce_scatter x12, waiting for transfers between devices, narrow_grad(): total = lax.psum_scatter(terms, 'mp', scatter_dimension=0, tiled=True)  275 us
    all_gather x16, waiting for transfers between devices, widen(): wide = lax.all_gather(rows, 'mp', axis=0, tiled=True)  166 us
    dynamic_update_slice x32, local copies, waits for them, and re-layouts, attend(): results, log_totals = lax.map(one_block, (query_blocks, segment_blocks))  135 us
    psum x1, waiting for transfers between devices, body(): lax.psum((gain_one_sum, shift_one_sum, out_bias_sum, gain_two_sum, shift_...  133 us
    unnamed x968, local copies, waits for them, and re-layouts  117 us
    reduce_scatter x1, waiting for transfers between devices, settle(): lax.psum_scatter(grad_up, 'dp', scatter_dimension=1, tiled=True)  74.9 us
    psum x1, blocking collectives, body(): head_total = lax.psum((held[7], held[8], held[9], held[10]), 'dp')  73.5 us
  transfers between devices with their start and end apart: 63, of which 42 were waited for; matrix products, arithmetic and copies ran while one was open for 38% of the time, Pallas kernels for 0%

commit v1 on v0

v1 whole, which is shorter than its diff:
```python
import functools
import math
import jax
import jax.numpy as jnp
from jax import lax
from jax.experimental import pallas as pl
from jax.experimental.pallas import tpu as pltpu
from jax.sharding import PartitionSpec as P

HEAD_DIM = 64
PAIR = 2 * HEAD_DIM
FAR = 1e30


def swap_halves(u, lane):
    half = HEAD_DIM // 2
    fwd = pltpu.roll(u, half, 1)
    bwd = pltpu.roll(u, PAIR - half, 1)
    return jnp.where(lane % HEAD_DIM < half, bwd, fwd)


def attend_kernel(q_ref, k_ref, v_ref, qf_ref, kf_ref, cos_ref, sin_ref, o_ref, lse_ref, qr_ref, kr_ref, *, tile):
    rows = k_ref.shape[0]
    lane_all = lax.broadcasted_iota(jnp.int32, (rows, PAIR), 1)
    cosine, sine = cos_ref[...], sin_ref[...]
    k = k_ref[...]
    kr = (k * cosine + swap_halves(k, lane_all) * sine).astype(jnp.bfloat16)
    kr_ref[...] = kr
    q = q_ref[...]
    qr_ref[...] = (q * cosine + swap_halves(q, lane_all) * sine).astype(jnp.bfloat16)
    low = lane_all < HEAD_DIM
    kf = kf_ref[...]
    v = v_ref[...].astype(jnp.bfloat16)
    one = jnp.ones_like(v)
    keys = (jnp.where(low, kr, kf), jnp.where(low, kf, kr))
    vals = (jnp.where(low, v, one), jnp.where(low, one, v))
    lane = lax.broadcasted_iota(jnp.int32, (tile, PAIR), 1)
    low_t = lane < HEAD_DIM

    for t in range(rows // tile):
        at = pl.ds(t * tile, tile)
        qs = qr_ref[at, :] * jnp.bfloat16(HEAD_DIM ** -0.5)
        qf = qf_ref[at, :]
        outs, lses = [], []
        for h in range(2):
            qh = jnp.where(low_t, qs, qf) if h == 0 else jnp.where(low_t, qf, qs)
            s = lax.dot_general(qh, keys[h], (((1,), (1,)), ((), ())), preferred_element_type=jnp.float32)
            top = jnp.max(s, -1, keepdims=True)
            p = jnp.exp(s - top).astype(jnp.bfloat16)
            o = jnp.dot(p, vals[h], preferred_element_type=jnp.float32)
            total = pltpu.roll(o, HEAD_DIM, 1)
            outs.append(o / total)
            lses.append(top + jnp.log(total))
        o_ref[at, :] = jnp.where(low_t, outs[0], outs[1]).astype(jnp.bfloat16)
        lse_ref[at, :] = jnp.where(low_t, lses[0], lses[1])


def three_parts(u):
    a = u.astype(jnp.bfloat16).astype(jnp.float32)
    r = u - a
    b = r.astype(jnp.bfloat16).astype(jnp.float32)
    return a, b, r - b


def attend_back_kernel(qr_ref, kr_ref, v_ref, o_ref, do_ref, lse_ref, qf_ref, kf_ref, cos_ref, sin_ref,
                       dq_ref, dk_ref, dv_ref, dk_acc, dv_acc, *, tile):
    rows = kr_ref.shape[0]
    lane_all = lax.broadcasted_iota(jnp.int32, (rows, PAIR), 1)
    low = lane_all < HEAD_DIM
    within = lane_all % HEAD_DIM
    kr = kr_ref[...]
    kf = kf_ref[...]
    v = v_ref[...]
    ones3 = jnp.where(within < 3, 1.0, 0.0).astype(jnp.bfloat16)
    ones6 = jnp.where((within >= 3) & (within < 6), 1.0, 0.0).astype(jnp.bfloat16)
    kfull = kf + ones6
    keys = (jnp.where(low, kr, kfull), jnp.where(low, kfull, kr))
    vals = (jnp.where(low, v, ones3), jnp.where(low, ones3, v))
    lane = lax.broadcasted_iota(jnp.int32, (tile, PAIR), 1)
    low_t = lane < HEAD_DIM
    within_t = lane % HEAD_DIM
    scale = HEAD_DIM ** -0.5
    nt = (((1,), (1,)), ((), ()))
    tn = (((0,), (0,)), ((), ()))
    for t in range(rows // tile):
        at = pl.ds(t * tile, tile)
        qr = qr_ref[at, :]
        qs = qr * jnp.bfloat16(scale)
        do = do_ref[at, :]
        prod = do.astype(jnp.float32) * o_ref[at, :].astype(jnp.float32)
        lse = lse_ref[at, :]
        lse_other = pltpu.roll(lse, HEAD_DIM, 1)
        qf = qf_ref[at, :].astype(jnp.float32)
        dqs = []
        for h in range(2):
            mine = low_t if h == 0 else ~low_t
            dsum = jnp.sum(jnp.where(mine, prod, 0.0), -1, keepdims=True)
            a, b, c = three_parts(-dsum)
            dfeat = jnp.where(within_t == 0, a, jnp.where(within_t == 1, b, jnp.where(within_t == 2, c, 0.0)))
            doh = jnp.where(mine, do, dfeat.astype(jnp.bfloat16))
            a, b, c = three_parts(-lse_other)
            qfeat = jnp.where(within_t == 3, a, jnp.where(within_t == 4, b, jnp.where(within_t == 5, c, qf)))
            qh = jnp.where(mine, qs, qfeat.astype(jnp.bfloat16))
            st = lax.dot_general(keys[h], qh, nt, preferred_element_type=jnp.float32)
            p = jnp.exp(st)
            dpt = lax.dot_general(vals[h], doh, nt, preferred_element_type=jnp.float32)
            ds = (p * dpt).astype(jnp.bfloat16)
            dv = jnp.dot(p.astype(jnp.bfloat16), do, preferred_element_type=jnp.float32)
            dk = jnp.dot(ds, qs, preferred_element_type=jnp.float32)
            dqs.append(lax.dot_general(ds, kr, tn, preferred_element_type=jnp.float32))
            if t == 0:
                dv_acc[h] = dv
                dk_acc[h] = dk
            else:
                dv_acc[h] += dv
                dk_acc[h] += dk
        dq = jnp.where(low_t, dqs[0], dqs[1]) * scale
        dq_ref[at, :] = (dq * cos_ref[at, :] - swap_halves(dq, lane) * sin_ref[at, :]).astype(jnp.bfloat16)
    dk = jnp.where(low, dk_acc[0], dk_acc[1])
    dk_ref[...] = (dk * cos_ref[...] - swap_halves(dk, lane_all) * sin_ref[...]).astype(jnp.bfloat16)
    dv_ref[...] = jnp.where(low, dv_acc[0], dv_acc[1]).astype(jnp.bfloat16)


def attend(q, k, v, feats, width, tile=512):
    qf, kf, cosine, sine = feats
    rows = q[0].shape[0]

    def from_col(start):
        return pl.BlockSpec((rows, PAIR), lambda j: (0, start // PAIR + j))

    col = from_col(0)
    whole = pl.BlockSpec((rows, PAIR), lambda j: (0, 0))
    bf = jax.ShapeDtypeStruct((rows, width), jnp.bfloat16)
    pairs = width // PAIR
    return pl.pallas_call(
        functools.partial(attend_kernel, tile=min(tile, rows)),
        grid=(pairs,),
        in_specs=[from_col(q[1]), from_col(k[1]), from_col(v[1]), whole, whole, whole, whole],
        out_specs=[col, col, col, col],
        out_shape=[bf, jax.ShapeDtypeStruct((rows, width), jnp.float32), bf, bf],
        cost_estimate=pl.CostEstimate(flops=8 * pairs * rows * rows * PAIR, bytes_accessed=rows * width * 24, transcendentals=2 * pairs * rows * rows),
        name="attend",
    )(q[0], k[0], v[0], qf, kf, cosine, sine)


def attend_back(qr, kr, v, o, do, lse, feats, tile=256):
    qf, kf, cosine, sine = feats
    rows, width = qr.shape
    col = pl.BlockSpec((rows, PAIR), lambda j: (0, j))
    whole = pl.BlockSpec((rows, PAIR), lambda j: (0, 0))
    bf = jax.ShapeDtypeStruct((rows, width), jnp.bfloat16)
    pairs = width // PAIR
    return pl.pallas_call(
        functools.partial(attend_back_kernel, tile=tile),
        grid=(pairs,),
        in_specs=[col] * 6 + [whole] * 4,
        out_specs=[col, col, col],
        out_shape=[bf, bf, bf],
        scratch_shapes=[pltpu.VMEM((2, rows, PAIR), jnp.float32), pltpu.VMEM((2, rows, PAIR), jnp.float32)],
        cost_estimate=pl.CostEstimate(flops=20 * pairs * rows * rows * PAIR, bytes_accessed=rows * width * 20, transcendentals=2 * pairs * rows * rows),
        name="attend_back",
    )(qr, kr, v, o, do, lse, qf, kf, cosine, sine)


def tables(image_sizes, count):
    images = image_sizes.shape[0]
    places = jnp.arange(count, dtype=jnp.int32)
    ends = jnp.cumsum(image_sizes)
    passed = places[:, None] >= ends[None, :]
    segment = jnp.sum(passed.astype(jnp.int32), -1)
    start = jnp.sum(jnp.where(passed, image_sizes[None, :], 0), -1)
    place = (places - start).astype(jnp.float32)
    half = HEAD_DIM // 2
    lane = jnp.arange(PAIR, dtype=jnp.int32)
    freqs = 100.0 ** (-((lane % half).astype(jnp.float32) / half))
    angles = place[:, None] * freqs[None, :]
    sign = jnp.where(lane % HEAD_DIM < half, -1.0, 1.0)
    member = (lane % HEAD_DIM)[None, :] == segment[:, None]
    slot = ((lane % HEAD_DIM) < images)[None, :]
    kf = member.astype(jnp.bfloat16)
    qf = jnp.where(slot & ~member, -FAR, 0.0).astype(jnp.bfloat16)
    return qf, kf, jnp.cos(angles), jnp.sin(angles) * sign[None, :]


norm_epsilon = 1e-06
BF = jnp.bfloat16
F32 = jnp.float32


def mm(a, b):
    return jnp.dot(a, b, preferred_element_type=F32)


def mm_t(a, b):
    return lax.dot_general(a, b, (((1,), (1,)), ((), ())), preferred_element_type=F32)


def t_mm(a, b):
    return lax.dot_general(a, b, (((0,), (0,)), ((), ())), preferred_element_type=F32)


def norm(rows, gain, shift):
    centre = jnp.mean(rows, -1, keepdims=True)
    centred = rows - centre
    spread = jnp.mean(centred * centred, -1, keepdims=True)
    scale = lax.rsqrt(spread + norm_epsilon)
    hat = centred * scale
    return (hat * gain + shift).astype(BF), (centre, scale)


def norm_back(grad, rows, stats, gain):
    centre, scale = stats
    hat = (rows - centre) * scale
    w = grad * gain
    back = scale * (w - jnp.mean(w, -1, keepdims=True) - hat * jnp.mean(w * hat, -1, keepdims=True))
    return back, jnp.sum(grad * hat, 0), jnp.sum(grad, 0)


def body(tokens, cotangent, lengths, norm1_gain, norm1_shift, qkv_w, qkv_b, out_w, out_b, norm2_gain, norm2_shift,
         normy_gain, normy_shift, cq_w, cq_b, ckv_w, ckv_b, cout_w, cout_b, norm3_gain, norm3_shift, up_w, up_b, down_w, down_b):
    batches = tokens.shape[0]
    members = lax.axis_size("mp")
    n_dp = lax.axis_size("dp")
    assert members == 2 * batches
    me = lax.axis_index("mp")
    view = me // batches
    batch = me % batches
    local = tokens.shape[2]
    rows = local * members
    width = tokens.shape[3]
    r = qkv_w.shape[1]
    hw = cq_w.shape[2]
    fw = up_w.shape[2]
    partner = [(i, (i + batches) % members) for i in range(members)]
    groups = [[d * members + v * batches + b for d in range(n_dp) for b in range(batches)] for v in range(2)]
    both = ("dp", "mp")

    def of_view(a, which):
        return lax.dynamic_index_in_dim(a, which, 0, keepdims=False)

    def swap_view(a):
        return jnp.stack([of_view(a, view), lax.ppermute(of_view(a, 1 - view), "mp", partner)], 0)

    def gather(pack):
        return lax.all_gather(swap_view(pack), both, axis=0, axis_index_groups=groups)

    def placed(g, start, parts, w):
        piece = g[..., start : start + parts * w].reshape(n_dp, batches, 2, r, parts, w)
        return piece.transpose(0, 3, 4, 2, 1, 5).reshape(n_dp * r, parts * members * w)

    pack_a = jnp.concatenate(
        [qkv_w.reshape(2, r, -1), out_w.swapaxes(1, 2), cq_w, ckv_w.reshape(2, r, -1), cout_w.swapaxes(1, 2)], -1)
    pack_f = jnp.concatenate([up_w, down_w.swapaxes(1, 2)], -1)
    got_a = gather(pack_a)
    got_f = gather(pack_f)

    bias_pack = jnp.concatenate([qkv_b.reshape(2, -1), cq_b, ckv_b.reshape(2, -1), up_b], -1)
    bias_len = bias_pack.shape[-1]
    bias_rows = -(-bias_len // width)
    bias_pack = jnp.pad(bias_pack, ((0, 0), (0, bias_rows * width - bias_len))).reshape(2, 1, bias_rows, width)
    bias_pack = jnp.broadcast_to(bias_pack, (2, batches, bias_rows, width))
    by_view = tokens.swapaxes(0, 1)
    sent_x = jnp.concatenate([by_view, bias_pack], 2).reshape(members, local + bias_rows, width)
    got_x = lax.all_to_all(sent_x, "mp", 0, 0, tiled=True)
    got_y = lax.all_to_all(by_view[::-1].reshape(members, local, width), "mp", 0, 0, tiled=True)
    got_z = lax.all_to_all(cotangent.swapaxes(0, 1).reshape(members, local, width), "mp", 0, 0, tiled=True)
    x_low = got_x[:, :local].reshape(rows, width)
    bias_all = got_x[:, local:].reshape(2, batches, bias_rows * width).astype(F32)
    bias_all = jnp.where(view == 0, bias_all, bias_all[::-1]).reshape(members, -1)
    x = x_low.astype(F32)
    y = got_y.reshape(rows, width).astype(F32)
    dz_low = got_z.reshape(rows, width)
    dz = dz_low.astype(F32)

    def bias_of(start, parts, w):
        return bias_all[:, start : start + parts * w].reshape(members, parts, w).swapaxes(0, 1).reshape(1, -1)

    qkv_bias = bias_of(0, 3, hw)
    cq_bias = bias_of(3 * hw, 1, hw)
    ckv_bias = bias_of(4 * hw, 2, hw)
    up_bias = bias_of(6 * hw, 1, fw)

    def mine(a):
        return of_view(a, view).astype(F32)[None]

    g1, s1, ob, g2, s2, gy, sy, cob, g3, s3, db = [
        mine(a) for a in (norm1_gain, norm1_shift, out_b, norm2_gain, norm2_shift, normy_gain, normy_shift, cout_b, norm3_gain, norm3_shift, down_b)]

    feats = tables(of_view(lengths[:, 0], batch), rows)

    w_qkv = placed(got_a, 0, 3, hw)
    w_out = placed(got_a, 3 * hw, 1, hw)
    w_cq = placed(got_a, 4 * hw, 1, hw)
    w_ckv = placed(got_a, 5 * hw, 2, hw)
    w_cout = placed(got_a, 7 * hw, 1, hw)
    w_up = placed(got_f, 0, 1, fw)
    w_down = placed(got_f, fw, 1, fw)

    n1, st1 = norm(x, g1, s1)
    side, sty = norm(y, gy, sy)
    qkv = mm(n1, w_qkv) + qkv_bias
    att, lse, q_rot, k_rot = attend((qkv, 0), (qkv, width), (qkv, 2 * width), feats, width)
    v_low = qkv[:, 2 * width :].astype(BF)
    middle = x + mm_t(att, w_out) + ob
    n2, st2 = norm(middle, g2, s2)
    cq = mm(n2, w_cq) + cq_bias
    ckv = mm(side, w_ckv) + ckv_bias
    catt, clse, cq_rot, ck_rot = attend((cq, 0), (ckv, 0), (ckv, width), feats, width)
    cv_low = ckv[:, width:].astype(BF)
    middle2 = middle + mm_t(catt, w_cout) + cob
    n3, st3 = norm(middle2, g3, s3)
    hidden_in = mm(n3, w_up) + up_bias
    phi = 0.5 * (1.0 + lax.erf(hidden_in * (0.5 ** 0.5)))
    slope = (phi + hidden_in * jnp.exp(-0.5 * hidden_in * hidden_in) * (0.5 / math.pi) ** 0.5).astype(BF)
    hidden = (hidden_in * phi).astype(BF)
    hidden, slope = lax.optimization_barrier((hidden, slope))
    output = (middle2 + mm_t(hidden, w_down) + db).astype(BF)

    d_hidden = (mm(dz_low, w_down) * slope.astype(F32)).astype(BF)
    grad_up = t_mm(n3, d_hidden)
    grad_down = t_mm(dz_low, hidden)
    part, gg3, gs3 = norm_back(mm_t(d_hidden, w_up), middle2, st3, g3)
    d_mid2 = dz + part
    d_cross = d_mid2.astype(BF)
    grad_cout = t_mm(d_cross, catt)
    d_catt = mm(d_cross, w_cout).astype(BF)
    dcq, dck, dcv = attend_back(cq_rot, ck_rot, cv_low, catt, d_catt, clse, feats)
    grad_cq = t_mm(n2, dcq)
    grad_ckv = jnp.concatenate([t_mm(side, dck), t_mm(side, dcv)], -1)
    part, gg2, gs2 = norm_back(mm_t(dcq, w_cq), middle, st2, g2)
    d_mid = d_mid2 + part
    other, ggy, gsy = norm_back(mm_t(dck, w_ckv[:, :width]) + mm_t(dcv, w_ckv[:, width:]), y, sty, gy)
    d_branch = d_mid.astype(BF)
    grad_out = t_mm(d_branch, att)
    d_att = mm(d_branch, w_out).astype(BF)
    dq, dk, dv = attend_back(q_rot, k_rot, v_low, att, d_att, lse, feats)
    grad_qkv = jnp.concatenate([t_mm(n1, dq), t_mm(n1, dk), t_mm(n1, dv)], -1)
    part, gg1, gs1 = norm_back(mm_t(dq, w_qkv[:, :width]) + mm_t(dk, w_qkv[:, width : 2 * width]) + mm_t(dv, w_qkv[:, 2 * width :]), x, st1, g1)
    own = d_mid + part

    def packed(g, parts, w):
        piece = g.astype(BF).reshape(n_dp, r, parts, 2, batches, w)
        return piece.transpose(0, 4, 3, 1, 2, 5).reshape(n_dp * batches, 2, r, parts * w)

    def settle(pieces):
        whole = jnp.concatenate(pieces, -1)
        mine = lax.psum_scatter(whole, both, scatter_dimension=0, axis_index_groups=groups)
        theirs = lax.ppermute(mine[1], "mp", partner)
        keep = mine[0].astype(F32)
        theirs = theirs.astype(F32)
        return jnp.stack([jnp.where(view == 0, keep, theirs), jnp.where(view == 0, theirs, keep)], 0)

    sum_f = settle([packed(grad_up, 1, fw), packed(grad_down, 1, fw)])
    sum_a = settle([packed(grad_qkv, 3, hw), packed(grad_out, 1, hw), packed(grad_cq, 1, hw), packed(grad_ckv, 2, hw), packed(grad_cout, 1, hw)])

    def bias_sum(g, parts, w):
        total = jnp.sum(g.astype(F32), 0).reshape(parts, 2, batches, w)
        return jnp.where(view == 0, total, total[:, ::-1]).reshape(-1)

    small = [gg1, gs1, jnp.sum(d_branch.astype(F32), 0), gg2, gs2, ggy, gsy, jnp.sum(d_cross.astype(F32), 0), gg3, gs3, jnp.sum(dz, 0)]
    bias_q = jnp.concatenate([bias_sum(dq, 1, hw), bias_sum(dk, 1, hw), bias_sum(dv, 1, hw)])
    bias_ckv = jnp.concatenate([bias_sum(dck, 1, hw), bias_sum(dcv, 1, hw)])
    flat = jnp.concatenate(small + [bias_q, bias_sum(dcq, 1, hw), bias_ckv, bias_sum(d_hidden, 1, fw)])
    flat = jnp.stack([jnp.where(view == 0, flat, 0.0), jnp.where(view == 1, flat, 0.0)], 0)
    total = lax.psum(flat, both)
    sm = [total[:, i * width : (i + 1) * width] for i in range(11)]
    at = 11 * width

    def bias_out(start, parts, w):
        piece = total[:, start : start + parts * members * w].reshape(2, parts, members, w)
        piece = lax.dynamic_index_in_dim(piece, me, 2, keepdims=False)
        return piece if parts > 1 else piece[:, 0]

    qkv_bias_grad = bias_out(at, 3, hw)
    cq_bias_grad = bias_out(at + 3 * width, 1, hw)
    ckv_bias_grad = bias_out(at + 4 * width, 2, hw)
    up_bias_grad = bias_out(at + 6 * width, 1, fw)

    back = lax.all_to_all(output.reshape(members, local, width), "mp", 0, 0, tiled=True)
    block_output = back.reshape(2, batches, local, width).swapaxes(0, 1)
    sent = jnp.stack([own.astype(BF).reshape(members, local, width), other.astype(BF).reshape(members, local, width)], 1)
    got = lax.all_to_all(sent, "mp", 0, 0, tiled=True).astype(F32).reshape(2, batches, 2, local, width)
    input_grad = (got[:, :, 0] + got[::-1, :, 1]).swapaxes(0, 1)

    qkv_wg = sum_a[..., : 3 * hw].reshape(2, r, 3, hw)
    out_wg = sum_a[..., 3 * hw : 4 * hw].swapaxes(1, 2)
    cq_wg = sum_a[..., 4 * hw : 5 * hw]
    ckv_wg = sum_a[..., 5 * hw : 7 * hw].reshape(2, r, 2, hw)
    cout_wg = sum_a[..., 7 * hw :].swapaxes(1, 2)
    up_wg = sum_f[..., :fw]
    down_wg = sum_f[..., fw:].swapaxes(1, 2)
    return (block_output, input_grad, sm[0], sm[1], qkv_wg, qkv_bias_grad, out_wg, sm[2], sm[3], sm[4], sm[5], sm[6], cq_wg, cq_bias_grad,
            ckv_wg, ckv_bias_grad, cout_wg, sm[7], sm[8], sm[9], up_wg, up_bias_grad, down_wg, sm[10])


def solution(mesh):
    rows = P(None, None, ("dp", "mp"), None)
    wide = P(None, "dp", None, "mp")
    by_rows = P(None, "dp", "mp")
    by_cols = P(None, "mp", "dp")
    parts = P(None, None, "mp")
    flat = P(None, "mp")
    whole = P()
    in_specs = (rows, rows, P(None, "dp", None), whole, whole, wide, parts, by_cols, whole, whole, whole, whole, whole, by_rows, flat, wide, parts,
                by_cols, whole, whole, whole, by_rows, flat, by_cols, whole)
    out_specs = (rows, rows, whole, whole, wide, parts, by_cols, whole, whole, whole, whole, whole, by_rows, flat, wide, parts, by_cols, whole,
                 whole, whole, by_rows, flat, by_cols, whole)
    return jax.shard_map(body, mesh=mesh, in_specs=in_specs, out_specs=out_specs, check_vma=False)
```

time: 2580 us -> 996 us (0.39)
  waiting for transfers between devices: 1250 us -> 358 us
  matrix products: 446 us -> 121 us
  other arithmetic: 243 us -> 55.2 us
  blocking collectives: 173 us -> 0 us
  Pallas kernels: 0 us -> 129 us
  local copies, waits for them, and re-layouts: 405 us -> 280 us
    reduce_scatter x25 -> x2, waiting for transfers between devices: 723 us -> 202 us  [settle(): lax.psum_scatter(whole, both, scatter_dimension=0, axis_index_groups=groups)]
    all_gather x32 -> x2, waiting for transfers between devices: 372 us -> 49.4 us  [gather(): lax.all_gather(swap_view(pack), both, axis=0, axis_index_groups=groups)]
    dot_general x180 -> x27, matrix products: 414 us -> 121 us  [the longest x10 42 us: t_mm(): lax.dot_general(a, b, (((0,), (0,)), ((), ())), preferred_element_type=F32)]
    dynamic_update_slice x32 -> x0, local copies, waits for them, and re-layouts: 135 us -> none  [attend(): results, log_totals = lax.map(one_block, (query_blocks, segment_blocks))]
    psum x1, waiting for transfers between devices: 133 us -> 0.02 us  [body(): total = lax.psum(flat, both)]
    pallas_call x0 -> x4, Pallas kernels: none -> 129 us  [the longest x2 80.2 us: attend_back(): pl.pallas_call(functools.partial(attend_back_kernel, tile=tile), grid=(pa...]
    all_gather x3 -> x0, blocking collectives: 99.7 us -> none  [the longest x1 35.1 us: fetch(): lax.all_gather(out_weight, 'dp', axis=2, tiled=True)]
    reduce_sum x67 -> x15, other arithmetic: 101 us -> 11.3 us  [the longest x6 4.51 us: bias_sum(): total = jnp.sum(g.astype(F32), 0).reshape(parts, 2, batches, w)]
  transfers between devices with their start and end apart: 63 -> 14, of which waited for: 42 -> 11; matrix products, arithmetic and copies ran while one was open for 38% -> 20% of each run, Pallas kernels for 0% -> 0%
where the time goes in v1:
time: 996 us; the launch traced here: 986 us
  waiting for transfers between devices  358 us (36%)
  local copies, waits for them, and re-layouts  280 us (28%)
  Pallas kernels  129 us (13%)
  matrix products  121 us (12%)
  other arithmetic  55.2 us (6%)
  starting transfers between devices  27 us (3%)
  between operations  15.5 us (2%)
    reduce_scatter x2, waiting for transfers between devices, settle(): lax.psum_scatter(whole, both, scatter_dimension=0, axis_index_groups=groups)  202 us
    pallas_call x2, Pallas kernels, attend_back(): pl.pallas_call(functools.partial(attend_back_kernel, tile=tile), grid=(pa...  80.2 us
    all_gather x2, waiting for transfers between devices, gather(): lax.all_gather(swap_view(pack), both, axis=0, axis_index_groups=groups)  49.4 us
    pallas_call x2, Pallas kernels, attend(): pl.pallas_call(functools.partial(attend_kernel, tile=min(tile, rows)), gr...  48.8 us
    unnamed x203, local copies, waits for them, and re-layouts  43.4 us
    reshape x7, local copies, waits for them, and re-layouts, placed(): piece.transpose(0, 3, 4, 2, 1, 5).reshape(n_dp * r, parts * members * w)  43.2 us
    dot_general x10, matrix products, t_mm(): lax.dot_general(a, b, (((0,), (0,)), ((), ())), preferred_element_type=F32)  42 us
    transpose x6, local copies, waits for them, and re-layouts, packed(): piece.transpose(0, 4, 3, 1, 2, 5).reshape(n_dp * batches, 2, r, parts * w)  41.4 us
  transfers between devices with their start and end apart: 14, of which 11 were waited for; matrix products, arithmetic and copies ran while one was open for 20% of the time, Pallas kernels for 0%

profile of v1, /device:TPU:0, one launch (start us, length us, event | category | flops | bytes accessed | tf_op | source)
XLA Modules:
  0.0 986.0 jit_solution(7146372218957324373)
XLA Ops:
  15.6 9.1 collective-permute-done
  28.9 6.5 collective-permute-done.1
  38.1 3.6 all-to-all-start.1
  45.4 16.3 %all-to-all-done.1 = bf16[4,256,768]{2,1,0:T(8,128)(2,1)S(1)} async-done(((bf16[4,256,768]{2,1,0:T(8,128)(2,1)}), bf16[4,256,768]{2,1,0:T(8,128)(2,1)S(1)}, u32[]{:S(2)}, u32[]{:S(2)}) %all-to-all-start.1) | async-done | bytes 1572896 | tf_op jit(solution)/shard_map/all_to_all | solution.py:265
  61.7 3.7 all-to-all-start.3
  72.9 12.5 %all-to-all-done.3 = bf16[4,256,768]{2,1,0:T(8,128)(2,1)S(1)} async-done(((bf16[4,256,768]{2,1,0:T(8,128)(2,1)}), bf16[4,256,768]{2,1,0:T(8,128)(2,1)S(1)}, u32[]{:S(2)}, u32[]{:S(2)}) %all-to-all-start.3) | async-done | bytes 1572896 | tf_op jit(solution)/shard_map/all_to_all | solution.py:266
  86.6 3.6 all-to-all-start
  94.9 15.8 %all-to-all-done = bf16[4,259,768]{2,1,0:T(8,128)(2,1)S(1)} async-done(((bf16[4,259,768]{2,1,0:T(8,128)(2,1)}), bf16[4,259,768]{2,1,0:T(8,128)(2,1)S(1)}, u32[]{:S(2)}, u32[]{:S(2)}) %all-to-all-start) | async-done | bytes 1591328 | tf_op jit(solution)/shard_map/all_to_all | solution.py:264
  115.3 15.0 %copy.166 = bf16[32,96,1536]{1,2,0:T(8,128)(2,1)} copy(bf16[32,96,1536]{2,1,0:T(8,128)(2,1)} %all-gather.5.cloned.1.call-done) | data formatting | bytes 18874368 | tf_op jit(solution)/shard_map/all_gather | solution.py:245
  132.4 5.0 slice.199
  137.4 4.7 fusion.91
  142.1 49.4 %all-gather.7.cloned.1.call-done = bf16[32,96,1536]{2,1,0:T(8,128)(2,1)} async-done(((bf16[2,96,1536]{2,1,0:T(8,128)(2,1)}), bf16[32,96,1536]{2,1,0:T(8,128)(2,1)}) %all-gather.7.cloned.1.call-update) | async-done | bytes 9437200 | tf_op jit(solution)/shard_map/all_gather | solution.py:245
  191.6 8.3 fusion.92
  199.8 9.4 copy.175
  209.3 11.8 %reshape.998 = bf16[768,3072]{1,0:T(8,128)(2,1)} reshape(bf16[8,96,1,2,2,768]{5,4,3,1,0,2:T(2,128)(2,1)} %copy.175) | data formatting | bytes 9437184 | tf_op jit(solution)/shard_map/reshape | solution.py:249
  221.1 9.4 copy.174
  230.4 11.2 %reshape.996 = bf16[768,3072]{1,0:T(8,128)(2,1)} reshape(bf16[8,96,1,2,2,768]{5,4,3,1,0,2:T(2,128)(2,1)} %copy.174) | data formatting | bytes 9437184 | tf_op jit(solution)/shard_map/reshape | solution.py:249
  241.7 3.8 copy.211
  245.5 5.2 reshape.991
  250.6 4.9 convolution_add_fusion.1.k_ref.v_ref
  264.6 8.1 copy.167
  272.7 8.3 reshape.980
  284.4 6.3 convolution_add_fusion.q_ref.k_ref.v_ref
  290.8 3.6 copy-done
  295.7 24.1 %attend.2 = (bf16[1024,768]{1,0:T(8,128)(2,1)}, f32[1024,768]{1,0:T(8,128)}, bf16[1024,768]{1,0:T(8,128)(2,1)}, bf16[1024,768]{1,0:T(8,128)(2,1)}) custom-call(f32[1024,2304]{1,0:T(8,128)} %copy-done, f32[1024,2304]{1,0:T(8,128)} %copy-done, f32[1024,2304]{1,0:T(8,128)} %copy-done, bf16[1024,128]{1,0:T(8,128)(2,1)} %select_convert_fusion.qf_ref, ...), custom_call_target="tpu_custom_call" | custom-call | flops 6442450944 | bytes 18874368 | tf_op jit(solution)/shard_map/attend/pallas_call | solution.py:135
  325.0 3.4 convolution_add_fusion.3.q_ref
  328.3 24.7 %attend.3 = (bf16[1024,768]{1,0:T(8,128)(2,1)}, f32[1024,768]{1,0:T(8,128)}, bf16[1024,768]{1,0:T(8,128)(2,1)}, bf16[1024,768]{1,0:T(8,128)(2,1)}) custom-call(f32[1024,768]{1,0:T(8,128)} %convolution_add_fusion.3.q_ref, f32[1024,1536]{1,0:T(8,128)} %copy-done.39, f32[1024,1536]{1,0:T(8,128)} %copy-done.39, bf16[1024,128]{1,0:T(8,128)(2,1)} %select_convert_fusion.qf_ref, ...), custom_call_target="tpu_custom_call" | custom-call | flops 6442450944 | bytes 18874368 | tf_op jit(solution)/shard_map/attend/pallas_call | solution.py:135
  353.0 3.4 fusion.95
  357.0 13.4 %fusion.4 = (bf16[1024,3072]{1,0:T(8,128)(2,1)}, bf16[1024,3072]{1,0:T(8,128)(2,1)}) fusion(f32[3072]{0:T(1024)S(1)} %add.343, bf16[768,3072]{1,0:T(8,128)(2,1)S(1)} %bitcast.309, f32[1024,768]{1,0:T(8,128)S(1)} %get-tuple-element.249, f32[768]{0:T(1024)S(1)} %get-tuple-element.263, f32[768]{0:T(1024)S(1)} %fusion.71, f32[1024]{0:T(1024)S(1)} %add_rsqrt_fusion, ...), kind=kOutput, calls=%fused_computation.5 | convolution fusion | flops 4873519104 | bytes 20473856 | tf_op jit(solution)/shard_map/dot_general | solution.py:191
  370.4 7.4 convert_reduce_fusion
  377.8 5.7 multiply_reduce_fusion
  390.2 40.2 %attend_back.2 = (bf16[1024,768]{1,0:T(8,128)(2,1)}, bf16[1024,768]{1,0:T(8,128)(2,1)}, bf16[1024,768]{1,0:T(8,128)(2,1)}) custom-call(bf16[1024,768]{1,0:T(8,128)(2,1)} %get-tuple-element.44.qr_ref, bf16[1024,768]{1,0:T(8,128)(2,1)} %get-tuple-element.45.kr_ref, bf16[1024,768]{1,0:T(8,128)(2,1)} %slice.317.v_ref, ...), custom_call_target="tpu_custom_call" | custom-call | flops 16106127360 | bytes 15728640 | tf_op jit(solution)/shard_map/attend_back/pallas_call | solution.py:153
  432.1 4.5 convolution_convert_fusion.7
  445.7 39.9 %attend_back.3 = (bf16[1024,768]{1,0:T(8,128)(2,1)}, bf16[1024,768]{1,0:T(8,128)(2,1)}, bf16[1024,768]{1,0:T(8,128)(2,1)}) custom-call(bf16[1024,768]{1,0:T(8,128)(2,1)} %get-tuple-element.48.qr_ref, bf16[1024,768]{1,0:T(8,128)(2,1)} %get-tuple-element.49.kr_ref, bf16[1024,768]{1,0:T(8,128)(2,1)} %slice.316.v_ref, ...), custom_call_target="tpu_custom_call" | custom-call | flops 16106127360 | bytes 15728640 | tf_op jit(solution)/shard_map/attend_back/pallas_call | solution.py:153
  487.4 3.3 fusion.35
  492.9 4.1 fusion.26
  506.7 3.7 multiply_reduce_fusion.1
  515.9 5.6 reshape.1018
  521.5 4.9 copy.183
  526.4 5.4 reshape.1015
  531.8 4.9 copy.181
  537.2 5.4 reshape.1013
  542.6 4.9 copy.180
  547.5 3.4 pad_maximum_fusion.1
  551.0 8.9 convert_element_type.254
  559.8 5.8 copy.179
  570.0 6.4 convert_element_type.258
  579.1 5.7 constant_dynamic-update-slice_fusion.25
  591.9 9.6 fusion.6
  601.5 6.7 copy.186
  608.2 11.7 %reshape.1027 = bf16[8,96,1,2,2,768]{5,4,3,1,0,2:T(2,128)(2,1)} reshape(bf16[768,3072]{1,0:T(8,128)(2,1)} %copy.186) | data formatting | bytes 9437184 | tf_op jit(solution)/shard_map/reshape | solution.py:342
  619.8 10.4 %convolution_convert_fusion.1 = bf16[768,3072]{1,0:T(8,128)(2,1)} fusion(bf16[1024,3072]{1,0:T(8,128)(2,1)} %copy-done.73, f32[1024,768]{1,0:T(8,128)} %copy-done.9, f32[768]{0:T(1024)S(1)} %copy-done.55, f32[768]{0:T(1024)S(1)} %fusion.71, f32[1024]{0:T(1024)S(1)} %add_rsqrt_fusion, f32[1024]{0:T(1024)S(1)} %broadcast_multiply_fusion.8), kind=kOutput, calls=%fused_computation.14 | convolution fusion | flops 4838129664 | bytes 14170112 | tf_op jit(solution)/shard_map/dot_general | solution.py:199
  630.2 11.6 %reshape.1025 = bf16[8,96,1,2,2,768]{5,4,3,1,0,2:T(2,128)(2,1)} reshape(bf16[768,3072]{1,0:T(8,128)(2,1)} %convolution_convert_fusion.1) | data formatting | bytes 9437184 | tf_op jit(solution)/shard_map/reshape | solution.py:342
  641.8 11.9 %copy.185 = bf16[8,2,2,96,1,768]{3,5,2,1,0,4:T(8,128)(2,1)} copy(bf16[8,2,2,96,1,768]{5,1,2,3,0,4:T(2,128)(2,1)} %bitcast.279) | data formatting | bytes 9437184 | tf_op jit(solution)/shard_map/transpose | solution.py:343
  653.8 11.9 %copy.187 = bf16[8,2,2,96,1,768]{3,5,2,1,0,4:T(8,128)(2,1)} copy(bf16[8,2,2,96,1,768]{5,1,2,3,0,4:T(2,128)(2,1)} %bitcast.276) | data formatting | bytes 9437184 | tf_op jit(solution)/shard_map/transpose | solution.py:343
  665.7 13.3 %pad_maximum_fusion = bf16[16,2,96,1536]{2,3,1,0:T(8,128)(2,1)} fusion(bf16[16,2,96,768]{2,3,1,0:T(8,128)(2,1)} %bitcast.273, bf16[16,2,96,768]{2,3,1,0:T(8,128)(2,1)} %bitcast.272), kind=kLoop, calls=%fused_computation.6 | loop fusion | flops 18874368 | bytes 18874368 | tf_op jit(solution)/shard_map/concatenate | solution.py:346
  679.7 10.1 %add_convert_fusion.1 = bf16[1024,768]{1,0:T(8,128)(2,1)} fusion(f32[1024,768]{1,0:T(8,128)} %copy-done.9, bf16[1024,3072]{1,0:T(8,128)(2,1)} %get-tuple-element.42, bf16[768,3072]{1,0:T(8,128)(2,1)} %reshape.998, f32[768]{0:T(1024)S(1)} %fusion.75), kind=kOutput, calls=%fused_computation.70 | convolution fusion | flops 4834197504 | bytes 15731712 | tf_op jit(solution)/shard_map/dot_general | solution.py:195
  689.9 4.4 all-to-all-start.2
  702.2 12.3 %all-to-all-done.2 = bf16[4,256,768]{2,1,0:T(8,128)(2,1)} async-done(((bf16[4,256,768]{2,1,0:T(8,128)(2,1)}), bf16[4,256,768]{2,1,0:T(8,128)(2,1)}, u32[]{:S(2)}, u32[]{:S(2)}) %all-to-all-start.2) | async-done | bytes 1572896 | tf_op jit(solution)/shard_map/all_to_all | solution.py:379
  714.4 3.7 all-to-all-start.4
  727.7 27.4 %all-to-all-done.4 = bf16[4,2,256,768]{3,2,1,0:T(8,128)(2,1)S(1)} async-done(((bf16[4,2,256,768]{3,2,1,0:T(8,128)(2,1)}), bf16[4,2,256,768]{3,2,1,0:T(8,128)(2,1)S(1)}, u32[]{:S(2)}, u32[]{:S(2)}) %all-to-all-start.4) | async-done | bytes 3145760 | tf_op jit(solution)/shard_map/all_to_all | solution.py:382
  758.2 66.9 %reduce-scatter.3.cloned.1.call-done = bf16[1,2,96,1536]{2,3,1,0:T(8,128)(2,1)} async-done(((bf16[16,2,96,1536]{2,3,1,0:T(8,128)(2,1)}), bf16[1,2,96,1536]{2,3,1,0:T(8,128)(2,1)}) %reduce-scatter.3.cloned.1.call-update) | async-done | bytes 589840 | tf_op jit(solution)/shard_map/reduce_scatter | solution.py:347
  827.7 135.3 %reduce-scatter.5.cloned.1.call-done = bf16[1,2,96,1536]{2,3,1,0:T(8,128)(2,1)} async-done(((bf16[16,2,96,1536]{2,3,1,0:T(8,128)(2,1)}), bf16[1,2,96,1536]{2,3,1,0:T(8,128)(2,1)}) %reduce-scatter.5.cloned.1.call-update) | async-done | bytes 589840 | tf_op jit(solution)/shard_map/reduce_scatter | solution.py:347
  967.5 6.6 collective-permute-done.3
  (379 shorter events, 142.3 us)
Async XLA Ops:
  7.2 108.1 %all-gather.5.cloned.1.call-start = ((), (), s32[]{:S(2)}) async-start(), calls=%async_computation.10 | async-start | bytes 10027008 | tf_op jit(solution)/shard_map/all_gather | solution.py:245
  10.6 15.5 %copy-start.40 = (bf16[2,96,768]{2,1,0:T(8,128)(2,1)S(1)}, bf16[2,96,768]{2,1,0:T(8,128)(2,1)}, u32[]{:S(2)}) copy-start(bf16[2,96,768]{2,1,0:T(8,128)(2,1)} %param.46) | copy-start | bytes 884740
  12.6 12.1 %collective-permute-start = (bf16[96,1536]{0,1:T(8,128)(2,1)S(1)}, bf16[96,1536]{0,1:T(8,128)(2,1)S(1)}, u32[]{:S(2)}, u32[]{:S(2)}) collective-permute-start(bf16[96,1536]{0,1:T(8,128)(2,1)S(1)} %get-tuple-element.217), channel_id=1, source_target_pairs={{0,2},{1,3},{2,0},{3,1},{4,6},{5,7},{6,4},{7,5},{8,10},{9,11},{10,... | collective-permute-start | bytes 884744 | tf_op jit(solution)/shard_map/ppermute | solution.py:242
  24.7 11.5 %copy-start.26 = (bf16[2,2,256,768]{3,2,1,0:T(8,128)(2,1)S(1)}, bf16[2,2,256,768]{3,2,1,0:T(8,128)(2,1)}, u32[]{:S(2)}) copy-start(bf16[2,2,256,768]{3,2,1,0:T(8,128)(2,1)} %param.25) | copy-start | bytes 4718596
  26.0 165.5 %all-gather.7.cloned.1.call-start = ((), (), s32[]{:S(2)}) async-start(), calls=%async_computation.11 | async-start | bytes 10027008 | tf_op jit(solution)/shard_map/all_gather | solution.py:245
  27.1 8.3 collective-permute-start.1
  36.4 5.2 copy-start.71
  36.4 5.4 copy-start.69
  36.4 5.5 copy-start.56
  36.4 5.6 copy-start.62
  36.5 5.6 copy-start.70
  37.7 7.2 copy-start.57
  37.7 7.2 copy-start.58
  37.7 7.2 copy-start.59
  37.7 7.3 copy-start.60
  37.7 7.3 copy-start.63
  37.7 7.3 copy-start.64
  37.7 7.4 copy-start.65
  37.8 7.4 copy-start.66
  37.8 7.4 copy-start.67
  37.8 7.4 copy-start.68
  38.1 23.6 %all-to-all-start.1 = ((bf16[4,256,768]{2,1,0:T(8,128)(2,1)}), bf16[4,256,768]{2,1,0:T(8,128)(2,1)S(1)}, u32[]{:S(2)}, u32[]{:S(2)}) async-start(bf16[4,256,768]{2,1,0:T(8,128)(2,1)} %bitcast.293), calls=%async_computation.1 | async-start | bytes 3145728 | tf_op jit(solution)/shard_map/all_to_all | solution.py:265
  45.0 48.2 %copy-start.48 = (f32[768]{0:T(1024)}, f32[768]{0:T(1024)S(1)}, u32[]{:S(2)}) copy-start(f32[768]{0:T(1024)S(1)} %fusion.67) | copy-start | bytes 9220
  45.1 68.4 %copy-start.41 = (f32[768]{0:T(1024)}, f32[768]{0:T(1024)S(1)}, u32[]{:S(2)}) copy-start(f32[768]{0:T(1024)S(1)} %get-tuple-element.258) | copy-start | bytes 9220
  45.1 68.3 %copy-start.50 = (f32[768]{0:T(1024)}, f32[768]{0:T(1024)S(1)}, u32[]{:S(2)}) copy-start(f32[768]{0:T(1024)S(1)} %get-tuple-element.259) | copy-start | bytes 9220
  45.2 48.0 %copy-start.43 = (f32[768]{0:T(1024)}, f32[768]{0:T(1024)S(1)}, u32[]{:S(2)}) copy-start(f32[768]{0:T(1024)S(1)} %get-tuple-element.261) | copy-start | bytes 9220
  45.2 311.7 %copy-start.54 = (f32[768]{0:T(1024)}, f32[768]{0:T(1024)S(1)}, u32[]{:S(2)}) copy-start(f32[768]{0:T(1024)S(1)} %get-tuple-element.263) | copy-start | bytes 9220
  61.7 31.5 %copy-start.3 = (bf16[4,256,768]{2,1,0:T(8,128)(2,1)}, bf16[4,256,768]{2,1,0:T(8,128)(2,1)S(1)}, u32[]{:S(2)}) copy-start(bf16[4,256,768]{2,1,0:T(8,128)(2,1)S(1)} %all-to-all-done.1) | copy-start | bytes 4718596
  61.7 23.7 %all-to-all-start.3 = ((bf16[4,256,768]{2,1,0:T(8,128)(2,1)}), bf16[4,256,768]{2,1,0:T(8,128)(2,1)S(1)}, u32[]{:S(2)}, u32[]{:S(2)}) async-start(bf16[4,256,768]{2,1,0:T(8,128)(2,1)} %bitcast.294), calls=%async_computation.3 | async-start | bytes 3145728 | tf_op jit(solution)/shard_map/all_to_all | solution.py:266
  86.6 24.1 %all-to-all-start = ((bf16[4,259,768]{2,1,0:T(8,128)(2,1)}), bf16[4,259,768]{2,1,0:T(8,128)(2,1)S(1)}, u32[]{:S(2)}, u32[]{:S(2)}) async-start(bf16[4,259,768]{2,1,0:T(8,128)(2,1)} %bitcast.289), calls=%async_computation | async-start | bytes 3244032 | tf_op jit(solution)/shard_map/all_to_all | solution.py:264
  90.1 628.0 %all-reduce.3.cloned.1.call-start = ((), (), s32[]{:S(2)}) async-start(), calls=%async_computation.7 | async-start | bytes 258048 | tf_op jit(solution)/shard_map/psum | solution.py:365
  110.7 2.8 copy-start.1
  250.6 4.9 copy-start.24
  255.5 3.7 copy-start.39
  256.9 4.5 copy-start.20
  272.7 8.4 copy-start.19
  290.8 3.6 copy-start
  295.7 24.2 %slice-start = ((bf16[4,259,768]{2,1,0:T(8,128)(2,1)}), bf16[4,256,768]{2,1,0:T(8,128)(2,1)S(1)}, s32[]{:S(2)}) async-start(bf16[4,259,768]{2,1,0:T(8,128)(2,1)} %copy-done.1), calls=%async_computation.12 | async-start | bytes 3145728 | tf_op jit(solution)/shard_map/slice | solution.py:267
  295.7 24.2 %copy-start.33 = (bf16[768,768]{0,1:T(8,128)(2,1)S(1)}, bf16[768,768]{0,1:T(8,128)(2,1)}, u32[]{:S(2)}) copy-start(bf16[768,768]{0,1:T(8,128)(2,1)} %reshape.986) | copy-start | bytes 3538948
  328.3 24.7 %copy-start.11 = (f32[1024,768]{1,0:T(8,128)S(1)}, f32[1024,768]{1,0:T(8,128)}, u32[]{:S(2)}) copy-start(f32[1024,768]{1,0:T(8,128)} %copy-done.10) | copy-start | bytes 9437188
  353.0 4.0 slice-start.3
  353.0 3.9 slice-start.4
  356.4 27.1 %copy-start.9 = (f32[1024,768]{1,0:T(8,128)}, f32[1024,768]{1,0:T(8,128)S(1)}, u32[]{:S(2)}) copy-start(f32[1024,768]{1,0:T(8,128)S(1)} %get-tuple-element.249) | copy-start | bytes 9437188
  356.5 13.9 %slice-start.1 = ((s8[4718592]{0:T(1024)(128)(4,1)}), s8[4194304]{0:T(1024)(128)(4,1)S(1)}, s32[]{:S(2)}) async-start(s8[4718592]{0:T(1024)(128)(4,1)} %bitcast.306), calls=%async_computation.13 | async-start | bytes 8388608
  357.0 13.4 %copy-start.7 = (bf16[4,256,768]{2,1,0:T(8,128)(2,1)S(1)}, bf16[4,256,768]{2,1,0:T(8,128)(2,1)}, u32[]{:S(2)}) copy-start(bf16[4,256,768]{2,1,0:T(8,128)(2,1)} %copy-done.5) | copy-start | bytes 4718596
  357.0 13.4 %slice-start.2 = ((s8[4718592]{0:T(1024)(128)(4,1)}), s8[524288]{0:T(1024)(128)(4,1)S(1)}, s32[]{:S(2)}) async-start(s8[4718592]{0:T(1024)(128)(4,1)} %bitcast.306), calls=%async_computation.14 | async-start | bytes 1048576
  377.8 5.7 copy-start.73
  432.1 4.5 copy-start.32
  432.1 4.5 copy-start.36
  487.4 3.3 copy-start.30
  487.4 3.6 copy-start.22
  502.0 2.8 copy-start.25
  559.8 5.9 copy-start.45
  566.8 258.4 %reduce-scatter.3.cloned.1.call-start = ((), (), s32[]{:S(2)}) async-start(), calls=%async_computation.8 | async-start | bytes 13369344 | tf_op jit(solution)/shard_map/reduce_scatter | solution.py:347
  579.1 5.7 copy-start.18
  591.8 371.1 %reduce-scatter.5.cloned.1.call-start = ((), (), s32[]{:S(2)}) async-start(), calls=%async_computation.9 | async-start | bytes 13369344 | tf_op jit(solution)/shard_map/reduce_scatter | solution.py:347
  608.1 11.7 %copy-start.55 = (f32[768]{0:T(1024)S(1)}, f32[768]{0:T(1024)}, u32[]{:S(2)}) copy-start(f32[768]{0:T(1024)} %copy-done.54) | copy-start | bytes 9220
  689.9 24.5 %all-to-all-start.2 = ((bf16[4,256,768]{2,1,0:T(8,128)(2,1)}), bf16[4,256,768]{2,1,0:T(8,128)(2,1)}, u32[]{:S(2)}, u32[]{:S(2)}) async-start(bf16[4,256,768]{2,1,0:T(8,128)(2,1)} %bitcast.313), calls=%async_computation.2 | async-start | bytes 3145728 | tf_op jit(solution)/shard_map/all_to_all | solution.py:379
  694.3 3.4 copy-start.13
  694.3 4.6 copy-start.23
  714.4 40.6 %all-to-all-start.4 = ((bf16[4,2,256,768]{3,2,1,0:T(8,128)(2,1)}), bf16[4,2,256,768]{3,2,1,0:T(8,128)(2,1)S(1)}, u32[]{:S(2)}, u32[]{:S(2)}) async-start(bf16[4,2,256,768]{3,2,1,0:T(8,128)(2,1)} %pad_maximum_fusion.2), calls=%async_computation.4 | async-start | bytes 6291456 | tf_op jit(solution)/shard_map/all_to_all | solution.py:382
  826.2 139.3 %collective-permute-start.2 = (bf16[96,1536]{0,1:T(8,128)(2,1)S(1)}, bf16[96,1536]{0,1:T(8,128)(2,1)S(1)}, u32[]{:S(2)}, u32[]{:S(2)}) collective-permute-start(bf16[96,1536]{0,1:T(8,128)(2,1)S(1)} %slice_bitcast_fusion.2), channel_id=1, source_target_pairs={{0,2},{1,3},{2,0},{3,1},{4,6},{5,7},{6,4},{7,5},{8,10},{9,11},{10,... | collective-permute-start | bytes 884744 | tf_op jit(solution)/shard_map/ppermute | solution.py:348
  964.0 10.1 %collective-permute-start.3 = (bf16[96,1536]{0,1:T(8,128)(2,1)S(1)}, bf16[96,1536]{0,1:T(8,128)(2,1)S(1)}, u32[]{:S(2)}, u32[]{:S(2)}) collective-permute-start(bf16[96,1536]{0,1:T(8,128)(2,1)S(1)} %slice_bitcast_fusion), channel_id=1, source_target_pairs={{0,2},{1,3},{2,0},{3,1},{4,6},{5,7},{6,4},{7,5},{8,10},{9,11},{10,... | collective-permute-start | bytes 884744 | tf_op jit(solution)/shard_map/ppermute | solution.py:348
  966.6 7.5 copy-start.38
  (30 other events, 58.6 us)
Sparse Core Ops, SparseCore 0:
  26.1 82.8 all-gather.4
  111.9 79.5 all-gather.6
  566.9 120.4 all-reduce.2
  691.3 133.8 reduce-scatter.2
  829.1 133.8 reduce-scatter.4

commit v2 on v1

v2 whole, which is shorter than its diff:
```python
import functools
import math

import jax
import jax.numpy as jnp
from jax import lax
from jax.experimental import pallas as pl
from jax.experimental.pallas import tpu as pltpu
from jax.sharding import PartitionSpec as P

HEAD_DIM = 64
PAIR = 2 * HEAD_DIM
FAR = 1e30
BF = jnp.bfloat16
F32 = jnp.float32
LONGEST = 768
ROWS = 256
TALL = 1024
CHEAP = 16
FFN_ROWS = 1024
PART = 768
norm_epsilon = 1e-06


def mm(a, b):
    return jnp.dot(a, b, preferred_element_type=F32)


def mm_t(a, b):
    return lax.dot_general(a, b, (((1,), (1,)), ((), ())), preferred_element_type=F32)


def t_mm(a, b):
    return lax.dot_general(a, b, (((0,), (0,)), ((), ())), preferred_element_type=F32)


def each(count, size, step, carry=None):
    def go(i, c):
        return step(i, pl.ds(pl.multiple_of(i * size, size), size), c)

    return lax.fori_loop(0, count // size, go, carry)


def normed(rows, gain, shift):
    centred = rows - jnp.mean(rows, -1, keepdims=True)
    spread = jnp.mean(centred * centred, -1, keepdims=True)
    return (centred * lax.rsqrt(spread + norm_epsilon) * gain + shift).astype(BF)


def norm_back(grad, rows, gain):
    centred = rows - jnp.mean(rows, -1, keepdims=True)
    scale = lax.rsqrt(jnp.mean(centred * centred, -1, keepdims=True) + norm_epsilon)
    hat = centred * scale
    w = grad * gain
    back = scale * (w - jnp.mean(w, -1, keepdims=True) - hat * jnp.mean(w * hat, -1, keepdims=True))
    return back, col_sum(grad * hat), col_sum(grad)


def col_sum(a):
    return jnp.sum(a, 0, keepdims=True)


def swap_halves(u):
    lane = lax.broadcasted_iota(jnp.int32, u.shape, 1)
    half = HEAD_DIM // 2
    return jnp.where(lane % HEAD_DIM < half, pltpu.roll(u, PAIR - half, 1), pltpu.roll(u, half, 1))


def turn(u, cosine, sine):
    return u * cosine + swap_halves(u) * sine


def turn_back(u, cosine, sine):
    return u * cosine - swap_halves(u) * sine


def other_half(u):
    return pltpu.roll(u.astype(F32), HEAD_DIM, 1).astype(u.dtype)


def is_low(count):
    return lax.broadcasted_iota(jnp.int32, (count, PAIR), 1) < HEAD_DIM


def matrix(ref, start=0, stop=None):
    stop = ref.shape[4] if stop is None else stop
    return ref[:, 0, 0, :, start:stop].reshape(ref.shape[0] * ref.shape[3], stop - start)


def put_rows(ref, i, value, cols=None):
    blocks, rows = ref.shape[0], ref.shape[3]
    cols = slice(None) if cols is None else cols
    value = value.astype(ref.dtype)
    if blocks == 1:
        ref[0, 0, 0, pl.ds(pl.multiple_of(i * PART, PART), PART), cols] = value
    else:
        k = PART // rows
        ref[pl.ds(i * k, k), 0, 0, :, cols] = value.reshape(k, rows, value.shape[-1])


def store_heads(ref, at, tiles, cosine, sine):
    low = is_low(tiles[0].shape[0])
    scale = HEAD_DIM ** -0.5
    mixed = turn(tiles[1], cosine, sine)
    done = (turn(tiles[0], cosine, sine) * scale, jnp.where(low, mixed * scale, mixed), turn(tiles[2], cosine, sine), tiles[3], tiles[4])
    for i, tile in enumerate(done):
        ref[0, at, i * PAIR : (i + 1) * PAIR] = tile.astype(BF)


def split_tiles(a):
    return [a[:, i * PAIR : (i + 1) * PAIR] for i in range(a.shape[1] // PAIR)]


def norm_kernel(x_ref, gain_ref, shift_ref, n_ref):
    n_ref[...] = normed(x_ref[...].astype(F32), gain_ref[...], shift_ref[...])


def self_in_kernel(n_ref, w_ref, bias_ref, cos_ref, sin_ref, heads_ref):
    w = matrix(w_ref, 0, 5 * PAIR)
    bias = bias_ref[0, :, : 5 * PAIR]

    def one(i, at, c):
        store_heads(heads_ref, at, split_tiles(mm(n_ref[at, :], w) + bias), cos_ref[at, :], sin_ref[at, :])

    each(n_ref.shape[0], TALL, one)


def cross_in_kernel(n_ref, side_ref, w_ref, bias_ref, cos_ref, sin_ref, heads_ref):
    wq = matrix(w_ref, 0, 2 * PAIR)
    wkv = matrix(w_ref, PAIR, 5 * PAIR)
    bias = split_tiles(bias_ref[0, :, : 5 * PAIR])
    low = is_low(TALL)

    def one(i, at, c):
        q0, q2 = split_tiles(mm(n_ref[at, :], wq))
        k2, k0, v0, v2 = split_tiles(mm(side_ref[at, :], wkv))
        tiles = [q0, jnp.where(low, q2, k2), k0, v0, v2]
        store_heads(heads_ref, at, [t + b for t, b in zip(tiles, bias)], cos_ref[at, :], sin_ref[at, :])

    each(n_ref.shape[0], TALL, one)


def spans(rows):
    return ((0, LONGEST), (LONGEST, rows - LONGEST))


def attend_kernel(heads_ref, qf_ref, kf_ref, o_ref, lse_ref, *, tile):
    rows = heads_ref.shape[1]
    for start, size in spans(rows):
        near = pl.ds(start, size)
        low = is_low(size)
        t3, t1, t2, t4 = [heads_ref[0, near, i * PAIR : (i + 1) * PAIR] for i in range(1, 5)]
        kf = kf_ref[near, :]
        one = jnp.ones_like(t2)
        keys = (jnp.where(low, t1, kf), jnp.where(low, kf, t1), jnp.where(low, other_half(t3), kf))
        vals = (jnp.where(low, t2, one), jnp.where(low, one, t2), jnp.where(low, one, other_half(t4)))
        step = min(tile, size)
        low_t = is_low(step)
        for t in range(size // step):
            at = pl.ds(start + t * step, step)
            qf = qf_ref[at, :]
            q0 = heads_ref[0, at, :PAIR]
            queries = (jnp.where(low_t, q0, qf), jnp.where(low_t, qf, q0), jnp.where(low_t, heads_ref[0, at, PAIR : 2 * PAIR], qf))
            outs, lses = [], []
            for h in range(3):
                s = mm_t(queries[h], keys[h])
                top = jnp.max(s, -1, keepdims=True)
                o = mm(jnp.exp(s - top).astype(BF), vals[h])
                total = pltpu.roll(o, HEAD_DIM, 1)
                outs.append(o / total)
                lses.append(top + jnp.log(total))
            o_ref[0, at, :PAIR] = jnp.where(low_t, 0.0, outs[2]).astype(BF)
            o_ref[0, at, PAIR:] = jnp.where(low_t, outs[0], outs[1]).astype(BF)
            lse_ref[0, at, :PAIR] = jnp.where(low_t, 0.0, lses[2])
            lse_ref[0, at, PAIR:] = jnp.where(low_t, lses[0], lses[1])


def three_parts(u):
    a = u.astype(BF).astype(F32)
    b = (u - a).astype(BF).astype(F32)
    return a, b, u - a - b


def attend_back_kernel(heads_ref, o_ref, do_ref, lse_ref, qf_ref, kf_ref, cos_ref, sin_ref, out_ref, dq2_acc, dk_acc, dv_acc, *, tile):
    rows = heads_ref.shape[1]
    scale = HEAD_DIM ** -0.5
    for start, size in spans(rows):
        near = pl.ds(start, size)
        low = is_low(size)
        within = lax.broadcasted_iota(jnp.int32, (size, PAIR), 1) % HEAD_DIM
        t3, t1, t2, t4 = [heads_ref[0, near, i * PAIR : (i + 1) * PAIR] for i in range(1, 5)]
        ones3 = jnp.where(within < 3, 1.0, 0.0).astype(BF)
        kf = kf_ref[near, :] + jnp.where((within >= 3) & (within < 6), 1.0, 0.0).astype(BF)
        k2 = other_half(t3)
        raw_keys = (t1, t1, k2)
        keys = (jnp.where(low, t1, kf), jnp.where(low, kf, t1), jnp.where(low, k2, kf))
        vals = (jnp.where(low, t2, ones3), jnp.where(low, ones3, t2), jnp.where(low, t4, ones3))
        step = min(tile, size)
        low_t = is_low(step)
        high_t = ~low_t
        within_t = lax.broadcasted_iota(jnp.int32, (step, PAIR), 1) % HEAD_DIM
        for t in range(size // step):
            at = pl.ds(start + t * step, step)
            q0, q2 = heads_ref[0, at, :PAIR], heads_ref[0, at, PAIR : 2 * PAIR]
            do2, do0 = do_ref[0, at, :PAIR], do_ref[0, at, PAIR:]
            prod2 = do2.astype(F32) * o_ref[0, at, :PAIR].astype(F32)
            prod0 = do0.astype(F32) * o_ref[0, at, PAIR:].astype(F32)
            lse2, lse0 = lse_ref[0, at, :PAIR], lse_ref[0, at, PAIR:]
            qf = qf_ref[at, :].astype(F32)
            lse_swapped = pltpu.roll(lse0, HEAD_DIM, 1)
            items = ((q0, do0, low_t, low_t, prod0, lse_swapped), (q0, do0, high_t, high_t, prod0, lse_swapped), (q2, other_half(do2), low_t, high_t, prod2, lse2))
            dqs = []
            for h, (q, do, mine, where_o, prod, lse) in enumerate(items):
                a, b, c = three_parts(-jnp.sum(jnp.where(where_o, prod, 0.0), -1, keepdims=True))
                feat = jnp.where(within_t == 0, a, jnp.where(within_t == 1, b, jnp.where(within_t == 2, c, 0.0)))
                doh = jnp.where(mine, do, feat.astype(BF))
                a, b, c = three_parts(-lse)
                feat = jnp.where(within_t == 3, a, jnp.where(within_t == 4, b, jnp.where(within_t == 5, c, qf)))
                qh = jnp.where(mine, q, feat.astype(BF))
                p = jnp.exp(mm_t(keys[h], qh))
                ds = (p * mm_t(vals[h], doh)).astype(BF)
                dv = mm(p.astype(BF), do)
                dk = mm(ds, q)
                dqs.append(t_mm(ds, raw_keys[h]) * scale)
                if t == 0:
                    dv_acc[h, near, :] = dv
                    dk_acc[h, near, :] = dk
                else:
                    dv_acc[h, near, :] += dv
                    dk_acc[h, near, :] += dk
            dq = jnp.where(low_t, dqs[0], dqs[1])
            out_ref[0, at, :PAIR] = turn_back(dq, cos_ref[at, :], sin_ref[at, :]).astype(BF)
            dq2_acc[at, :] = dqs[2]

    def finish(i, at, c):
        low_r = is_low(ROWS)
        cosine, sine = cos_ref[at, :], sin_ref[at, :]
        out_ref[0, at, 2 * PAIR : 3 * PAIR] = turn_back(jnp.where(low_r, dk_acc[0, at, :], dk_acc[1, at, :]), cosine, sine).astype(BF)
        out_ref[0, at, 3 * PAIR : 4 * PAIR] = jnp.where(low_r, dv_acc[0, at, :], dv_acc[1, at, :]).astype(BF)
        last = jnp.where(low_r, dq2_acc[at, :], pltpu.roll(dk_acc[2, at, :], HEAD_DIM, 1))
        out_ref[0, at, PAIR : 2 * PAIR] = turn_back(last, cosine, sine).astype(BF)
        out_ref[0, at, 4 * PAIR :] = jnp.where(low_r, dv_acc[2, at, :], 0.0).astype(BF)

    each(rows, ROWS, finish)


def out_kernel(att_ref, w_ref, res_ref, bias_ref, gain_ref, shift_ref, mid_ref, n_ref):
    blocks, batches, two, deep, cols = w_ref.shape
    total = None
    for b in range(batches):
        for t in range(two):
            part = mm_t(att_ref[2 * b + t], w_ref[:, b, t].reshape(blocks * deep, cols))
            total = part if total is None else total + part
    mid = res_ref[...].astype(F32) + total + bias_ref[...]
    mid_ref[...] = mid
    n_ref[...] = normed(mid, gain_ref[...], shift_ref[...])


def clear(*refs):
    @pl.when(pl.program_id(0) == 0)
    def _():
        def zero(i, at, c):
            for ref in refs:
                ref[at, :] = jnp.zeros((ROWS, ref.shape[1]), F32)

        each(refs[0].shape[0], ROWS, zero)


def ffn_kernel(mid_ref, n_ref, dz_ref, up_ref, down_ref, upb_ref, downb_ref, gain_ref,
               out_ref, dmid_ref, dlow_ref, dw_ref, dupb_ref, dgain_ref, dshift_ref, ddownb_ref, dcob_ref,
               acc_out, acc_dn, hid, dhid):
    j = pl.program_id(0)
    rows = mid_ref.shape[0]
    width = mid_ref.shape[1]
    up = matrix(up_ref)
    down = matrix(down_ref)
    bias = upb_ref[0]
    clear(acc_out, acc_dn)

    def one(i, at, total):
        h = mm(n_ref[at, :], up) + bias
        phi = 0.5 * (1.0 + lax.erf(h * (0.5 ** 0.5)))
        slope = phi + h * jnp.exp(-0.5 * h * h) * (0.5 / math.pi) ** 0.5
        low = (h * phi).astype(BF)
        hid[at, :] = low
        acc_out[at, :] += mm_t(low, down)
        d = (mm(dz_ref[at, :], down) * slope).astype(BF)
        dhid[at, :] = d
        acc_dn[at, :] += mm_t(d, up)
        return total + col_sum(d.astype(F32))

    dupb_ref[0] = each(rows, FFN_ROWS, one, jnp.zeros((1, up.shape[1]), F32))

    def weight(i, at, c):
        put_rows(dw_ref, i, t_mm(n_ref[:, at], dhid[...]), slice(0, dhid.shape[1]))
        put_rows(dw_ref, i, t_mm(dz_ref[:, at], hid[...]), slice(dhid.shape[1], None))

    each(width, PART, weight)

    @pl.when(j == pl.num_programs(0) - 1)
    def _():
        def last(i, at, sums):
            mid = mid_ref[at, :]
            out_ref[at, :] = (mid + acc_out[at, :] + downb_ref[...]).astype(BF)
            back, dg, ds = norm_back(acc_dn[at, :], mid, gain_ref[...])
            dz = dz_ref[at, :].astype(F32)
            total = dz + back
            dmid_ref[at, :] = total
            low = total.astype(BF)
            dlow_ref[at, :] = low
            return tuple(s + a for s, a in zip(sums, (dg, ds, col_sum(dz), col_sum(low.astype(F32)))))

        sums = each(rows, ROWS, last, (jnp.zeros((1, width), F32),) * 4)
        dgain_ref[...], dshift_ref[...], ddownb_ref[...], dcob_ref[...] = sums


def out_back_kernel(d_ref, w_ref, datt_ref):
    datt_ref[0] = mm(d_ref[...], matrix(w_ref)).astype(BF)


def cross_back_kernel(dh_ref, w_ref, n_ref, side_ref, dlow_ref, att_ref, mid_ref, y_ref, dmid_ref, gain_ref, gainy_ref,
                      dw_ref, dbias_ref, dout_ref, dbranch_ref, other_ref, dg_ref, ds_ref, dgy_ref, dsy_ref, dob_ref,
                      acc_n, acc_side):
    j = pl.program_id(0)
    rows, width = mid_ref.shape
    wq = matrix(w_ref, 0, 2 * PAIR)
    wkv = matrix(w_ref, PAIR, 5 * PAIR)
    low = is_low(TALL)
    nought = jnp.zeros((TALL, PAIR), BF)
    clear(acc_n, acc_side)

    def one(i, at, total):
        d = dh_ref[0, at, :]
        t0, t1, t2, t3, t4 = split_tiles(d)
        acc_n[at, :] += mm_t(jnp.concatenate([t0, jnp.where(low, t1, nought)], 1), wq)
        acc_side[at, :] += mm_t(jnp.concatenate([jnp.where(low, nought, t1), t2, t3, t4], 1), wkv)
        return total + col_sum(d.astype(F32))

    dbias_ref[0] = each(rows, TALL, one, jnp.zeros((1, 5 * PAIR), F32))
    low_p = is_low(PART)

    def weight(i, at, c):
        dq = t_mm(n_ref[:, at], dh_ref[0, :, : 2 * PAIR])
        dkv = t_mm(side_ref[:, at], dh_ref[0, :, PAIR:])
        do = t_mm(dlow_ref[:, at], att_ref[0])
        put_rows(dw_ref, i, dq[:, :PAIR], slice(0, PAIR))
        put_rows(dw_ref, i, jnp.where(low_p, dq[:, PAIR:], dkv[:, :PAIR]), slice(PAIR, 2 * PAIR))
        put_rows(dw_ref, i, dkv[:, PAIR : 3 * PAIR], slice(2 * PAIR, 4 * PAIR))
        put_rows(dw_ref, i, dkv[:, 3 * PAIR :] + do[:, :PAIR], slice(4 * PAIR, 5 * PAIR))
        put_rows(dw_ref, i, do[:, PAIR:], slice(5 * PAIR, 6 * PAIR))

    each(width, PART, weight)

    @pl.when(j == pl.num_programs(0) - 1)
    def _():
        def last(i, at, sums):
            back, dg, ds = norm_back(acc_n[at, :], mid_ref[at, :], gain_ref[...])
            total = dmid_ref[at, :] + back
            dout_ref[at, :] = total
            branch = total.astype(BF)
            dbranch_ref[at, :] = branch
            other, dgy, dsy = norm_back(acc_side[at, :], y_ref[at, :].astype(F32), gainy_ref[...])
            other_ref[at, :] = other.astype(BF)
            return tuple(s + a for s, a in zip(sums, (dg, ds, dgy, dsy, col_sum(branch.astype(F32)))))

        sums = each(rows, ROWS, last, (jnp.zeros((1, width), F32),) * 5)
        dg_ref[...], ds_ref[...], dgy_ref[...], dsy_ref[...], dob_ref[...] = sums


def self_back_part(dh_ref, w_ref, n_ref, dlow_ref, att_ref, dw_ref, dbias_ref, acc_ref):
    rows, width = n_ref.shape
    w = matrix(w_ref, 0, 5 * PAIR)
    clear(acc_ref)

    def one(i, at, total):
        d = dh_ref[0, at, :]
        acc_ref[at, :] += mm_t(d, w)
        return total + col_sum(d.astype(F32))

    dbias_ref[0] = each(rows, TALL, one, jnp.zeros((1, 5 * PAIR), F32))

    def weight(i, at, c):
        dqkv = t_mm(n_ref[:, at], dh_ref[0])
        do = t_mm(dlow_ref[:, at], att_ref[0])
        put_rows(dw_ref, i, dqkv[:, : 4 * PAIR], slice(0, 4 * PAIR))
        put_rows(dw_ref, i, dqkv[:, 4 * PAIR :] + do[:, :PAIR], slice(4 * PAIR, 5 * PAIR))
        put_rows(dw_ref, i, do[:, PAIR:], slice(5 * PAIR, 6 * PAIR))

    each(width, PART, weight)


def self_back_first_kernel(dh_ref, w_ref, n_ref, dlow_ref, att_ref, dw_ref, dbias_ref, acc_ref):
    self_back_part(dh_ref, w_ref, n_ref, dlow_ref, att_ref, dw_ref, dbias_ref, acc_ref)


def self_back_last_kernel(dh_ref, w_ref, n_ref, dlow_ref, att_ref, x_ref, dmid_ref, before_ref, gain_ref,
                          dw_ref, dbias_ref, own_ref, dg_ref, ds_ref, acc_ref):
    j = pl.program_id(0)
    rows, width = x_ref.shape
    self_back_part(dh_ref, w_ref, n_ref, dlow_ref, att_ref, dw_ref, dbias_ref, acc_ref)

    @pl.when(j == pl.num_programs(0) - 1)
    def _():
        def last(i, at, sums):
            back, dg, ds = norm_back(acc_ref[at, :] + before_ref[at, :], x_ref[at, :].astype(F32), gain_ref[...])
            own_ref[at, :] = (dmid_ref[at, :] + back).astype(BF)
            return sums[0] + dg, sums[1] + ds

        dg_ref[...], ds_ref[...] = each(rows, ROWS, last, (jnp.zeros((1, width), F32),) * 2)


def tables(image_sizes, count):
    images = image_sizes.shape[0]
    ends = jnp.cumsum(image_sizes)
    first = jnp.sum(jnp.where(image_sizes == LONGEST, ends - image_sizes, 0))
    places = (jnp.arange(count, dtype=jnp.int32) + first) % count
    passed = places[:, None] >= ends[None, :]
    segment = jnp.sum(passed.astype(jnp.int32), -1)
    start = jnp.sum(jnp.where(passed, image_sizes[None, :], 0), -1)
    place = (places - start).astype(F32)
    half = HEAD_DIM // 2
    lane = jnp.arange(PAIR, dtype=jnp.int32)
    freqs = 100.0 ** (-((lane % half).astype(F32) / half))
    angles = place[:, None] * freqs[None, :]
    sign = jnp.where(lane % HEAD_DIM < half, -1.0, 1.0)
    member = (lane % HEAD_DIM)[None, :] == segment[:, None]
    slot = ((lane % HEAD_DIM) < images)[None, :]
    kf = member.astype(BF)
    qf = jnp.where(slot & ~member, -FAR, 0.0).astype(BF)
    return first, qf, kf, jnp.cos(angles), jnp.sin(angles) * sign[None, :]


def whole(a):
    return pl.BlockSpec(a.shape, lambda j: (0,) * a.ndim)


def per_step(a, side=None):
    return pl.BlockSpec((1,) + a.shape[1:], lambda j: (j if side is None else 2 * j + side,) + (0,) * (a.ndim - 1))


def weight_block(g, cols, at, side=None):
    return pl.BlockSpec((g.shape[0], 1, 1, g.shape[3], cols), lambda j: (0, j // 2, j % 2, 0, at) if side is None else (0, j, side, 0, at))


def sds(shape, dtype):
    return jax.ShapeDtypeStruct(shape, dtype)


def call(kernel, name, steps, ins, outs, scratch=(), flops=0, moved=0, exps=0):
    return pl.pallas_call(
        kernel,
        grid=(steps,),
        in_specs=[s for _, s in ins],
        out_specs=[s for _, s in outs],
        out_shape=[o for o, _ in outs],
        scratch_shapes=list(scratch),
        cost_estimate=pl.CostEstimate(flops=int(flops) // CHEAP, bytes_accessed=int(moved) // CHEAP, transcendentals=int(exps) // CHEAP),
        name=name,
    )(*[a for a, _ in ins])


def body(tokens, cotangent, lengths, norm1_gain, norm1_shift, qkv_w, qkv_b, out_w, out_b, norm2_gain, norm2_shift,
         normy_gain, normy_shift, cq_w, cq_b, ckv_w, ckv_b, cout_w, cout_b, norm3_gain, norm3_shift, up_w, up_b, down_w, down_b):
    batches = tokens.shape[0]
    members = lax.axis_size("mp")
    n_dp = lax.axis_size("dp")
    assert members == 2 * batches
    me = lax.axis_index("mp")
    view = me // batches
    batch = me % batches
    local = tokens.shape[2]
    rows = local * members
    width = tokens.shape[3]
    r = qkv_w.shape[1]
    hw = cq_w.shape[2]
    fw = up_w.shape[2]
    partner = [(i, (i + batches) % members) for i in range(members)]
    groups = [[d * members + v * batches + b for d in range(n_dp) for b in range(batches)] for v in range(2)]
    both = ("dp", "mp")
    split = r % 16 == 0
    blocks, deep = (n_dp, r) if split else (1, n_dp * r)

    def of_view(a, which):
        return lax.dynamic_index_in_dim(a, which, 0, keepdims=False)

    def cols(q, k, v, o):
        return jnp.concatenate([q, k[..., PAIR:], k[..., :PAIR], v, o[..., PAIR:], o[..., :PAIR]], -1)

    def uncols(a):
        t = [a[..., i * PAIR : (i + 1) * PAIR] for i in range(a.shape[-1] // PAIR)]
        h = HEAD_DIM
        join = lambda x, y: jnp.concatenate([x, y], -1)
        heads = (join(t[0], t[1][..., :h]), join(t[2], t[1][..., h:]), join(t[3], t[4][..., :h]))
        return heads + ((join(t[5], t[4][..., h:]),) if len(t) > 5 else ())

    def gather(pack):
        pair = jnp.stack([of_view(pack, view), lax.ppermute(of_view(pack, 1 - view), "mp", partner)], 0)
        got = lax.all_gather(pair, both, axis=0, axis_index_groups=groups).reshape(n_dp, batches, 2, r, -1)
        return got if split else got.transpose(1, 2, 0, 3, 4).reshape(1, batches, 2, deep, -1)

    flip = lambda a: a.swapaxes(-1, -2)
    pack_self = cols(qkv_w[:, :, 0], qkv_w[:, :, 1], qkv_w[:, :, 2], flip(out_w))
    pack_cross = cols(cq_w, ckv_w[:, :, 0], ckv_w[:, :, 1], flip(cout_w))
    w_att = gather(jnp.concatenate([pack_self, pack_cross], -1))
    w_ffn = gather(jnp.concatenate([up_w, flip(down_w)], -1))

    none = jnp.zeros_like(cq_b)
    bias_pack = jnp.concatenate([cols(qkv_b[:, 0], qkv_b[:, 1], qkv_b[:, 2], none), cols(cq_b, ckv_b[:, 0], ckv_b[:, 1], none), up_b], -1)
    bias_rows = bias_pack.shape[-1] // width
    bias_pack = jnp.broadcast_to(bias_pack.reshape(2, 1, bias_rows, width), (2, batches, bias_rows, width))
    by_view = tokens.swapaxes(0, 1)
    sent_x = jnp.concatenate([by_view, bias_pack], 2).reshape(members, local + bias_rows, width)
    got_x = lax.all_to_all(sent_x, "mp", 0, 0, tiled=True)
    got_y = lax.all_to_all(by_view[::-1].reshape(members, local, width), "mp", 0, 0, tiled=True)
    got_z = lax.all_to_all(cotangent.swapaxes(0, 1).reshape(members, local, width), "mp", 0, 0, tiled=True)
    first, qf, kf, cosine, sine = tables(of_view(lengths[:, 0], batch), rows)

    def from_row(a, at):
        return lax.dynamic_slice_in_dim(jnp.concatenate([a, a], 0), at, rows, 0)

    x = from_row(got_x[:, :local].reshape(rows, width), first)
    y = from_row(got_y.reshape(rows, width), first)
    dz = from_row(got_z.reshape(rows, width), first)

    def by_step(a):
        a = a.reshape((2, batches) + a.shape[1:])
        return jnp.where(view == 0, a, a[::-1]).swapaxes(0, 1).reshape((members,) + a.shape[2:])

    def by_member(a):
        a = a.reshape((batches, 2) + a.shape[1:]).swapaxes(0, 1)
        return jnp.where(view == 0, a, a[::-1]).reshape((members,) + a.shape[2:])

    biases = by_step(got_x[:, local:]).astype(F32)
    self_bias, cross_bias, up_bias = biases[:, 0:1], biases[:, 1:2], biases[:, 2:]
    up_bias = up_bias.reshape(members, 1, fw)

    def mine(a):
        return of_view(a, view).astype(F32)[None]

    g1, s1, ob, g2, s2, gy, sy, cob, g3, s3, db = [
        mine(a) for a in (norm1_gain, norm1_shift, out_b, norm2_gain, norm2_shift, normy_gain, normy_shift, cout_b, norm3_gain, norm3_shift, down_b)]
    def given(*arrays):
        return [(a, whole(a)) for a in arrays]

    def steps(*arrays):
        return [(a, per_step(a)) for a in arrays]

    def full(*shape_types):
        return [(s, whole(s)) for s in shape_types]

    low = sds((rows, width), BF)
    high = sds((rows, width), F32)
    line = sds((1, width), F32)
    heads = sds((members, rows, 5 * PAIR), BF)
    att_low = sds((members, rows, 2 * PAIR), BF)
    att_high = sds((members, rows, 2 * PAIR), F32)
    bias_out = sds((members, 1, 5 * PAIR), F32)
    gemm = 2 * rows * width * width * members

    def attend(h):
        return call(functools.partial(attend_kernel, tile=384), "attend", members, steps(h) + given(qf, kf), [(s, per_step(s)) for s in (att_low, att_high)],
                    flops=12 * members * rows * rows * PAIR, moved=members * rows * PAIR * 22, exps=3 * members * rows * rows)

    def attend_back(h, o, do, lse, side=None):
        count = members if side is None else batches
        out = sds((count, rows, 5 * PAIR), BF)
        acc = pltpu.VMEM((3, rows, PAIR), F32)
        ins = [(a, per_step(a, side)) for a in (h, o, do, lse)]
        return call(functools.partial(attend_back_kernel, tile=256), "attend_back", count, ins + given(qf, kf, cosine, sine), [(out, per_step(out))],
                    [pltpu.VMEM((rows, PAIR), F32), acc, acc], flops=30 * count * rows * rows * PAIR, moved=count * rows * PAIR * 40,
                    exps=3 * count * rows * rows)[0]

    def project(att, at, res, bias, gain, shift):
        tall = 512
        part = lambda cols: pl.BlockSpec((tall, cols), lambda i: (i, 0))
        att_spec = pl.BlockSpec((members, tall, 2 * PAIR), lambda i: (0, i, 0))
        w_spec = pl.BlockSpec((blocks, batches, 2, deep, 2 * PAIR), lambda i: (0, 0, 0, 0, at))
        return call(out_kernel, "project", rows // tall, [(att, att_spec), (w_att, w_spec), (res, part(width))] + given(bias, gain, shift),
                    [(high, part(width)), (low, part(width))], flops=gemm / 3, moved=rows * width * 14)

    def project_back(d, at):
        return call(out_back_kernel, "project_back", members, given(d) + [(w_att, weight_block(w_att, 2 * PAIR, at))], [(att_low, per_step(att_low))],
                    flops=gemm / 3, moved=rows * width * 8)[0]

    def norm(a, gain, shift):
        spec = pl.BlockSpec((ROWS, width), lambda i: (i, 0))
        return call(norm_kernel, "norm", rows // ROWS, [(a, spec)] + given(gain, shift), [(low, spec)], moved=rows * width * 4)[0]

    def by_owner(piece):
        if not split:
            piece = piece.reshape(batches, piece.shape[2], n_dp, r, -1).transpose(2, 0, 1, 3, 4)
        return piece

    def scatter(piece):
        return lax.psum_scatter(by_owner(piece).reshape(n_dp * batches, 2, r, -1), both, scatter_dimension=0, axis_index_groups=groups)

    core_pairs = [(i, i ^ 1) for i in range(members)]
    x_pairs = [(i, i ^ 1) for i in range(n_dp)]
    place = lax.axis_index("dp")
    lines = n_dp // 2

    def pick(a, i, axis):
        return lax.dynamic_index_in_dim(a, i, axis, keepdims=False)

    by_hand = batches == 2 and n_dp <= 8

    def over_cores(piece):
        got = lax.ppermute(pick(piece, 1 - batch, 1), "mp", core_pairs)
        return (pick(piece, batch, 1).astype(F32) + got.astype(F32)).astype(BF)

    def over_x(piece):
        piece = piece.reshape((piece.shape[0] // 2, 2) + piece.shape[1:])
        got = lax.ppermute(pick(piece, 1 - place % 2, 1), "dp", x_pairs)
        return (pick(piece, place % 2, 1).astype(F32) + got.astype(F32)).astype(BF)

    def over_z(piece):
        total = pick(piece, place // 2, 0).astype(F32)
        for s in range(1, lines):
            perm = [(i, (i + 2 * s) % n_dp) for i in range(n_dp)]
            total = total + lax.ppermute(pick(piece, (place // 2 + s) % lines, 0), "dp", perm).astype(F32)
        return total.astype(BF)

    def settle(total):
        theirs = lax.ppermute(total[1], "mp", partner).astype(F32)
        keep = total[0].astype(F32)
        return jnp.stack([jnp.where(view == 0, keep, theirs), jnp.where(view == 0, theirs, keep)], 0)

    n1 = norm(x, g1, s1)
    side = norm(y, gy, sy)
    hs = call(self_in_kernel, "self_in", members, given(n1) + [(w_att, weight_block(w_att, 6 * PAIR, 0))] + steps(self_bias) + given(cosine, sine),
              [(heads, per_step(heads))], flops=gemm, moved=rows * width * 16)[0]
    att, lse = attend(hs)
    middle, n2 = project(att, 2, x, ob, g2, s2)
    hc = call(cross_in_kernel, "cross_in", members, given(n2, side) + [(w_att, weight_block(w_att, 6 * PAIR, 1))] + steps(cross_bias) + given(cosine, sine),
              [(heads, per_step(heads))], flops=gemm, moved=rows * width * 16)[0]
    catt, clse = attend(hc)
    middle2, n3 = project(catt, 5, middle, cob, g3, s3)

    dw_ffn = sds((blocks, batches, 2, deep, 2 * fw), BF)
    dw_ffn_spec = pl.BlockSpec((blocks, 1, 1, deep, 2 * fw), lambda j: (0, j // 2, j % 2, 0, 0))
    up_line = sds((members, 1, fw), F32)
    output, d_mid2, d_cross, dw_f, d_upb, gg3, gs3, d_db, d_cob = call(
        ffn_kernel, "ffn", members,
        given(middle2, n3, dz) + [(w_ffn, weight_block(w_ffn, fw, 0)), (w_ffn, weight_block(w_ffn, fw, 1))] + steps(up_bias) + given(db, g3),
        full(low, high, low) + [(dw_ffn, dw_ffn_spec), (up_line, per_step(up_line))] + full(line, line, line, line),
        [pltpu.VMEM((rows, width), F32)] * 2 + [pltpu.VMEM((rows, fw), BF)] * 2,
        flops=6 * gemm, moved=rows * width * 60, exps=rows * fw * members * 2)

    total_ffn = scatter(dw_f)
    d_catt = project_back(d_cross, 5)
    d_hc = attend_back(hc, catt, d_catt, clse)
    dw_att = sds((blocks, batches, 2, deep, 6 * PAIR), BF)
    dw_spec = pl.BlockSpec((blocks, 1, 1, deep, 6 * PAIR), lambda j: (0, j // 2, j % 2, 0, 0))
    dw_cross, d_crossb, d_mid, d_branch, other, gg2, gs2, ggy, gsy, d_ob = call(
        cross_back_kernel, "cross_back", members,
        steps(d_hc) + [(w_att, weight_block(w_att, 6 * PAIR, 1))] + given(n2, side, d_cross) + steps(catt) + given(middle, y, d_mid2, g2, gy),
        [(dw_att, dw_spec), (bias_out, per_step(bias_out))] + full(high, low, low, line, line, line, line, line),
        [pltpu.VMEM((rows, width), F32)] * 2, flops=3 * gemm, moved=rows * width * 40)
    d_att = project_back(d_branch, 2)
    if by_hand:
        cross = over_cores(by_owner(dw_cross))
        d_att, cross = lax.optimization_barrier((d_att, cross))
        cross_a = over_x(cross[: n_dp // 2])

    dw_part = sds((blocks, batches, 1, deep, 6 * PAIR), BF)
    dw_part_spec = pl.BlockSpec((blocks, 1, 1, deep, 6 * PAIR), lambda j: (0, j, 0, 0, 0))
    bias_part = sds((batches, 1, 5 * PAIR), F32)

    def self_back(t, dh, *more):
        ins = steps(dh) + [(w_att, weight_block(w_att, 6 * PAIR, 0, t))] + given(n1, d_branch) + [(att, per_step(att, t))]
        outs = [(dw_part, dw_part_spec), (bias_part, per_step(bias_part))]
        if more:
            return call(self_back_last_kernel, "self_back_last", batches, ins + given(*more), outs + full(low, line, line),
                        [pltpu.VMEM((rows, width), F32)], flops=1.5 * gemm, moved=rows * width * 30)
        return call(self_back_first_kernel, "self_back_first", batches, ins, outs + full(high), flops=1.5 * gemm, moved=rows * width * 24)

    d_h1 = attend_back(hs, att, d_att, lse, 1)
    if by_hand:
        d_h1, cross, cross_a = lax.optimization_barrier((d_h1, cross, cross_a))
        cross_b = over_x(cross[n_dp // 2 :])
    dw_self1, d_selfb1, acc = self_back(1, d_h1)
    if by_hand:
        d_att, acc, cross_a, cross_b, dw_self1 = lax.optimization_barrier((d_att, acc, cross_a, cross_b, dw_self1))
        cross = over_z(jnp.concatenate([cross_a, cross_b], 0))
        self1 = over_cores(by_owner(dw_self1))
    d_h0 = attend_back(hs, att, d_att, lse, 0)
    if by_hand:
        d_h0, total_ffn, self1, cross = lax.optimization_barrier((d_h0, total_ffn, self1, cross))
        self1 = over_x(self1)
    else:
        d_h0, total_ffn = lax.optimization_barrier((d_h0, total_ffn))
    dw_self0, d_selfb0, own, gg1, gs1 = self_back(0, d_h0, x, d_mid, acc, g1)
    d_selfb = jnp.stack([d_selfb0, d_selfb1], 1).reshape(members, 1, 5 * PAIR)
    sum_ffn = settle(total_ffn)
    if by_hand:
        own, dw_self0, self1 = lax.optimization_barrier((own, dw_self0, self1))
        self0 = over_z(over_x(over_cores(by_owner(dw_self0))))
        self1 = over_z(self1)
        sum_cross = settle(cross)
        sum_self = settle(jnp.concatenate([self0, self1], 0))
    else:
        sum_cross = settle(scatter(dw_cross))
        sum_self = settle(scatter(jnp.concatenate([dw_self0, dw_self1], 2)))

    def over_all(flat):
        for perm in [[(i, i // batches * batches + (i + s) % batches) for i in range(members)] for s in range(1, batches)]:
            flat = flat + lax.ppermute(flat, "mp", perm)
        step = 1
        while step < n_dp:
            flat = flat + lax.ppermute(flat, "dp", [(i, i ^ step) for i in range(n_dp)])
            step *= 2
        theirs = lax.ppermute(flat, "mp", partner)
        return jnp.stack([jnp.where(view == 0, flat, theirs), jnp.where(view == 0, theirs, flat)], 0)

    sums = over_all(jnp.concatenate([gg1, gs1, d_ob, gg2, gs2, ggy, gsy, d_cob, gg3, gs3, d_db] + [by_member(a[:, 0]).reshape(1, -1) for a in (d_selfb, d_crossb, d_upb)], -1)[0])
    g1g, s1g, obg, g2g, s2g, gyg, syg, cobg, g3g, s3g, dbg = [sums[:, i * width : (i + 1) * width] for i in range(11)]
    at_self = 11 * width
    at_cross = at_self + members * 5 * PAIR
    at_up = at_cross + members * 5 * PAIR

    def member_part(flat, size):
        return lax.dynamic_index_in_dim(flat.reshape(2, members, size), me, 1, keepdims=False)

    cross_part = uncols(member_part(sums[:, at_cross:at_up], 5 * PAIR))
    upb_grad = member_part(sums[:, at_up:], fw)
    self_part = uncols(member_part(sums[:, at_self:at_cross], 5 * PAIR))

    output, other, own = [from_row(a, rows - first) for a in (output, other, own)]
    back = lax.all_to_all(output.reshape(members, local, width), "mp", 0, 0, tiled=True)
    block_output = back.reshape(2, batches, local, width).swapaxes(0, 1)
    got_other = lax.all_to_all(other.reshape(members, local, width), "mp", 0, 0, tiled=True).reshape(2, batches, local, width)
    got_own = lax.all_to_all(own.reshape(members, local, width), "mp", 0, 0, tiled=True).reshape(2, batches, local, width)
    input_grad = (got_own.astype(F32) + got_other[::-1].astype(F32)).swapaxes(0, 1)

    q, k, v, o = uncols(sum_self)
    cq, ck, cv, co = uncols(sum_cross)
    return (block_output, input_grad, g1g, s1g, jnp.stack([q, k, v], 2), jnp.stack(self_part, 1), flip(o), obg, g2g, s2g, gyg, syg,
            cq, cross_part[0], jnp.stack([ck, cv], 2), jnp.stack(cross_part[1:], 1), flip(co), cobg, g3g, s3g,
            sum_ffn[..., :fw], upb_grad, flip(sum_ffn[..., fw:]), dbg)


def solution(mesh):
    rows = P(None, None, ("dp", "mp"), None)
    wide = P(None, "dp", None, "mp")
    by_rows = P(None, "dp", "mp")
    by_cols = P(None, "mp", "dp")
    parts = P(None, None, "mp")
    flat = P(None, "mp")
    same = P()
    in_specs = (rows, rows, P(None, "dp", None), same, same, wide, parts, by_cols, same, same, same, same, same, by_rows, flat, wide, parts,
                by_cols, same, same, same, by_rows, flat, by_cols, same)
    out_specs = (rows, rows, same, same, wide, parts, by_cols, same, same, same, same, same, by_rows, flat, wide, parts, by_cols, same,
                 same, same, by_rows, flat, by_cols, same)
    return jax.shard_map(body, mesh=mesh, in_specs=in_specs, out_specs=out_specs, check_vma=False)
```

time: 996 us -> 505 us (0.51)
  waiting for transfers between devices: 358 us -> 79.7 us
  local copies, waits for them, and re-layouts: 280 us -> 34.4 us
  matrix products: 121 us -> 0 us
  Pallas kernels: 129 us -> 249 us
  starting transfers between devices: 27 us -> 55.9 us
    reduce_scatter x2 -> x1, waiting for transfers between devices: 202 us -> 0.02 us  [scatter(): lax.psum_scatter(by_owner(piece).reshape(n_dp * batches, 2, r, -1), both,...]
    dot_general x27 -> x0, matrix products: 121 us -> none  [the longest x10 42 us: t_mm(): lax.dot_general(a, b, (((0,), (0,)), ((), ())), preferred_element_type=F32)]
    pallas_call x4 -> x17, Pallas kernels: 129 us -> 249 us  [call(): pl.pallas_call(kernel, grid=(steps,), in_specs=[s for _, s in ins], out_s...]
    reshape x32 -> x3, local copies, waits for them, and re-layouts: 90.7 us -> 0.06 us  [the longest x2 0.05 us: member_part(): flat.reshape(2, members, size)]
    transpose x11 -> x0, local copies, waits for them, and re-layouts: 68.3 us -> none  [the longest x6 41.4 us: packed(): piece.transpose(0, 4, 3, 1, 2, 5).reshape(n_dp * batches, 2, r, parts * w)]
    all_gather x2, waiting for transfers between devices: 49.4 us -> 4.48 us  [gather(): lax.all_gather(pair, both, axis=0, axis_index_groups=groups)]
    unnamed x203 -> x123, local copies, waits for them, and re-layouts: 43.4 us -> 14.8 us
    convert_element_type x5 -> x0, local copies, waits for them, and re-layouts: 27.8 us -> none  [the longest x4 27.7 us: packed(): piece = g.astype(BF).reshape(n_dp, r, parts, 2, batches, w)]
  transfers between devices with their start and end apart: 14 -> 35, of which waited for: 11 -> 15; matrix products, arithmetic and copies ran while one was open for 20% -> 18% of each run, Pallas kernels for 0% -> 41%
where the time goes in v2:
time: 505 us; the launch traced here: 500 us
  Pallas kernels  249 us (49%)
  waiting for transfers between devices  79.7 us (16%)
  other arithmetic  62.2 us (12%)
  starting transfers between devices  55.9 us (11%)
  local copies, waits for them, and re-layouts  34.4 us (7%)
  between operations  18.6 us (4%)
    pallas_call x17, Pallas kernels, call(): pl.pallas_call(kernel, grid=(steps,), in_specs=[s for _, s in ins], out_s...  249 us
    concatenate x5, other arithmetic, from_row(): return lax.dynamic_slice_in_dim(jnp.concatenate([a, a], 0), at, rows, 0)  22.3 us
    all_to_all x1, waiting for transfers between devices, body(): got_x = lax.all_to_all(sent_x, 'mp', 0, 0, tiled=True)  15.6 us
    unnamed x123, local copies, waits for them, and re-layouts  14.8 us
    ppermute x9, waiting for transfers between devices, over_z(): lax.ppermute(pick(piece, (place // 2 + s) % lines, 0), 'dp', perm)  13.8 us
    ppermute x2, waiting for transfers between devices, gather(): lax.ppermute(of_view(pack, 1 - view), 'mp', partner)  13.5 us
    ppermute x9, starting transfers between devices, over_z(): lax.ppermute(pick(piece, (place // 2 + s) % lines, 0), 'dp', perm)  13.2 us
    all_to_all x1, waiting for transfers between devices, body(): lax.all_to_all(cotangent.swapaxes(0, 1).reshape(members, local, width), '...  12.9 us
  transfers between devices with their start and end apart: 35, of which 15 were waited for; matrix products, arithmetic and copies ran while one was open for 18% of the time, Pallas kernels for 41%

profile of v2, /device:TPU:0, one launch (start us, length us, event | category | flops | bytes accessed | tf_op | source)
XLA Modules:
  0.0 499.9 jit_solution(3048054390454353940)
XLA Ops:
  7.3 1.5 fusion.94
  9.6 3.0 collective-permute-start
  12.7 7.0 %collective-permute-done = bf16[96,1536]{1,0:T(8,128)(2,1)S(1)} collective-permute-done((bf16[96,1536]{1,0:T(8,128)(2,1)S(1)}, bf16[96,1536]{1,0:T(8,128)(2,1)S(1)}, u32[]{:S(2)}, u32[]{:S(2)}) %collective-permute-start) | collective-permute-done | bytes 294944 | tf_op jit(solution)/shard_map/ppermute | solution.py:497
  20.7 1.8 collective-permute-start.1
  22.5 6.5 %collective-permute-done.1 = bf16[96,1536]{1,0:T(8,128)(2,1)S(1)} collective-permute-done((bf16[96,1536]{1,0:T(8,128)(2,1)S(1)}, bf16[96,1536]{1,0:T(8,128)(2,1)S(1)}, u32[]{:S(2)}, u32[]{:S(2)}) %collective-permute-start.1) | collective-permute-done | bytes 294944 | tf_op jit(solution)/shard_map/ppermute | solution.py:497
  31.1 3.7 all-to-all-start.2
  37.3 1.5 copy.182
  42.0 12.9 %all-to-all-done.2 = bf16[4,256,768]{2,1,0:T(8,128)(2,1)S(1)} async-done(((bf16[4,256,768]{2,1,0:T(8,128)(2,1)}), bf16[4,256,768]{2,1,0:T(8,128)(2,1)S(1)}, u32[]{:S(2)}, u32[]{:S(2)}) %all-to-all-start.2) | async-done | bytes 1572896 | tf_op jit(solution)/shard_map/all_to_all | solution.py:515
  55.0 3.7 all-to-all-start
  63.7 15.6 %all-to-all-done = bf16[4,259,768]{2,1,0:T(8,128)(2,1)S(1)} async-done(((bf16[4,259,768]{2,1,0:T(8,128)(2,1)}), bf16[4,259,768]{2,1,0:T(8,128)(2,1)S(1)}, u32[]{:S(2)}, u32[]{:S(2)}) %all-to-all-start) | async-done | bytes 1591328 | tf_op jit(solution)/shard_map/all_to_all | solution.py:513
  79.3 4.4 all-to-all-start.1
  86.4 3.0 fusion.21
  89.5 3.8 fusion.7.dz_ref
  93.4 10.4 %all-to-all-done.1 = bf16[4,256,768]{2,1,0:T(8,128)(2,1)} async-done(((bf16[4,256,768]{2,1,0:T(8,128)(2,1)}), bf16[4,256,768]{2,1,0:T(8,128)(2,1)}, u32[]{:S(2)}, u32[]{:S(2)}) %all-to-all-start.1) | async-done | bytes 1572896 | tf_op jit(solution)/shard_map/all_to_all | solution.py:514
  103.8 6.8 %fusion.8 = (bf16[1024,768]{1,0:T(8,128)(2,1)}, bf16[1024,768]{1,0:T(8,128)(2,1)}) fusion(s32[]{:T(128)S(6)} %select_n.295, bf16[1024,768]{1,0:T(8,128)(2,1)} %bitcast.25, bf16[1024,768]{1,0:T(8,128)(2,1)S(1)} %bitcast.246), kind=kLoop, calls=%fused_computation.26 | loop fusion | flops 6291456 | bytes 6291460 | tf_op jit(solution)/shard_map/concatenate | solution.py:519
  110.6 4.2 norm.2.n_ref
  114.9 4.2 norm.3.side_ref
  119.7 9.4 %self_in.1.heads_ref = bf16[4,1024,640]{2,1,0:T(8,128)(2,1)} custom-call(bf16[1024,768]{1,0:T(8,128)(2,1)} %norm.2.n_ref, bf16[8,2,2,96,1536]{4,3,2,1,0:T(8,128)(2,1)} %bitcast.227, f32[4,1,768]{2,1,0:T(1,128)} %get-tuple-element.281.bias_ref, f32[1024,128]{1,0:T(8,128)} %get-tuple-element.287.cos_ref, f32[1024,128]{1,0:T(8,128)} %get-tuple-element.286.sin_ref), custom_call_target="tpu_custom_call" | custom-call | flops 301989888 | bytes 786432 | tf_op jit(solution)/shard_map/self_in/pallas_call | solution.py:450
  129.1 14.7 %attend.2 = (bf16[4,1024,256]{2,1,0:T(8,128)(2,1)}, f32[4,1024,256]{2,1,0:T(8,128)}) custom-call(bf16[4,1024,640]{2,1,0:T(8,128)(2,1)} %self_in.1.heads_ref, bf16[1024,128]{1,0:T(8,128)(2,1)} %select_convert_fusion.qf_ref, bf16[1024,128]{1,0:T(8,128)(2,1)} %compare_convert_fusion.kf_ref), custom_call_target="tpu_custom_call" | custom-call | flops 402653184 | bytes 720896 | tf_op jit(solution)/shard_map/attend/pallas_call | solution.py:450
  143.9 6.1 %project.2 = (f32[1024,768]{1,0:T(8,128)}, bf16[1024,768]{1,0:T(8,128)(2,1)}) custom-call(bf16[4,1024,256]{2,1,0:T(8,128)(2,1)} %get-tuple-element.76.att_ref.o_ref, bf16[8,2,2,96,1536]{4,3,2,1,0:T(8,128)(2,1)} %bitcast.228, bf16[1024,768]{1,0:T(8,128)(2,1)} %get-tuple-element.296.x_ref.res_ref, f32[1,768]{1,0:T(1,128)} %get-tuple-element.299.bias_ref, ...), custom_call_target="tpu_custom_call" | custom-call | flops 100663296 | bytes 688128 | tf_op jit(solution)/shard_map/project/pallas_call | solution.py:450
  149.9 10.8 %cross_in.1.heads_ref = bf16[4,1024,640]{2,1,0:T(8,128)(2,1)} custom-call(bf16[1024,768]{1,0:T(8,128)(2,1)} %get-tuple-element.77.n_ref, bf16[1024,768]{1,0:T(8,128)(2,1)} %norm.3.side_ref, bf16[8,2,2,96,1536]{4,3,2,1,0:T(8,128)(2,1)} %bitcast.229, f32[4,1,768]{2,1,0:T(1,128)} %get-tuple-element.280.bias_ref, f32[1024,128]{1,0:T(8,128)} %get-tuple-element.287.cos_ref, ...), custom_call_target="tpu_custom_call" | custom-call | flops 301989888 | bytes 786432 | tf_op jit(solution)/shard_map/cross_in/pallas_call | solution.py:450
  160.8 14.5 %attend.3 = (bf16[4,1024,256]{2,1,0:T(8,128)(2,1)}, f32[4,1024,256]{2,1,0:T(8,128)}) custom-call(bf16[4,1024,640]{2,1,0:T(8,128)(2,1)} %cross_in.1.heads_ref, bf16[1024,128]{1,0:T(8,128)(2,1)} %select_convert_fusion.qf_ref, bf16[1024,128]{1,0:T(8,128)(2,1)} %compare_convert_fusion.kf_ref), custom_call_target="tpu_custom_call" | custom-call | flops 402653184 | bytes 720896 | tf_op jit(solution)/shard_map/attend/pallas_call | solution.py:450
  175.2 6.4 %project.3 = (f32[1024,768]{1,0:T(8,128)}, bf16[1024,768]{1,0:T(8,128)(2,1)}) custom-call(bf16[4,1024,256]{2,1,0:T(8,128)(2,1)} %get-tuple-element.78.att_ref.o_ref, bf16[8,2,2,96,1536]{4,3,2,1,0:T(8,128)(2,1)} %bitcast.230, f32[1024,768]{1,0:T(8,128)} %get-tuple-element.79.res_ref.mid_ref, f32[1,768]{1,0:T(1,128)} %get-tuple-element.303.bias_ref, ...), custom_call_target="tpu_custom_call" | custom-call | flops 100663296 | bytes 688128 | tf_op jit(solution)/shard_map/project/pallas_call | solution.py:450
  181.6 4.5 all-gather.7.cloned.1.call-done
  186.1 43.6 %ffn.1 = (bf16[1024,768]{1,0:T(8,128)(2,1)}, f32[1024,768]{1,0:T(8,128)}, bf16[1024,768]{1,0:T(8,128)(2,1)}, bf16[8,2,2,96,1536]{4,3,2,1,0:T(8,128)(2,1)}, f32[4...) custom-call(f32[1024,768]{1,0:T(8,128)} %get-tuple-element.80.mid_ref, ...), custom_call_target="tpu_custom_call" | custom-call | flops 1811939328 | bytes 2949120 | tf_op jit(solution)/shard_map/ffn/pallas_call | solution.py:450
  229.7 5.6 %project_back.2.do_ref = bf16[4,1024,256]{2,1,0:T(8,128)(2,1)} custom-call(bf16[1024,768]{1,0:T(8,128)(2,1)} %get-tuple-element.83.d_ref.dlow_ref, bf16[8,2,2,96,1536]{4,3,2,1,0:T(8,128)(2,1)} %bitcast.231), custom_call_target="tpu_custom_call" | custom-call | flops 100663296 | bytes 393216 | tf_op jit(solution)/shard_map/project_back/pallas_call | solution.py:450
  235.4 33.3 %attend_back.3.dh_ref = bf16[4,1024,640]{2,1,0:T(8,128)(2,1)} custom-call(bf16[4,1024,640]{2,1,0:T(8,128)(2,1)} %cross_in.1.heads_ref, bf16[4,1024,256]{2,1,0:T(8,128)(2,1)} %get-tuple-element.78.att_ref.o_ref, bf16[4,1024,256]{2,1,0:T(8,128)(2,1)} %project_back.2.do_ref, f32[4,1024,256]{2,1,0:T(8,128)} %get-tuple-element.84.lse_ref, ...), custom_call_target="tpu_custom_call" | custom-call | flops 1006632960 | bytes 1310720 | tf_op jit(solution)/shard_map/attend_back/pallas_call | solution.py:450
  268.7 26.8 %cross_back.1 = (bf16[8,2,2,96,768]{4,3,2,1,0:T(8,128)(2,1)}, f32[4,1,640]{2,1,0:T(1,128)}, f32[1024,768]{1,0:T(8,128)}, bf16[1024,768]{1,0:T(8,128)(2,1)}, bf16...) custom-call(bf16[4,1024,640]{2,1,0:T(8,128)(2,1)} %attend_back.3.dh_, ...), custom_call_target="tpu_custom_call" | custom-call | flops 905969664 | bytes 1966080 | tf_op jit(solution)/shard_map/cross_back/pallas_call | solution.py:450
  295.5 1.9 dynamic-slice_bitcast_fusion
  297.8 5.7 %project_back.3.do_ref = bf16[4,1024,256]{2,1,0:T(8,128)(2,1)} custom-call(bf16[1024,768]{1,0:T(8,128)(2,1)} %get-tuple-element.86.d_ref.dlow_ref, bf16[8,2,2,96,1536]{4,3,2,1,0:T(8,128)(2,1)} %bitcast.233), custom_call_target="tpu_custom_call" | custom-call | flops 100663296 | bytes 393216 | tf_op jit(solution)/shard_map/project_back/pallas_call | solution.py:450
  303.6 3.1 fusion
  308.1 18.2 %attend_back.4.dh_ref = bf16[2,1024,640]{2,1,0:T(8,128)(2,1)} custom-call(bf16[4,1024,640]{2,1,0:T(8,128)(2,1)} %self_in.1.heads_ref, bf16[4,1024,256]{2,1,0:T(8,128)(2,1)} %get-tuple-element.76.att_ref.o_ref, bf16[4,1024,256]{2,1,0:T(8,128)(2,1)} %project_back.3.do_ref, f32[4,1024,256]{2,1,0:T(8,128)} %get-tuple-element.89.lse_ref, ...), custom_call_target="tpu_custom_call" | custom-call | flops 503316480 | bytes 655360 | tf_op jit(solution)/shard_map/attend_back/pallas_call | solution.py:450
  326.3 1.9 collective-permute-done.3
  328.2 2.0 fusion.13
  334.5 4.1 fusion.6
  338.6 3.6 all-to-all-start.3
  342.2 11.5 %self_back_first.1 = (bf16[8,2,1,96,768]{4,3,2,1,0:T(8,128)(2,1)}, f32[2,1,640]{2,1,0:T(1,128)}, f32[1024,768]{1,0:T(8,128)}) custom-call(bf16[2,1024,640]{2,1,0:T(8,128)(2,1)} %attend_back.4.dh_ref, bf16[8,2,2,96,1536]{4,3,2,1,0:T(8,128)(2,1)} %bitcast.234, bf16[1024,768]{1,0:T(8,128)(2,1)} %norm.2.n_ref, ...), custom_call_target="tpu_custom_call" | custom-call | flops 452984832 | bytes 1179648 | tf_op jit(solution)/shard_map/self_back_first/pallas_call | solution.py:450
  354.9 2.4 dynamic-slice_bitcast_fusion.2
  360.4 3.3 collective-permute-start.8
  363.8 3.8 fusion.4
  367.6 3.7 all-to-all-start.5
  372.6 18.1 %attend_back.5.dh_ref = bf16[2,1024,640]{2,1,0:T(8,128)(2,1)} custom-call(bf16[4,1024,640]{2,1,0:T(8,128)(2,1)} %self_in.1.heads_ref, bf16[4,1024,256]{2,1,0:T(8,128)(2,1)} %get-tuple-element.76.att_ref.o_ref, bf16[4,1024,256]{2,1,0:T(8,128)(2,1)} %project_back.3.do_ref, f32[4,1024,256]{2,1,0:T(8,128)} %get-tuple-element.89.lse_ref, ...), custom_call_target="tpu_custom_call" | custom-call | flops 503316480 | bytes 655360 | tf_op jit(solution)/shard_map/attend_back/pallas_call | solution.py:450
  392.1 1.9 fusion.3
  394.2 15.7 %self_back_last.1 = (bf16[8,2,1,96,768]{4,3,2,1,0:T(8,128)(2,1)}, f32[2,1,640]{2,1,0:T(1,128)}, bf16[1024,768]{1,0:T(8,128)(2,1)}, f32[1,768]{1,0:T(1,128)}, f32[1,768]{1,0:T(1,128)}) custom-call(bf16[2,1024,640]{2,1,0:T(8,128)(2,1)} %attend_back.5.dh_ref, bf16[8,2,2,96,1536]{4,3,2,1,0:T(8,128)(2,1)} %bitcast.235, bf16[1024,768]{1,0:T(8,128)(2,1)} %norm.2.n_ref, ...), custom_call_target="tpu_custom_call" | custom-call | flops 452984832 | bytes 1474560 | tf_op jit(solution)/shard_map/self_back_last/pallas_call | solution.py:450
  414.1 1.8 collective-permute-start.24
  415.8 1.7 slice_bitcast_fusion
  417.9 1.5 collective-permute-start.11
  423.7 2.9 collective-permute-done.12
  427.3 2.0 collective-permute-start.13
  431.1 2.4 collective-permute-done.13
  434.4 1.7 collective-permute-start.14
  439.0 2.1 fusion.11
  444.3 3.8 fusion.5
  448.1 2.6 fusion.2
  450.7 3.7 all-to-all-start.4
  455.6 2.0 collective-permute-start.16
  460.1 2.8 collective-permute-start.22
  464.8 2.6 collective-permute-done.20
  467.4 5.4 %collective-permute-done.21 = bf16[1,96,768]{2,1,0:T(8,128)(2,1)S(1)} collective-permute-done((bf16[1,96,768]{2,1,0:T(8,128)(2,1)S(1)}, bf16[1,96,768]{2,1,0:T(8,128)(2,1)S(1)}, u32[]{:S(2)}, u32[]{:S(2)}) %collective-permute-start.21) | collective-permute-done | bytes 147488 | tf_op jit(solution)/shard_map/ppermute | solution.py:620
  473.8 1.9 collective-permute-start.23
  476.7 2.8 collective-permute-start.17
  482.2 1.9 copy.153
  484.2 1.6 collective-permute-done.17
  485.7 4.1 collective-permute-done.18
  (292 shorter events, 59.1 us)
Async XLA Ops:
  7.2 112.5 %all-gather.5.cloned.1.call-start = ((), (), s32[]{:S(2)}) async-start(), calls=%async_computation.8 | async-start | bytes 10027008 | tf_op jit(solution)/shard_map/all_gather | solution.py:498
  9.5 11.1 %copy-start.13 = (bf16[2,96,768]{2,1,0:T(8,128)(2,1)S(1)}, bf16[2,96,768]{2,1,0:T(8,128)(2,1)}, u32[]{:S(2)}) copy-start(bf16[2,96,768]{2,1,0:T(8,128)(2,1)} %param.46) | copy-start | bytes 884740
  9.6 11.1 %copy-start.14 = (bf16[2,768,96]{1,2,0:T(8,128)(2,1)S(1)}, bf16[2,768,96]{1,2,0:T(8,128)(2,1)}, u32[]{:S(2)}) copy-start(bf16[2,768,96]{1,2,0:T(8,128)(2,1)} %param.48) | copy-start | bytes 884740
  9.6 10.0 %collective-permute-start = (bf16[96,1536]{1,0:T(8,128)(2,1)S(1)}, bf16[96,1536]{1,0:T(8,128)(2,1)S(1)}, u32[]{:S(2)}, u32[]{:S(2)}) collective-permute-start(bf16[96,1536]{1,0:T(8,128)(2,1)S(1)} %get-tuple-element.256), channel_id=1, source_target_pairs={{0,2},{1,3},{2,0},{3,1},{4,6},{5,7},{6,4},{7,5},{8,10},{9,11},{10,... | collective-permute-start | bytes 884744 | tf_op jit(solution)/shard_map/ppermute | solution.py:497
  20.6 9.3 %copy-start.8 = (bf16[2,2,256,768]{3,2,1,0:T(8,128)(2,1)S(1)}, bf16[2,2,256,768]{3,2,1,0:T(8,128)(2,1)}, u32[]{:S(2)}) copy-start(bf16[2,2,256,768]{3,2,1,0:T(8,128)(2,1)} %param.26) | copy-start | bytes 4718596
  20.6 165.5 %all-gather.7.cloned.1.call-start = ((), (), s32[]{:S(2)}) async-start(), calls=%async_computation.9 | async-start | bytes 10027008 | tf_op jit(solution)/shard_map/all_gather | solution.py:498
  20.7 8.3 %collective-permute-start.1 = (bf16[96,1536]{1,0:T(8,128)(2,1)S(1)}, bf16[96,1536]{1,0:T(8,128)(2,1)S(1)}, u32[]{:S(2)}, u32[]{:S(2)}) collective-permute-start(bf16[96,1536]{1,0:T(8,128)(2,1)S(1)} %get-tuple-element.254), channel_id=1, source_target_pairs={{0,2},{1,3},{2,0},{3,1},{4,6},{5,7},{6,4},{7,5},{8,10},{9,11},{10,... | collective-permute-start | bytes 884744 | tf_op jit(solution)/shard_map/ppermute | solution.py:497
  31.1 6.0 %copy-start.23 = (bf16[2,768]{1,0:T(2,128)(2,1)S(1)}, bf16[2,768]{1,0:T(2,128)(2,1)}, u32[]{:S(2)}) copy-start(bf16[2,768]{1,0:T(2,128)(2,1)} %param.47) | copy-start | bytes 9220
  31.1 6.0 %copy-start.45 = (bf16[2,192]{1,0:T(2,128)(2,1)S(1)}, bf16[2,192]{1,0:T(2,128)(2,1)}, u32[]{:S(2)}) copy-start(bf16[2,192]{1,0:T(2,128)(2,1)} %param.39) | copy-start | bytes 2308
  31.1 23.8 %all-to-all-start.2 = ((bf16[4,256,768]{2,1,0:T(8,128)(2,1)}), bf16[4,256,768]{2,1,0:T(8,128)(2,1)S(1)}, u32[]{:S(2)}, u32[]{:S(2)}) async-start(bf16[4,256,768]{2,1,0:T(8,128)(2,1)} %bitcast.28), calls=%async_computation.2 | async-start | bytes 3145728 | tf_op jit(solution)/shard_map/all_to_all | solution.py:515
  54.9 6.3 %copy-start.37 = (bf16[2,768]{1,0:T(2,128)(2,1)S(1)}, bf16[2,768]{1,0:T(2,128)(2,1)}, u32[]{:S(2)}) copy-start(bf16[2,768]{1,0:T(2,128)(2,1)} %param.28) | copy-start | bytes 9220
  54.9 6.3 %copy-start.38 = (bf16[2,768]{1,0:T(2,128)(2,1)S(1)}, bf16[2,768]{1,0:T(2,128)(2,1)}, u32[]{:S(2)}) copy-start(bf16[2,768]{1,0:T(2,128)(2,1)} %param.29) | copy-start | bytes 9220
  54.9 6.9 %copy-start.39 = (bf16[2,768]{1,0:T(2,128)(2,1)S(1)}, bf16[2,768]{1,0:T(2,128)(2,1)}, u32[]{:S(2)}) copy-start(bf16[2,768]{1,0:T(2,128)(2,1)} %param.33) | copy-start | bytes 9220
  54.9 6.9 %copy-start.40 = (bf16[2,768]{1,0:T(2,128)(2,1)S(1)}, bf16[2,768]{1,0:T(2,128)(2,1)}, u32[]{:S(2)}) copy-start(bf16[2,768]{1,0:T(2,128)(2,1)} %param.35) | copy-start | bytes 9220
  54.9 7.4 %copy-start.41 = (bf16[2,768]{1,0:T(2,128)(2,1)S(1)}, bf16[2,768]{1,0:T(2,128)(2,1)}, u32[]{:S(2)}) copy-start(bf16[2,768]{1,0:T(2,128)(2,1)} %param.36) | copy-start | bytes 9220
  55.0 7.4 %copy-start.42 = (bf16[2,768]{1,0:T(2,128)(2,1)S(1)}, bf16[2,768]{1,0:T(2,128)(2,1)}, u32[]{:S(2)}) copy-start(bf16[2,768]{1,0:T(2,128)(2,1)} %param.37) | copy-start | bytes 9220
  55.0 8.0 %copy-start.43 = (bf16[2,768]{1,0:T(2,128)(2,1)S(1)}, bf16[2,768]{1,0:T(2,128)(2,1)}, u32[]{:S(2)}) copy-start(bf16[2,768]{1,0:T(2,128)(2,1)} %param.43) | copy-start | bytes 9220
  55.0 8.0 %copy-start.44 = (bf16[2,768]{1,0:T(2,128)(2,1)S(1)}, bf16[2,768]{1,0:T(2,128)(2,1)}, u32[]{:S(2)}) copy-start(bf16[2,768]{1,0:T(2,128)(2,1)} %param.45) | copy-start | bytes 9220
  55.0 24.3 %all-to-all-start = ((bf16[4,259,768]{2,1,0:T(8,128)(2,1)}), bf16[4,259,768]{2,1,0:T(8,128)(2,1)S(1)}, u32[]{:S(2)}, u32[]{:S(2)}) async-start(bf16[4,259,768]{2,1,0:T(8,128)(2,1)} %bitcast.6), calls=%async_computation | async-start | bytes 3244032 | tf_op jit(solution)/shard_map/all_to_all | solution.py:513
  79.3 24.5 %all-to-all-start.1 = ((bf16[4,256,768]{2,1,0:T(8,128)(2,1)}), bf16[4,256,768]{2,1,0:T(8,128)(2,1)}, u32[]{:S(2)}, u32[]{:S(2)}) async-start(bf16[4,256,768]{2,1,0:T(8,128)(2,1)} %bitcast.24), calls=%async_computation.1 | async-start | bytes 3145728 | tf_op jit(solution)/shard_map/all_to_all | solution.py:514
  83.7 310.4 %reduce-scatter.2.cloned.1.call-start = ((), (), s32[]{:S(2)}) async-start(), calls=%async_computation.7 | async-start | bytes 10027008 | tf_op jit(solution)/shard_map/reduce_scatter | solution.py:595
  297.5 6.1 %collective-permute-start.2 = (bf16[8,2,96,768]{3,2,1,0:T(8,128)(2,1)S(1)}, bf16[8,2,96,768]{3,2,1,0:T(8,128)(2,1)}, u32[]{:S(2)}, u32[]{:S(2)}) collective-permute-start(bf16[8,2,96,768]{3,2,1,0:T(8,128)(2,1)S(1)} %dynamic-slice_bitcast_fusion), channel_id=1, source_target_pairs={{0,1},{1,0},{2,3},{3,2},{4,5},{5,4},{6,7},{7,6},{8,9},{9,8},{10,11... | collective-permute-start | bytes 7077896 | tf_op jit(solution)/shard_map/ppermute | solution.py:608
  307.6 20.6 %collective-permute-start.3 = (bf16[2,2,96,768]{3,2,1,0:T(8,128)(2,1)}, bf16[2,2,96,768]{3,2,1,0:T(8,128)(2,1)}, u32[]{:S(2)}, u32[]{:S(2)}) collective-permute-start(bf16[2,2,96,768]{3,2,1,0:T(8,128)(2,1)} %dynamic-slice_bitcast_fusion.6), channel_id=1, source_target_pairs={{0,4},{4,0},{8,12},{12,8},{16,20},{20,16},{24,28},{28,24},{1,5},{5... | collective-permute-start | bytes 1769480 | tf_op jit(solution)/shard_map/ppermute | solution.py:613
  332.2 21.5 %collective-permute-start.4 = (bf16[2,2,96,768]{3,2,1,0:T(8,128)(2,1)}, bf16[2,2,96,768]{3,2,1,0:T(8,128)(2,1)}, u32[]{:S(2)}, u32[]{:S(2)}) collective-permute-start(bf16[2,2,96,768]{3,2,1,0:T(8,128)(2,1)} %dynamic-slice_bitcast_fusion.5), channel_id=1, source_target_pairs={{0,4},{4,0},{8,12},{12,8},{16,20},{20,16},{24,28},{28,24},{1,5},{5... | collective-permute-start | bytes 1769480 | tf_op jit(solution)/shard_map/ppermute | solution.py:613
  338.6 29.0 %all-to-all-start.3 = ((bf16[4,256,768]{2,1,0:T(8,128)(2,1)}), bf16[4,256,768]{2,1,0:T(8,128)(2,1)S(1)}, u32[]{:S(2)}, u32[]{:S(2)}) async-start(bf16[4,256,768]{2,1,0:T(8,128)(2,1)} %bitcast.34), calls=%async_computation.3 | async-start | bytes 3145728 | tf_op jit(solution)/shard_map/all_to_all | solution.py:729
  342.2 11.5 %copy-start.1 = (bf16[4,2,96,768]{3,2,1,0:T(8,128)(2,1)S(1)}, bf16[4,2,96,768]{3,2,1,0:T(8,128)(2,1)}, u32[]{:S(2)}) copy-start(bf16[4,2,96,768]{3,2,1,0:T(8,128)(2,1)} %copy-done) | copy-start | bytes 3538948
  357.4 34.7 %collective-permute-start.5 = (bf16[8,1,96,768]{3,2,0,1:T(8,128)(2,1)}, bf16[8,1,96,768]{3,2,0,1:T(8,128)(2,1)}, u32[]{:S(2)}, u32[]{:S(2)}) collective-permute-start(bf16[8,1,96,768]{3,2,0,1:T(8,128)(2,1)} %dynamic-slice_bitcast_fusion.2), channel_id=1, source_target_pairs={{0,1},{1,0},{2,3},{3,2},{4,5},{5,4},{6,7},{7,6},{8,9},{9,8},{10,11... | collective-permute-start | bytes 3538952 | tf_op jit(solution)/shard_map/ppermute | solution.py:608
  357.9 5.9 %copy-start.9 = (bf16[1024,768]{1,0:T(8,128)(2,1)S(1)}, bf16[1024,768]{1,0:T(8,128)(2,1)}, u32[]{:S(2)}) copy-start(bf16[1024,768]{1,0:T(8,128)(2,1)} %get-tuple-element.108) | copy-start | bytes 4718596
  359.9 30.8 %collective-permute-start.6 = (bf16[2,96,768]{2,1,0:T(8,128)(2,1)}, bf16[2,96,768]{2,1,0:T(8,128)(2,1)}, u32[]{:S(2)}, u32[]{:S(2)}) collective-permute-start(bf16[2,96,768]{2,1,0:T(8,128)(2,1)} %get-tuple-element.232), channel_id=1, source_target_pairs={{0,8},{4,12},{8,16},{12,20},{16,24},{20,28},{24,0},{28,4},{1,9},{5... | collective-permute-start | bytes 884744 | tf_op jit(solution)/shard_map/ppermute | solution.py:620
  359.9 30.8 %collective-permute-start.7 = (bf16[2,96,768]{2,1,0:T(8,128)(2,1)}, bf16[2,96,768]{2,1,0:T(8,128)(2,1)}, u32[]{:S(2)}, u32[]{:S(2)}) collective-permute-start(bf16[2,96,768]{2,1,0:T(8,128)(2,1)} %get-tuple-element.234), channel_id=1, source_target_pairs={{0,16},{4,20},{8,24},{12,28},{16,0},{20,4},{24,8},{28,12},{1,17},{... | collective-permute-start | bytes 884744 | tf_op jit(solution)/shard_map/ppermute | solution.py:620
  360.4 30.3 %collective-permute-start.8 = (bf16[2,96,768]{2,1,0:T(8,128)(2,1)S(1)}, bf16[2,96,768]{2,1,0:T(8,128)(2,1)}, u32[]{:S(2)}, u32[]{:S(2)}) collective-permute-start(bf16[2,96,768]{2,1,0:T(8,128)(2,1)S(1)} %get-tuple-element.233), channel_id=1, source_target_pairs={{0,24},{4,28},{8,0},{12,4},{16,8},{20,12},{24,16},{28,20},{1,25},{... | collective-permute-start | bytes 884744 | tf_op jit(solution)/shard_map/ppermute | solution.py:620
  367.6 83.1 %all-to-all-start.5 = ((bf16[4,256,768]{2,1,0:T(8,128)(2,1)}), bf16[4,256,768]{2,1,0:T(8,128)(2,1)S(1)}, u32[]{:S(2)}, u32[]{:S(2)}) async-start(bf16[4,256,768]{2,1,0:T(8,128)(2,1)} %bitcast.243), calls=%async_computation.6 | async-start | bytes 3145728 | tf_op jit(solution)/shard_map/all_to_all | solution.py:731
  394.0 15.8 %copy-start.19 = (f32[2,1,640]{2,1,0:T(1,128)S(1)}, f32[2,1,640]{2,1,0:T(1,128)}, u32[]{:S(2)}) copy-start(f32[2,1,640]{2,1,0:T(1,128)} %get-tuple-element.121) | copy-start | bytes 15364
  394.1 19.1 %copy-start.33 = (f32[1,768]{1,0:T(1,128)S(1)}, f32[1,768]{1,0:T(1,128)}, u32[]{:S(2)}) copy-start(f32[1,768]{1,0:T(1,128)} %get-tuple-element.111) | copy-start | bytes 9220
  394.1 19.1 %copy-start.32 = (f32[1,768]{1,0:T(1,128)S(1)}, f32[1,768]{1,0:T(1,128)}, u32[]{:S(2)}) copy-start(f32[1,768]{1,0:T(1,128)} %get-tuple-element.112) | copy-start | bytes 9220
  394.1 19.1 %copy-start.31 = (f32[1,768]{1,0:T(1,128)S(1)}, f32[1,768]{1,0:T(1,128)}, u32[]{:S(2)}) copy-start(f32[1,768]{1,0:T(1,128)} %get-tuple-element.113) | copy-start | bytes 9220
  394.1 19.1 %copy-start.30 = (f32[1,768]{1,0:T(1,128)S(1)}, f32[1,768]{1,0:T(1,128)}, u32[]{:S(2)}) copy-start(f32[1,768]{1,0:T(1,128)} %get-tuple-element.114) | copy-start | bytes 9220
  394.1 19.1 %copy-start.29 = (f32[1,768]{1,0:T(1,128)S(1)}, f32[1,768]{1,0:T(1,128)}, u32[]{:S(2)}) copy-start(f32[1,768]{1,0:T(1,128)} %get-tuple-element.115) | copy-start | bytes 9220
  394.1 19.1 %copy-start.28 = (f32[1,768]{1,0:T(1,128)S(1)}, f32[1,768]{1,0:T(1,128)}, u32[]{:S(2)}) copy-start(f32[1,768]{1,0:T(1,128)} %get-tuple-element.116) | copy-start | bytes 9220
  394.1 19.1 %copy-start.27 = (f32[1,768]{1,0:T(1,128)S(1)}, f32[1,768]{1,0:T(1,128)}, u32[]{:S(2)}) copy-start(f32[1,768]{1,0:T(1,128)} %get-tuple-element.117) | copy-start | bytes 9220
  394.1 19.1 %copy-start.26 = (f32[1,768]{1,0:T(1,128)S(1)}, f32[1,768]{1,0:T(1,128)}, u32[]{:S(2)}) copy-start(f32[1,768]{1,0:T(1,128)} %get-tuple-element.118) | copy-start | bytes 9220
  394.1 19.1 %copy-start.25 = (f32[1,768]{1,0:T(1,128)S(1)}, f32[1,768]{1,0:T(1,128)}, u32[]{:S(2)}) copy-start(f32[1,768]{1,0:T(1,128)} %get-tuple-element.119) | copy-start | bytes 9220
  413.5 4.3 collective-permute-start.10
  414.1 8.8 %collective-permute-start.24 = (bf16[96,768]{1,0:T(8,128)(2,1)S(1)}, bf16[96,768]{1,0:T(8,128)(2,1)S(1)}, u32[]{:S(2)}, u32[]{:S(2)}) collective-permute-start(bf16[96,768]{1,0:T(8,128)(2,1)S(1)} %slice_bitcast_fusion.1), channel_id=1, source_target_pairs={{0,2},{1,3},{2,0},{3,1},{4,6},{5,7},{6,4},{7,5},{8,10},{9,11},{10,... | collective-permute-start | bytes 442376 | tf_op jit(solution)/shard_map/ppermute | solution.py:624
  417.5 18.7 %collective-permute-start.25 = (bf16[96,1536]{1,0:T(8,128)(2,1)}, bf16[96,1536]{1,0:T(8,128)(2,1)}, u32[]{:S(2)}, u32[]{:S(2)}) collective-permute-start(bf16[96,1536]{1,0:T(8,128)(2,1)} %slice_bitcast_fusion), channel_id=1, source_target_pairs={{0,2},{1,3},{2,0},{3,1},{4,6},{5,7},{6,4},{7,5},{8,10},{9,11},{10,... | collective-permute-start | bytes 884744 | tf_op jit(solution)/shard_map/ppermute | solution.py:624
  417.9 4.4 collective-permute-start.11
  420.2 18.8 %collective-permute-start.9 = (bf16[4,1,96,768]{3,2,1,0:T(8,128)(2,1)}, bf16[4,1,96,768]{3,2,1,0:T(8,128)(2,1)}, u32[]{:S(2)}, u32[]{:S(2)}) collective-permute-start(bf16[4,1,96,768]{3,2,1,0:T(8,128)(2,1)} %dynamic-slice_bitcast_fusion.4), channel_id=1, source_target_pairs={{0,4},{4,0},{8,12},{12,8},{16,20},{20,16},{24,28},{28,24},{1,5},{5... | collective-permute-start | bytes 1769480 | tf_op jit(solution)/shard_map/ppermute | solution.py:613
  422.2 4.4 collective-permute-start.12
  423.6 12.5 %copy-start.11 = (bf16[1,2,96,1536]{3,2,1,0:T(8,128)(2,1)S(1)}, bf16[1,2,96,1536]{3,2,1,0:T(8,128)(2,1)}, u32[]{:S(2)}) copy-start(bf16[1,2,96,1536]{3,2,1,0:T(8,128)(2,1)} %reduce-scatter.2.cloned.1.call-done) | copy-start | bytes 1769476
  427.3 6.2 %collective-permute-start.13 = (f32[16640]{0:T(1024)}, f32[16640]{0:T(1024)}, u32[]{:S(2)}, u32[]{:S(2)}) collective-permute-start(f32[16640]{0:T(1024)} %add.297), channel_id=1, source_target_pairs={{0,16},{4,20},{8,24},{12,28},{16,0},{20,4},{24,8},{28,12},{1,17},{... | collective-permute-start | bytes 199688 | tf_op jit(solution)/shard_map/ppermute | solution.py:710
  434.4 4.4 collective-permute-start.14
  442.2 5.8 %collective-permute-start.15 = (bf16[8,1,96,768]{3,2,0,1:T(8,128)(2,1)}, bf16[8,1,96,768]{3,2,0,1:T(8,128)(2,1)}, u32[]{:S(2)}, u32[]{:S(2)}) collective-permute-start(bf16[8,1,96,768]{3,2,0,1:T(8,128)(2,1)} %dynamic-slice_bitcast_fusion.1), channel_id=1, source_target_pairs={{0,1},{1,0},{2,3},{3,2},{4,5},{5,4},{6,7},{7,6},{8,9},{9,8},{10,11... | collective-permute-start | bytes 3538952 | tf_op jit(solution)/shard_map/ppermute | solution.py:608
  442.2 5.8 %copy-start.18 = (f32[2,640]{1,0:T(2,128)}, f32[2,640]{1,0:T(2,128)S(1)}, u32[]{:S(2)}) copy-start(f32[2,640]{1,0:T(2,128)S(1)} %fusion.69) | copy-start | bytes 15364
  450.7 6.9 %slice-start = ((f32[2,640]{1,0:T(2,128)}), f32[2,128]{1,0:T(2,128)S(1)}, s32[]{:S(2)}) async-start(f32[2,640]{1,0:T(2,128)} %copy-done.18), calls=%async_computation.10 | async-start | bytes 2048 | tf_op jit(solution)/shard_map/slice | solution.py:490
  450.7 31.2 %all-to-all-start.4 = ((bf16[4,256,768]{2,1,0:T(8,128)(2,1)}), bf16[4,256,768]{2,1,0:T(8,128)(2,1)S(1)}, u32[]{:S(2)}, u32[]{:S(2)}) async-start(bf16[4,256,768]{2,1,0:T(8,128)(2,1)} %bitcast.56), calls=%async_computation.5 | async-start | bytes 3145728 | tf_op jit(solution)/shard_map/all_to_all | solution.py:732
  454.4 21.3 %copy-start.2 = (bf16[8,1,96,768]{3,2,0,1:T(8,128)(2,1)S(1)}, bf16[8,1,96,768]{3,2,0,1:T(8,128)(2,1)}, u32[]{:S(2)}) copy-start(bf16[8,1,96,768]{3,2,0,1:T(8,128)(2,1)} %fusion.2) | copy-start | bytes 3538948
  455.6 20.0 %collective-permute-start.16 = (bf16[4,1,96,768]{3,2,1,0:T(8,128)(2,1)S(1)}, bf16[4,1,96,768]{3,2,1,0:T(8,128)(2,1)S(1)}, u32[]{:S(2)}, u32[]{:S(2)}) collective-permute-start(bf16[4,1,96,768]{3,2,1,0:T(8,128)(2,1)S(1)} %dynamic-slice_bitcast_fusion.3), channel_id=1, source_target_pairs={{0,4},{4,0},{8,12},{12,8},{16,20},{20,16},{24,28},{28,24},{1,5},{5... | collective-permute-start | bytes 1769480 | tf_op jit(solution)/shard_map/ppermute | solution.py:613
  458.7 8.7 %collective-permute-start.20 = (bf16[1,96,768]{2,1,0:T(8,128)(2,1)S(1)}, bf16[1,96,768]{2,1,0:T(8,128)(2,1)S(1)}, u32[]{:S(2)}, u32[]{:S(2)}) collective-permute-start(bf16[1,96,768]{2,1,0:T(8,128)(2,1)S(1)} %get-tuple-element.250), channel_id=1, source_target_pairs={{0,8},{4,12},{8,16},{12,20},{16,24},{20,28},{24,0},{28,4},{1,9},{5... | collective-permute-start | bytes 442376 | tf_op jit(solution)/shard_map/ppermute | solution.py:620
  458.8 14.0 %collective-permute-start.21 = (bf16[1,96,768]{2,1,0:T(8,128)(2,1)S(1)}, bf16[1,96,768]{2,1,0:T(8,128)(2,1)S(1)}, u32[]{:S(2)}, u32[]{:S(2)}) collective-permute-start(bf16[1,96,768]{2,1,0:T(8,128)(2,1)S(1)} %get-tuple-element.252), channel_id=1, source_target_pairs={{0,16},{4,20},{8,24},{12,28},{16,0},{20,4},{24,8},{28,12},{1,17},{... | collective-permute-start | bytes 442376 | tf_op jit(solution)/shard_map/ppermute | solution.py:620
  460.1 12.7 %collective-permute-start.22 = (bf16[1,96,768]{2,1,0:T(8,128)(2,1)S(1)}, bf16[1,96,768]{2,1,0:T(8,128)(2,1)S(1)}, u32[]{:S(2)}, u32[]{:S(2)}) collective-permute-start(bf16[1,96,768]{2,1,0:T(8,128)(2,1)S(1)} %get-tuple-element.251), channel_id=1, source_target_pairs={{0,24},{4,28},{8,0},{12,4},{16,8},{20,12},{24,16},{28,20},{1,25},{... | collective-permute-start | bytes 442376 | tf_op jit(solution)/shard_map/ppermute | solution.py:620
  473.8 10.4 %collective-permute-start.23 = (bf16[96,768]{1,0:T(8,128)(2,1)S(1)}, bf16[96,768]{1,0:T(8,128)(2,1)S(1)}, u32[]{:S(2)}, u32[]{:S(2)}) collective-permute-start(bf16[96,768]{1,0:T(8,128)(2,1)S(1)} %fusion.48), channel_id=1, source_target_pairs={{0,2},{1,3},{2,0},{3,1},{4,6},{5,7},{6,4},{7,5},{8,10},{9,11},{10,... | collective-permute-start | bytes 442376 | tf_op jit(solution)/shard_map/ppermute | solution.py:624
  476.7 9.0 %collective-permute-start.17 = (bf16[1,96,768]{2,1,0:T(8,128)(2,1)}, bf16[1,96,768]{2,1,0:T(8,128)(2,1)}, u32[]{:S(2)}, u32[]{:S(2)}) collective-permute-start(bf16[1,96,768]{2,1,0:T(8,128)(2,1)} %get-tuple-element.247), channel_id=1, source_target_pairs={{0,8},{4,12},{8,16},{12,20},{16,24},{20,28},{24,0},{28,4},{1,9},{5... | collective-permute-start | bytes 442376 | tf_op jit(solution)/shard_map/ppermute | solution.py:620
  479.5 10.3 %collective-permute-start.18 = (bf16[1,96,768]{2,1,0:T(8,128)(2,1)}, bf16[1,96,768]{2,1,0:T(8,128)(2,1)}, u32[]{:S(2)}, u32[]{:S(2)}) collective-permute-start(bf16[1,96,768]{2,1,0:T(8,128)(2,1)} %get-tuple-element.249), channel_id=1, source_target_pairs={{0,16},{4,20},{8,24},{12,28},{16,0},{20,4},{24,8},{28,12},{1,17},{... | collective-permute-start | bytes 442376 | tf_op jit(solution)/shard_map/ppermute | solution.py:620
  480.7 9.2 %collective-permute-start.19 = (bf16[1,96,768]{2,1,0:T(8,128)(2,1)}, bf16[1,96,768]{2,1,0:T(8,128)(2,1)}, u32[]{:S(2)}, u32[]{:S(2)}) collective-permute-start(bf16[1,96,768]{2,1,0:T(8,128)(2,1)} %get-tuple-element.248), channel_id=1, source_target_pairs={{0,24},{4,28},{8,0},{12,4},{16,8},{20,12},{24,16},{28,20},{1,25},{... | collective-permute-start | bytes 442376 | tf_op jit(solution)/shard_map/ppermute | solution.py:620
  (19 other events, 59.5 us)
Sparse Core Ops, SparseCore 0:
  20.7 82.8 all-gather.4
  106.5 79.5 all-gather.6
  229.9 111.1 reduce-scatter.1

commit v3 on v2

--- a/solution.py
+++ b/solution.py
@@ -5,6 +5,7 @@
 import jax.numpy as jnp
 from jax import lax
 from jax.experimental import pallas as pl
+from jax.experimental.layout import Layout, with_layout_constraint
 from jax.experimental.pallas import tpu as pltpu
 from jax.sharding import PartitionSpec as P
 
@@ -318,25 +319,22 @@
     datt_ref[0] = mm(d_ref[...], matrix(w_ref)).astype(BF)
 
 
-def cross_back_kernel(dh_ref, w_ref, n_ref, side_ref, dlow_ref, att_ref, mid_ref, y_ref, dmid_ref, gain_ref, gainy_ref,
-                      dw_ref, dbias_ref, dout_ref, dbranch_ref, other_ref, dg_ref, ds_ref, dgy_ref, dsy_ref, dob_ref,
-                      acc_n, acc_side):
+def cross_back_kernel(dh_ref, w_ref, n_ref, side_ref, dlow_ref, att_ref, mid_ref, dmid_ref, gain_ref,
+                      dw_ref, dbias_ref, dout_ref, dbranch_ref, dg_ref, ds_ref, dob_ref, acc_n):
     j = pl.program_id(0)
     rows, width = mid_ref.shape
     wq = matrix(w_ref, 0, 2 * PAIR)
-    wkv = matrix(w_ref, PAIR, 5 * PAIR)
     low = is_low(TALL)
     nought = jnp.zeros((TALL, PAIR), BF)
-    clear(acc_n, acc_side)
+    clear(acc_n)
 
     def one(i, at, total):
         d = dh_ref[0, at, :]
-        t0, t1, t2, t3, t4 = split_tiles(d)
-        acc_n[at, :] += mm_t(jnp.concatenate([t0, jnp.where(low, t1, nought)], 1), wq)
-        acc_side[at, :] += mm_t(jnp.concatenate([jnp.where(low, nought, t1), t2, t3, t4], 1), wkv)
+        acc_n[at, :] += mm_t(jnp.concatenate([d[:, :PAIR], jnp.where(low, d[:, PAIR : 2 * PAIR], nought)], 1), wq)
         return total + col_sum(d.astype(F32))
 
-    dbias_ref[0] = each(rows, TALL, one, jnp.zeros((1, 5 * PAIR), F32))
+    dbias_ref[0, :, : 5 * PAIR] = each(rows, TALL, one, jnp.zeros((1, 5 * PAIR), F32))
+    dbias_ref[0, :, 5 * PAIR :] = jnp.zeros((1, PAIR), F32)
     low_p = is_low(PART)
 
     def weight(i, at, c):
@@ -359,12 +357,33 @@
             dout_ref[at, :] = total
             branch = total.astype(BF)
             dbranch_ref[at, :] = branch
-            other, dgy, dsy = norm_back(acc_side[at, :], y_ref[at, :].astype(F32), gainy_ref[...])
+            return tuple(s + a for s, a in zip(sums, (dg, ds, col_sum(branch.astype(F32)))))
+
+        sums = each(rows, ROWS, last, (jnp.zeros((1, width), F32),) * 3)
+        dg_ref[...], ds_ref[...], dob_ref[...] = sums
+
+
+def side_back_kernel(dh_ref, w_ref, y_ref, gain_ref, other_ref, dg_ref, ds_ref, acc):
+    rows, width = y_ref.shape
+    w = matrix(w_ref, PAIR, 5 * PAIR)
+    low = is_low(TALL)
+    nought = jnp.zeros((TALL, PAIR), BF)
+    clear(acc)
+
+    def one(i, at, c):
+        d = dh_ref[0, at, :]
+        acc[at, :] += mm_t(jnp.concatenate([jnp.where(low, nought, d[:, PAIR : 2 * PAIR]), d[:, 2 * PAIR :]], 1), w)
+
+    each(rows, TALL, one)
+
+    @pl.when(pl.program_id(0) == pl.num_programs(0) - 1)
+    def _():
+        def last(i, at, sums):
+            other, dg, ds = norm_back(acc[at, :], y_ref[at, :].astype(F32), gain_ref[...])
             other_ref[at, :] = other.astype(BF)
-            return tuple(s + a for s, a in zip(sums, (dg, ds, dgy, dsy, col_sum(branch.astype(F32)))))
-
-        sums = each(rows, ROWS, last, (jnp.zeros((1, width), F32),) * 5)
-        dg_ref[...], ds_ref[...], dgy_ref[...], dsy_ref[...], dob_ref[...] = sums
+            return sums[0] + dg, sums[1] + ds
+
+        dg_ref[...], ds_ref[...] = each(rows, ROWS, last, (jnp.zeros((1, width), F32),) * 2)
 
 
 def self_back_part(dh_ref, w_ref, n_ref, dlow_ref, att_ref, dw_ref, dbias_ref, acc_ref):
@@ -377,7 +396,8 @@
         acc_ref[at, :] += mm_t(d, w)
         return total + col_sum(d.astype(F32))
 
-    dbias_ref[0] = each(rows, TALL, one, jnp.zeros((1, 5 * PAIR), F32))
+    dbias_ref[0, :, : 5 * PAIR] = each(rows, TALL, one, jnp.zeros((1, 5 * PAIR), F32))
+    dbias_ref[0, :, 5 * PAIR :] = jnp.zeros((1, PAIR), F32)
 
     def weight(i, at, c):
         dqkv = t_mm(n_ref[:, at], dh_ref[0])
@@ -407,6 +427,16 @@
             return sums[0] + dg, sums[1] + ds
 
         dg_ref[...], ds_ref[...] = each(rows, ROWS, last, (jnp.zeros((1, width), F32),) * 2)
+
+
+def collect_kernel(*refs):
+    *ins, out_ref = refs
+    out_ref[...] = jnp.zeros(out_ref.shape, F32)
+    at = 0
+    for ref in ins:
+        for i in range(ref.shape[0]):
+            out_ref[at : at + 1, :] = ref[i] if len(ref.shape) == 3 else ref[...]
+            at += 1
 
 
 def tables(image_sizes, count):
@@ -493,16 +523,18 @@
         heads = (join(t[0], t[1][..., :h]), join(t[2], t[1][..., h:]), join(t[3], t[4][..., :h]))
         return heads + ((join(t[5], t[4][..., h:]),) if len(t) > 5 else ())
 
-    def gather(pack):
-        pair = jnp.stack([of_view(pack, view), lax.ppermute(of_view(pack, 1 - view), "mp", partner)], 0)
+    def pair_of(pack):
+        return jnp.stack([of_view(pack, view), lax.ppermute(of_view(pack, 1 - view), "mp", partner)], 0)
+
+    def gather(pair):
         got = lax.all_gather(pair, both, axis=0, axis_index_groups=groups).reshape(n_dp, batches, 2, r, -1)
         return got if split else got.transpose(1, 2, 0, 3, 4).reshape(1, batches, 2, deep, -1)
 
     flip = lambda a: a.swapaxes(-1, -2)
     pack_self = cols(qkv_w[:, :, 0], qkv_w[:, :, 1], qkv_w[:, :, 2], flip(out_w))
     pack_cross = cols(cq_w, ckv_w[:, :, 0], ckv_w[:, :, 1], flip(cout_w))
-    w_att = gather(jnp.concatenate([pack_self, pack_cross], -1))
-    w_ffn = gather(jnp.concatenate([up_w, flip(down_w)], -1))
+    w_att = gather(pair_of(jnp.concatenate([pack_self, pack_cross], -1)))
+    pair_ffn = pair_of(jnp.concatenate([up_w, flip(down_w)], -1))
 
     none = jnp.zeros_like(cq_b)
     bias_pack = jnp.concatenate([cols(qkv_b[:, 0], qkv_b[:, 1], qkv_b[:, 2], none), cols(cq_b, ckv_b[:, 0], ckv_b[:, 1], none), up_b], -1)
@@ -554,7 +586,7 @@
     heads = sds((members, rows, 5 * PAIR), BF)
     att_low = sds((members, rows, 2 * PAIR), BF)
     att_high = sds((members, rows, 2 * PAIR), F32)
-    bias_out = sds((members, 1, 5 * PAIR), F32)
+    bias_out = sds((members, 1, 6 * PAIR), F32)
     gemm = 2 * rows * width * width * members
 
     def attend(h):
@@ -592,7 +624,9 @@
         return piece
 
     def scatter(piece):
-        return lax.psum_scatter(by_owner(piece).reshape(n_dp * batches, 2, r, -1), both, scatter_dimension=0, axis_index_groups=groups)
+        whole_piece = by_owner(piece).reshape(n_dp * batches, 2, r, -1)
+        total = lax.psum_scatter(whole_piece, both, scatter_dimension=0, axis_index_groups=groups)
+        return with_layout_constraint(total, Layout(major_to_minor=(0, 1, 2)))
 
     core_pairs = [(i, i ^ 1) for i in range(members)]
     x_pairs = [(i, i ^ 1) for i in range(n_dp)]
@@ -603,30 +637,43 @@
         return lax.dynamic_index_in_dim(a, i, axis, keepdims=False)
 
     by_hand = batches == 2 and n_dp <= 8
+    x_place, z_place = place % 2, place // 2
+
+    def added(terms):
+        total = terms[0].astype(F32)
+        for term in terms[1:]:
+            total = total + term.astype(F32)
+        return total
+
+    def hop(terms, axis, other, mine, name, perm):
+        got = lax.ppermute(added([pick(t, other, axis) for t in terms]).astype(BF), name, perm)
+        return [pick(t, mine, axis) for t in terms] + [got]
 
     def over_cores(piece):
-        got = lax.ppermute(pick(piece, 1 - batch, 1), "mp", core_pairs)
-        return (pick(piece, batch, 1).astype(F32) + got.astype(F32)).astype(BF)
-
-    def over_x(piece):
-        piece = piece.reshape((piece.shape[0] // 2, 2) + piece.shape[1:])
-        got = lax.ppermute(pick(piece, 1 - place % 2, 1), "dp", x_pairs)
-        return (pick(piece, place % 2, 1).astype(F32) + got.astype(F32)).astype(BF)
-
-    def over_z(piece):
-        total = pick(piece, place // 2, 0).astype(F32)
+        return hop([piece], 1, 1 - batch, batch, "mp", core_pairs)
+
+    def over_x(terms):
+        terms = [t.reshape((t.shape[0] // 2, 2) + t.shape[1:]) for t in terms]
+        return hop(terms, 1, 1 - x_place, x_place, "dp", x_pairs)
+
+    def over_z(terms):
+        total = added([pick(t, z_place, 0) for t in terms])
         for s in range(1, lines):
             perm = [(i, (i + 2 * s) % n_dp) for i in range(n_dp)]
-            total = total + lax.ppermute(pick(piece, (place // 2 + s) % lines, 0), "dp", perm).astype(F32)
+            total = total + lax.ppermute(added([pick(t, (z_place + s) % lines, 0) for t in terms]).astype(BF), "dp", perm).astype(F32)
         return total.astype(BF)
 
-    def settle(total):
-        theirs = lax.ppermute(total[1], "mp", partner).astype(F32)
-        keep = total[0].astype(F32)
+    def to_partner(a):
+        return lax.ppermute(a, "mp", partner)
+
+    def both_views(keep, theirs):
+        keep, theirs = keep.astype(F32), theirs.astype(F32)
         return jnp.stack([jnp.where(view == 0, keep, theirs), jnp.where(view == 0, theirs, keep)], 0)
 
     n1 = norm(x, g1, s1)
     side = norm(y, gy, sy)
+    pair_ffn, n1, side, qf, kf, cosine, sine = lax.optimization_barrier((pair_ffn, n1, side, qf, kf, cosine, sine))
+    w_ffn = gather(pair_ffn)
     hs = call(self_in_kernel, "self_in", members, given(n1) + [(w_att, weight_block(w_att, 6 * PAIR, 0))] + steps(self_bias) + given(cosine, sine),
               [(heads, per_step(heads))], flops=gemm, moved=rows * width * 16)[0]
     att, lse = attend(hs)
@@ -651,20 +698,22 @@
     d_hc = attend_back(hc, catt, d_catt, clse)
     dw_att = sds((blocks, batches, 2, deep, 6 * PAIR), BF)
     dw_spec = pl.BlockSpec((blocks, 1, 1, deep, 6 * PAIR), lambda j: (0, j // 2, j % 2, 0, 0))
-    dw_cross, d_crossb, d_mid, d_branch, other, gg2, gs2, ggy, gsy, d_ob = call(
+    dw_cross, d_crossb, d_mid, d_branch, gg2, gs2, d_ob = call(
         cross_back_kernel, "cross_back", members,
-        steps(d_hc) + [(w_att, weight_block(w_att, 6 * PAIR, 1))] + given(n2, side, d_cross) + steps(catt) + given(middle, y, d_mid2, g2, gy),
-        [(dw_att, dw_spec), (bias_out, per_step(bias_out))] + full(high, low, low, line, line, line, line, line),
-        [pltpu.VMEM((rows, width), F32)] * 2, flops=3 * gemm, moved=rows * width * 40)
+        steps(d_hc) + [(w_att, weight_block(w_att, 6 * PAIR, 1))] + given(n2, side, d_cross) + steps(catt) + given(middle, d_mid2, g2),
+        [(dw_att, dw_spec), (bias_out, per_step(bias_out))] + full(high, low, line, line, line),
+        [pltpu.VMEM((rows, width), F32)], flops=2 * gemm, moved=rows * width * 30)
+
+    def side_back(dh):
+        return call(side_back_kernel, "side_back", members, steps(dh) + [(w_att, weight_block(w_att, 6 * PAIR, 1))] + given(y, gy),
+                    full(low, line, line), [pltpu.VMEM((rows, width), F32)], flops=gemm, moved=rows * width * 16)
+
     d_att = project_back(d_branch, 2)
-    if by_hand:
-        cross = over_cores(by_owner(dw_cross))
-        d_att, cross = lax.optimization_barrier((d_att, cross))
-        cross_a = over_x(cross[: n_dp // 2])
+    total_cross = scatter(dw_cross)
 
     dw_part = sds((blocks, batches, 1, deep, 6 * PAIR), BF)
     dw_part_spec = pl.BlockSpec((blocks, 1, 1, deep, 6 * PAIR), lambda j: (0, j, 0, 0, 0))
-    bias_part = sds((batches, 1, 5 * PAIR), F32)
+    bias_part = sds((batches, 1, 6 * PAIR), F32)
 
     def self_back(t, dh, *more):
         ins = steps(dh) + [(w_att, weight_block(w_att, 6 * PAIR, 0, t))] + given(n1, d_branch) + [(att, per_step(att, t))]
@@ -674,69 +723,98 @@
                         [pltpu.VMEM((rows, width), F32)], flops=1.5 * gemm, moved=rows * width * 30)
         return call(self_back_first_kernel, "self_back_first", batches, ins, outs + full(high), flops=1.5 * gemm, moved=rows * width * 24)
 
+    def home(a):
+        return lax.all_to_all(a.reshape(members, local, width), "mp", 0, 0, tiled=True).reshape(2, batches, local, width)
+
     d_h1 = attend_back(hs, att, d_att, lse, 1)
+    dw_self1, d_selfb1, acc = self_back(1, d_h1)
+    d_att, acc, dw_self1 = lax.optimization_barrier((d_att, acc, dw_self1))
+    output = from_row(output, rows - first)
     if by_hand:
-        d_h1, cross, cross_a = lax.optimization_barrier((d_h1, cross, cross_a))
-        cross_b = over_x(cross[n_dp // 2 :])
-    dw_self1, d_selfb1, acc = self_back(1, d_h1)
+        self1 = over_cores(by_owner(dw_self1))
+        d_att, output, got = lax.optimization_barrier((d_att, output, self1[1]))
+        self1 = over_x([self1[0], got])
+    got_output = home(output)
+    d_h0 = attend_back(hs, att, d_att, lse, 0)
+    d_h0, total_ffn, got_output = lax.optimization_barrier((d_h0, total_ffn, got_output))
+    their_ffn = to_partner(total_ffn[1])
     if by_hand:
-        d_att, acc, cross_a, cross_b, dw_self1 = lax.optimization_barrier((d_att, acc, cross_a, cross_b, dw_self1))
-        cross = over_z(jnp.concatenate([cross_a, cross_b], 0))
-        self1 = over_cores(by_owner(dw_self1))
-    d_h0 = attend_back(hs, att, d_att, lse, 0)
+        d_h0, got = lax.optimization_barrier((d_h0, self1[2]))
+        total1 = over_z(self1[:2] + [got])
+    dw_self0, d_selfb0, own, gg1, gs1 = self_back(0, d_h0, x, d_mid, acc, g1)
     if by_hand:
-        d_h0, total_ffn, self1, cross = lax.optimization_barrier((d_h0, total_ffn, self1, cross))
-        self1 = over_x(self1)
+        own, dw_self0, gg1, their_ffn, total1 = lax.optimization_barrier((own, dw_self0, gg1, their_ffn, total1))
+        self0 = over_cores(by_owner(dw_self0))
+        own = from_row(own, rows - first)
+        own, got, gg1 = lax.optimization_barrier((own, self0[1], gg1))
+        self0 = [t.reshape((lines, 2) + t.shape[1:]) for t in (self0[0], got)]
+        send = added([pick(t, 1 - x_place, 1) for t in self0]).astype(BF)
+        own, send, d_hc = lax.optimization_barrier((own, send, d_hc))
+        self0 = [pick(t, x_place, 1) for t in self0] + [lax.ppermute(send, "dp", x_pairs)]
     else:
-        d_h0, total_ffn = lax.optimization_barrier((d_h0, total_ffn))
-    dw_self0, d_selfb0, own, gg1, gs1 = self_back(0, d_h0, x, d_mid, acc, g1)
-    d_selfb = jnp.stack([d_selfb0, d_selfb1], 1).reshape(members, 1, 5 * PAIR)
-    sum_ffn = settle(total_ffn)
+        own = from_row(own, rows - first)
+    got_own = home(own)
+    other, ggy, gsy = side_back(d_hc)
     if by_hand:
-        own, dw_self0, self1 = lax.optimization_barrier((own, dw_self0, self1))
-        self0 = over_z(over_x(over_cores(by_owner(dw_self0))))
-        self1 = over_z(self1)
-        sum_cross = settle(cross)
-        sum_self = settle(jnp.concatenate([self0, self1], 0))
+        other, x_sum = lax.optimization_barrier((other, self0[2]))
+        self0 = self0[:2] + [x_sum]
+    lines_out = [gg1, gs1, d_ob, gg2, gs2, ggy, gsy, d_cob, gg3, gs3, d_db, d_selfb0, d_selfb1, d_crossb, d_upb]
+    count = 11 + 3 * members
+    collected = sds((-(-count // 8) * 8, width), F32)
+    small = call(collect_kernel, "collect", 1, given(*lines_out), full(collected))[0]
+    if by_hand:
+        small = small + lax.ppermute(small, "mp", core_pairs)
+        sum_ffn = both_views(total_ffn[0], their_ffn)
+        up_wg, down_wg = sum_ffn[..., :fw], flip(sum_ffn[..., fw:])
+        their1 = to_partner(total1)
+        flat = small + lax.ppermute(small, "dp", x_pairs)
+        flat, got, their1, got_own, other, up_wg, down_wg, total_cross = lax.optimization_barrier((flat, self0[2], their1, got_own, other, up_wg, down_wg, total_cross))
+        other = from_row(other, rows - first)
+        got_other = home(other)
+        their_cross = to_partner(total_cross[1])
+        flat = lax.reduce_precision(flat, 8, 7)
+        self0 = self0[:2] + [got]
+        total0 = added([pick(t, z_place, 0) for t in self0])
+        on_line = [flat]
+        for s in range(1, lines):
+            send = added([pick(t, (z_place + s) % lines, 0) for t in self0]).astype(BF)
+            got = lax.ppermute(jnp.concatenate([send.reshape(-1, width), flat.astype(BF)], 0), "dp", [(i, (i + 2 * s) % n_dp) for i in range(n_dp)])
+            total0 = total0 + got[: send.size // width].reshape(total0.shape).astype(F32)
+            on_line.append(got[send.size // width :].astype(F32))
+        on_line = jnp.stack(on_line, 0)
+        flat = sum(pick(on_line, (z_place - p) % lines, 0) for p in range(lines))
+        flat_in = to_partner(flat)
+        sum_self = both_views(total0[0], their1[0])
     else:
-        sum_cross = settle(scatter(dw_cross))
-        sum_self = settle(scatter(jnp.concatenate([dw_self0, dw_self1], 2)))
-
-    def over_all(flat):
-        for perm in [[(i, i // batches * batches + (i + s) % batches) for i in range(members)] for s in range(1, batches)]:
-            flat = flat + lax.ppermute(flat, "mp", perm)
-        step = 1
-        while step < n_dp:
-            flat = flat + lax.ppermute(flat, "dp", [(i, i ^ step) for i in range(n_dp)])
-            step *= 2
-        theirs = lax.ppermute(flat, "mp", partner)
-        return jnp.stack([jnp.where(view == 0, flat, theirs), jnp.where(view == 0, theirs, flat)], 0)
-
-    sums = over_all(jnp.concatenate([gg1, gs1, d_ob, gg2, gs2, ggy, gsy, d_cob, gg3, gs3, d_db] + [by_member(a[:, 0]).reshape(1, -1) for a in (d_selfb, d_crossb, d_upb)], -1)[0])
+        got_other = home(from_row(other, rows - first))
+        total_self = scatter(jnp.concatenate([dw_self0, dw_self1], 2))
+        their_cross = to_partner(total_cross[1])
+        sum_self = both_views(total_self[0], to_partner(total_self[1]))
+        sums = lax.psum(jnp.stack([jnp.where(view == 0, small, 0.0), jnp.where(view == 1, small, 0.0)], 0), both)
+        flat, flat_in = pick(sums, view, 0), pick(sums, 1 - view, 0)
+        sum_ffn = both_views(total_ffn[0], their_ffn)
+        up_wg, down_wg = sum_ffn[..., :fw], flip(sum_ffn[..., fw:])
+    sum_cross = both_views(total_cross[0], their_cross)
+
+    sums = both_views(flat[:11].reshape(-1), flat_in[:11].reshape(-1))
     g1g, s1g, obg, g2g, s2g, gyg, syg, cobg, g3g, s3g, dbg = [sums[:, i * width : (i + 1) * width] for i in range(11)]
-    at_self = 11 * width
-    at_cross = at_self + members * 5 * PAIR
-    at_up = at_cross + members * 5 * PAIR
-
-    def member_part(flat, size):
-        return lax.dynamic_index_in_dim(flat.reshape(2, members, size), me, 1, keepdims=False)
-
-    cross_part = uncols(member_part(sums[:, at_cross:at_up], 5 * PAIR))
-    upb_grad = member_part(sums[:, at_up:], fw)
-    self_part = uncols(member_part(sums[:, at_self:at_cross], 5 * PAIR))
-
-    output, other, own = [from_row(a, rows - first) for a in (output, other, own)]
-    back = lax.all_to_all(output.reshape(members, local, width), "mp", 0, 0, tiled=True)
-    block_output = back.reshape(2, batches, local, width).swapaxes(0, 1)
-    got_other = lax.all_to_all(other.reshape(members, local, width), "mp", 0, 0, tiled=True).reshape(2, batches, local, width)
-    got_own = lax.all_to_all(own.reshape(members, local, width), "mp", 0, 0, tiled=True).reshape(2, batches, local, width)
+
+    def member_row(own_row, other_row):
+        return both_views(pick(flat, own_row, 0), pick(flat_in, other_row, 0))
+
+    self_part = uncols(member_row(11 + batch, 11 + batches + batch)[:, : 5 * PAIR])
+    start = 11 + members + 2 * batch
+    cross_part = uncols(member_row(start, start + 1)[:, : 5 * PAIR])
+    upb_grad = member_row(start + members, start + members + 1)
+
+    block_output = got_output.swapaxes(0, 1)
     input_grad = (got_own.astype(F32) + got_other[::-1].astype(F32)).swapaxes(0, 1)
 
     q, k, v, o = uncols(sum_self)
     cq, ck, cv, co = uncols(sum_cross)
     return (block_output, input_grad, g1g, s1g, jnp.stack([q, k, v], 2), jnp.stack(self_part, 1), flip(o), obg, g2g, s2g, gyg, syg,
             cq, cross_part[0], jnp.stack([ck, cv], 2), jnp.stack(cross_part[1:], 1), flip(co), cobg, g3g, s3g,
-            sum_ffn[..., :fw], upb_grad, flip(sum_ffn[..., fw:]), dbg)
+            up_wg, upb_grad, down_wg, dbg)
 
 
 def solution(mesh):

time: 505 us -> 483 us (0.956)
  local copies, waits for them, and re-layouts: 34.4 us -> 19.4 us
  starting transfers between devices: 55.9 us -> 44.7 us
  waiting for transfers between devices: 79.7 us -> 74.5 us
    ppermute x26 -> x18, waiting for transfers between devices: 36.2 us -> 20.9 us  [the longest x4 7.73 us: to_partner(): return lax.ppermute(a, 'mp', partner)]
    squeeze x13 -> x3, local copies, waits for them, and re-layouts: 13.8 us -> 0.04 us  [the longest x1 0.02 us: body(): their_ffn = to_partner(total_ffn[1])]
    all_gather x2, waiting for transfers between devices: 4.48 us -> 16.5 us  [gather(): lax.all_gather(pair, both, axis=0, axis_index_groups=groups)]
    all_to_all x1, waiting for transfers between devices: 15.6 us -> 4.18 us  [body(): got_x = lax.all_to_all(sent_x, 'mp', 0, 0, tiled=True)]
    ppermute x26 -> x18, starting transfers between devices: 32.8 us -> 22.3 us  [the longest x4 7 us: to_partner(): return lax.ppermute(a, 'mp', partner)]
    convert_element_type x7 -> x4, other arithmetic: 13.1 us -> 6.96 us  [the longest x1 2.26 us: over_z(): added([pick(t, (z_place + s) % lines, 0) for t in terms]).astype(BF)]
    pallas_call x17 -> x19, Pallas kernels: 249 us -> 254 us  [call(): pl.pallas_call(kernel, grid=(steps,), in_specs=[s for _, s in ins], out_s...]
    unnamed x123 -> x85, local copies, waits for them, and re-layouts: 14.8 us -> 10.4 us
  transfers between devices with their start and end apart: 35 -> 28, of which waited for: 15 -> 10; matrix products, arithmetic and copies ran while one was open for 18% -> 16% of each run, Pallas kernels for 41% -> 44%
where the time goes in v3:
time: 483 us; the launch traced here: 474 us
  Pallas kernels  254 us (53%)
  waiting for transfers between devices  74.5 us (15%)
  other arithmetic  63.1 us (13%)
  starting transfers between devices  44.7 us (9%)
  local copies, waits for them, and re-layouts  19.4 us (4%)
  between operations  18.3 us (4%)
    pallas_call x19, Pallas kernels, call(): pl.pallas_call(kernel, grid=(steps,), in_specs=[s for _, s in ins], out_s...  254 us
    concatenate x6, other arithmetic, from_row(): return lax.dynamic_slice_in_dim(jnp.concatenate([a, a], 0), at, rows, 0)  22.5 us
    all_to_all x1, waiting for transfers between devices, body(): lax.all_to_all(cotangent.swapaxes(0, 1).reshape(members, local, width), '...  16.8 us
    all_gather x2, waiting for transfers between devices, gather(): lax.all_gather(pair, both, axis=0, axis_index_groups=groups)  16.5 us
    all_to_all x1, waiting for transfers between devices, body(): lax.all_to_all(by_view[::-1].reshape(members, local, width), 'mp', 0, 0,...  11.4 us
    all_to_all x3, starting transfers between devices, home(): lax.all_to_all(a.reshape(members, local, width), 'mp', 0, 0, tiled=True)  11.1 us
    unnamed x85, local copies, waits for them, and re-layouts  10.4 us
  transfers between devices with their start and end apart: 28, of which 10 were waited for; matrix products, arithmetic and copies ran while one was open for 16% of the time, Pallas kernels for 44%

profile of v3, /device:TPU:0, one launch (start us, length us, event | category | flops | bytes accessed | tf_op | source)
XLA Modules:
  0.0 473.7 jit_solution(4078394242126714562)
XLA Ops:
  7.3 1.5 fusion.102
  9.6 3.0 collective-permute-start.1
  12.6 7.0 %collective-permute-done.1 = bf16[96,1536]{1,0:T(8,128)(2,1)S(1)} collective-permute-done((bf16[96,1536]{1,0:T(8,128)(2,1)S(1)}, bf16[96,1536]{1,0:T(8,128)(2,1)S(1)}, u32[]{:S(2)}, u32[]{:S(2)}) %collective-permute-start.1) | collective-permute-done | bytes 294944 | tf_op jit(solution)/shard_map/ppermute | solution.py:527
  22.0 3.7 all-to-all-start.1
  25.7 1.9 fusion.18
  27.6 2.0 collective-permute-start
  34.8 11.4 %all-to-all-done.1 = bf16[4,256,768]{2,1,0:T(8,128)(2,1)S(1)} async-done(((bf16[4,256,768]{2,1,0:T(8,128)(2,1)}), bf16[4,256,768]{2,1,0:T(8,128)(2,1)S(1)}, u32[]{:S(2)}, u32[]{:S(2)}) %all-to-all-start.1) | async-done | bytes 1572896 | tf_op jit(solution)/shard_map/all_to_all | solution.py:546
  46.2 3.6 all-to-all-start
  53.4 3.1 fusion.12
  56.4 1.8 pad_maximum_fusion.2
  58.3 3.7 fusion.4.x_ref.y_ref
  62.0 4.2 norm.3.side_ref
  66.2 4.2 all-to-all-done
  70.5 3.8 fusion.5.x_ref.res_ref
  74.2 4.3 norm.2.n_ref
  79.9 3.7 all-to-all-start.2
  86.8 16.8 %all-to-all-done.2 = bf16[4,256,768]{2,1,0:T(8,128)(2,1)S(1)} async-done(((bf16[4,256,768]{2,1,0:T(8,128)(2,1)}), bf16[4,256,768]{2,1,0:T(8,128)(2,1)S(1)}, u32[]{:S(2)}, u32[]{:S(2)}) %all-to-all-start.2) | async-done | bytes 1572896 | tf_op jit(solution)/shard_map/all_to_all | solution.py:547
  103.6 3.7 fusion.3.dz_ref
  108.0 9.5 %self_in.1.heads_ref = bf16[4,1024,640]{2,1,0:T(8,128)(2,1)} custom-call(bf16[1024,768]{1,0:T(8,128)(2,1)} %norm.2.n_ref, bf16[8,2,2,96,1536]{4,3,2,1,0:T(8,128)(2,1)} %bitcast.229, f32[4,1,768]{2,1,0:T(1,128)} %get-tuple-element.332.bias_ref, f32[1024,128]{1,0:T(8,128)} %get-tuple-element.99.cos_ref, f32[1024,128]{1,0:T(8,128)} %get-tuple-element.100.sin_ref), custom_call_target="tpu_custom_call" | custom-call | flops 301989888 | bytes 786432 | tf_op jit(solution)/shard_map/self_in/pallas_call | solution.py:480
  117.5 14.5 %attend.2 = (bf16[4,1024,256]{2,1,0:T(8,128)(2,1)}, f32[4,1024,256]{2,1,0:T(8,128)}) custom-call(bf16[4,1024,640]{2,1,0:T(8,128)(2,1)} %self_in.1.heads_ref, bf16[1024,128]{1,0:T(8,128)(2,1)} %select_convert_fusion.qf_ref, bf16[1024,128]{1,0:T(8,128)(2,1)} %compare_convert_fusion.kf_ref), custom_call_target="tpu_custom_call" | custom-call | flops 402653184 | bytes 720896 | tf_op jit(solution)/shard_map/attend/pallas_call | solution.py:480
  132.0 6.0 %project.2 = (f32[1024,768]{1,0:T(8,128)}, bf16[1024,768]{1,0:T(8,128)(2,1)}) custom-call(bf16[4,1024,256]{2,1,0:T(8,128)(2,1)} %get-tuple-element.103.att_ref.o_ref, bf16[8,2,2,96,1536]{4,3,2,1,0:T(8,128)(2,1)} %bitcast.230, bf16[1024,768]{1,0:T(8,128)(2,1)} %fusion.5.x_ref.res_ref, f32[1,768]{1,0:T(1,128)} %get-tuple-element.353.bias_ref, ...), custom_call_target="tpu_custom_call" | custom-call | flops 100663296 | bytes 688128 | tf_op jit(solution)/shard_map/project/pallas_call | solution.py:480
  138.0 10.8 %cross_in.1.heads_ref = bf16[4,1024,640]{2,1,0:T(8,128)(2,1)} custom-call(bf16[1024,768]{1,0:T(8,128)(2,1)} %get-tuple-element.104.n_ref, bf16[1024,768]{1,0:T(8,128)(2,1)} %norm.3.side_ref, bf16[8,2,2,96,1536]{4,3,2,1,0:T(8,128)(2,1)} %bitcast.231, f32[4,1,768]{2,1,0:T(1,128)} %get-tuple-element.331.bias_ref, f32[1024,128]{1,0:T(8,128)} %get-tuple-element.99.cos_ref, ...), custom_call_target="tpu_custom_call" | custom-call | flops 301989888 | bytes 786432 | tf_op jit(solution)/shard_map/cross_in/pallas_call | solution.py:480
  148.9 14.5 %attend.3 = (bf16[4,1024,256]{2,1,0:T(8,128)(2,1)}, f32[4,1024,256]{2,1,0:T(8,128)}) custom-call(bf16[4,1024,640]{2,1,0:T(8,128)(2,1)} %cross_in.1.heads_ref, bf16[1024,128]{1,0:T(8,128)(2,1)} %select_convert_fusion.qf_ref, bf16[1024,128]{1,0:T(8,128)(2,1)} %compare_convert_fusion.kf_ref), custom_call_target="tpu_custom_call" | custom-call | flops 402653184 | bytes 720896 | tf_op jit(solution)/shard_map/attend/pallas_call | solution.py:480
  163.3 6.3 %project.3 = (f32[1024,768]{1,0:T(8,128)}, bf16[1024,768]{1,0:T(8,128)(2,1)}) custom-call(bf16[4,1024,256]{2,1,0:T(8,128)(2,1)} %get-tuple-element.106.att_ref.o_ref, bf16[8,2,2,96,1536]{4,3,2,1,0:T(8,128)(2,1)} %bitcast.232, f32[1024,768]{1,0:T(8,128)} %get-tuple-element.107.res_ref.mid_ref, f32[1,768]{1,0:T(1,128)} %get-tuple-element.356.bias_ref, ...), custom_call_target="tpu_custom_call" | custom-call | flops 100663296 | bytes 688128 | tf_op jit(solution)/shard_map/project/pallas_call | solution.py:480
  169.6 16.5 %all-gather.7.cloned.1.call-done = bf16[32,96,1536]{2,1,0:T(8,128)(2,1)} async-done(((bf16[2,96,1536]{2,1,0:T(8,128)(2,1)}), bf16[32,96,1536]{2,1,0:T(8,128)(2,1)}) %all-gather.7.cloned.1.call-update) | async-done | bytes 9437200 | tf_op jit(solution)/shard_map/all_gather | solution.py:530
  186.1 43.5 %ffn.1 = (bf16[1024,768]{1,0:T(8,128)(2,1)}, f32[1024,768]{1,0:T(8,128)}, bf16[1024,768]{1,0:T(8,128)(2,1)}, bf16[8,2,2,96,1536]{4,3,2,1,0:T(8,128)(2,1)}, f32[4...) custom-call(f32[1024,768]{1,0:T(8,128)} %get-tuple-element.108.mid_ref, ...), custom_call_target="tpu_custom_call" | custom-call | flops 1811939328 | bytes 2949120 | tf_op jit(solution)/shard_map/ffn/pallas_call | solution.py:480
  229.6 5.7 %project_back.2.do_ref = bf16[4,1024,256]{2,1,0:T(8,128)(2,1)} custom-call(bf16[1024,768]{1,0:T(8,128)(2,1)} %get-tuple-element.111.d_ref.dlow_ref, bf16[8,2,2,96,1536]{4,3,2,1,0:T(8,128)(2,1)} %bitcast.233), custom_call_target="tpu_custom_call" | custom-call | flops 100663296 | bytes 393216 | tf_op jit(solution)/shard_map/project_back/pallas_call | solution.py:480
  235.3 33.2 %attend_back.3.dh_ref = bf16[4,1024,640]{2,1,0:T(8,128)(2,1)} custom-call(bf16[4,1024,640]{2,1,0:T(8,128)(2,1)} %cross_in.1.heads_ref, bf16[4,1024,256]{2,1,0:T(8,128)(2,1)} %get-tuple-element.106.att_ref.o_ref, bf16[4,1024,256]{2,1,0:T(8,128)(2,1)} %project_back.2.do_ref, f32[4,1024,256]{2,1,0:T(8,128)} %get-tuple-element.112.lse_ref, ...), custom_call_target="tpu_custom_call" | custom-call | flops 1006632960 | bytes 1310720 | tf_op jit(solution)/shard_map/attend_back/pallas_call | solution.py:480
  268.5 20.0 %cross_back.1 = (bf16[8,2,2,96,768]{4,3,2,1,0:T(8,128)(2,1)}, f32[4,1,768]{2,1,0:T(1,128)}, f32[1024,768]{1,0:T(8,128)}, bf16[1024,768]{1,0:T(8,128)(2,1)}, f32[...) custom-call(bf16[4,1024,640]{2,1,0:T(8,128)(2,1)} %attend_back.3.dh_ref, bf16[8,2,2,96,1536]{4,3,2,1,0:T(8,128)(2,1)} %bitcast.234, ...), custom_call_target="tpu_custom_call" | custom-call | flops 603979776 | bytes 1474560 | tf_op jit(solution)/shard_map/cross_back/pallas_call | solution.py:480
  288.5 5.4 %project_back.3.do_ref = bf16[4,1024,256]{2,1,0:T(8,128)(2,1)} custom-call(bf16[1024,768]{1,0:T(8,128)(2,1)} %get-tuple-element.114.d_ref.dlow_ref, bf16[8,2,2,96,1536]{4,3,2,1,0:T(8,128)(2,1)} %bitcast.235), custom_call_target="tpu_custom_call" | custom-call | flops 100663296 | bytes 393216 | tf_op jit(solution)/shard_map/project_back/pallas_call | solution.py:480
  293.9 18.2 %attend_back.4.dh_ref = bf16[2,1024,640]{2,1,0:T(8,128)(2,1)} custom-call(bf16[4,1024,640]{2,1,0:T(8,128)(2,1)} %self_in.1.heads_ref, bf16[4,1024,256]{2,1,0:T(8,128)(2,1)} %get-tuple-element.103.att_ref.o_ref, bf16[4,1024,256]{2,1,0:T(8,128)(2,1)} %project_back.3.do_ref, f32[4,1024,256]{2,1,0:T(8,128)} %get-tuple-element.115.lse_ref, ...), custom_call_target="tpu_custom_call" | custom-call | flops 503316480 | bytes 655360 | tf_op jit(solution)/shard_map/attend_back/pallas_call | solution.py:480
  312.1 11.4 %self_back_first.1 = (bf16[8,2,1,96,768]{4,3,2,1,0:T(8,128)(2,1)}, f32[2,1,768]{2,1,0:T(1,128)}, f32[1024,768]{1,0:T(8,128)}) custom-call(bf16[2,1024,640]{2,1,0:T(8,128)(2,1)} %attend_back.4.dh_ref, bf16[8,2,2,96,1536]{4,3,2,1,0:T(8,128)(2,1)} %bitcast.236, bf16[1024,768]{1,0:T(8,128)(2,1)} %norm.2.n_ref, ...), custom_call_target="tpu_custom_call" | custom-call | flops 452984832 | bytes 1179648 | tf_op jit(solution)/shard_map/self_back_first/pallas_call | solution.py:480
  323.6 2.9 constant_dynamic-slice_fusion.6
  328.2 3.8 fusion.2
  332.0 4.0 all-to-all-start.3
  336.0 2.0 fusion.8
  338.3 18.0 %attend_back.5.dh_ref = bf16[2,1024,640]{2,1,0:T(8,128)(2,1)} custom-call(bf16[4,1024,640]{2,1,0:T(8,128)(2,1)} %self_in.1.heads_ref, bf16[4,1024,256]{2,1,0:T(8,128)(2,1)} %get-tuple-element.103.att_ref.o_ref, bf16[4,1024,256]{2,1,0:T(8,128)(2,1)} %project_back.3.do_ref, f32[4,1024,256]{2,1,0:T(8,128)} %get-tuple-element.115.lse_ref, ...), custom_call_target="tpu_custom_call" | custom-call | flops 503316480 | bytes 655360 | tf_op jit(solution)/shard_map/attend_back/pallas_call | solution.py:480
  356.4 2.3 fusion.28
  358.9 1.7 collective-permute-start.6
  360.7 2.1 collective-permute-start.7
  362.8 2.0 collective-permute-start.4
  364.8 15.9 %self_back_last.1 = (bf16[8,2,1,96,768]{4,3,2,1,0:T(8,128)(2,1)}, f32[2,1,768]{2,1,0:T(1,128)}, bf16[1024,768]{1,0:T(8,128)(2,1)}, f32[1,768]{1,0:T(1,128)}, f32[1,768]{1,0:T(1,128)}) custom-call(bf16[2,1024,640]{2,1,0:T(8,128)(2,1)} %attend_back.5.dh_ref, bf16[8,2,2,96,1536]{4,3,2,1,0:T(8,128)(2,1)} %bitcast.237, bf16[1024,768]{1,0:T(8,128)(2,1)} %norm.2.n_ref, ...), custom_call_target="tpu_custom_call" | custom-call | flops 452984832 | bytes 1474560 | tf_op jit(solution)/shard_map/self_back_last/pallas_call | solution.py:480
  380.7 2.0 fusion.32
  382.7 1.9 constant_dynamic-slice_fusion.3
  384.9 3.8 fusion.1
  390.0 3.6 all-to-all-start.4
  394.9 1.9 collective-permute-start.12
  396.8 2.0 collective-permute-start.11
  398.8 10.9 %side_back.1 = (bf16[1024,768]{1,0:T(8,128)(2,1)}, f32[1,768]{1,0:T(1,128)}, f32[1,768]{1,0:T(1,128)}) custom-call(bf16[4,1024,640]{2,1,0:T(8,128)(2,1)} %attend_back.3.dh_ref, bf16[8,2,2,96,1536]{4,3,2,1,0:T(8,128)(2,1)} %bitcast.238, bf16[1024,768]{1,0:T(8,128)(2,1)} %fusion.4.x_ref.y_ref, f32[1,768]{1,0:T(1,128)} %get-tuple-element.350.gain_ref), custom_call_target="tpu_custom_call" | custom-call | flops 301989888 | bytes 786432 | tf_op jit(solution)/shard_map/side_back/pallas_call | solution.py:480
  409.7 1.5 collect.1
  411.4 1.3 collective-permute-done.9
  413.9 3.2 collective-permute-done.10
  417.2 4.6 reduce-scatter.5.cloned.1.call-done
  421.8 1.5 fusion.25
  424.8 2.0 collective-permute-start.15
  426.8 1.3 collective-permute-start.13
  428.1 1.9 collective-permute-start.17
  430.0 3.8 fusion
  433.7 3.6 all-to-all-start.5
  441.1 1.6 collective-permute-done.14
  442.7 1.4 convert_select_fusion.4
  449.6 1.7 copy.129
  451.3 7.7 %collective-permute-done.16 = f32[24,768]{1,0:T(8,128)} collective-permute-done((f32[24,768]{1,0:T(8,128)S(1)}, f32[24,768]{1,0:T(8,128)}, u32[]{:S(2)}, u32[]{:S(2)}) %collective-permute-start.16) | collective-permute-done | bytes 73760 | tf_op jit(solution)/shard_map/ppermute | solution.py:667
  465.0 1.9 copy.127
  (210 shorter events, 36.9 us)
Async XLA Ops:
  7.2 1.6 copy-start.12
  7.2 1.7 copy-start.17
  7.2 1.8 copy-start.18
  7.2 100.8 %all-gather.5.cloned.1.call-start = ((), (), s32[]{:S(2)}) async-start(), calls=%async_computation.10 | async-start | bytes 10027008 | tf_op jit(solution)/shard_map/all_gather | solution.py:530
  7.3 1.9 copy-start.19
  9.6 10.9 %copy-start.1 = (bf16[2,2,256,768]{3,2,1,0:T(8,128)(2,1)S(1)}, bf16[2,2,256,768]{3,2,1,0:T(8,128)(2,1)}, u32[]{:S(2)}) copy-start(bf16[2,2,256,768]{3,2,1,0:T(8,128)(2,1)} %param.25) | copy-start | bytes 4718596
  9.6 10.0 %collective-permute-start.1 = (bf16[96,1536]{1,0:T(8,128)(2,1)S(1)}, bf16[96,1536]{1,0:T(8,128)(2,1)S(1)}, u32[]{:S(2)}, u32[]{:S(2)}) collective-permute-start(bf16[96,1536]{1,0:T(8,128)(2,1)S(1)} %get-tuple-element.299), channel_id=1, source_target_pairs={{0,2},{1,3},{2,0},{3,1},{4,6},{5,7},{6,4},{7,5},{8,10},{9,11},{10,... | collective-permute-start | bytes 884744 | tf_op jit(solution)/shard_map/ppermute | solution.py:527
  21.9 7.7 %copy-start.22 = (bf16[2,3,192]{2,0,1:T(2,128)(2,1)S(1)}, bf16[2,3,192]{2,0,1:T(2,128)(2,1)}, u32[]{:S(2)}) copy-start(bf16[2,3,192]{2,0,1:T(2,128)(2,1)} %param.31) | copy-start | bytes 6916
  21.9 7.7 %copy-start.20 = (bf16[2,2,192]{2,1,0:T(2,128)(2,1)S(1)}, bf16[2,2,192]{2,1,0:T(2,128)(2,1)}, u32[]{:S(2)}) copy-start(bf16[2,2,192]{2,1,0:T(2,128)(2,1)} %param.41) | copy-start | bytes 4612
  21.9 7.7 %copy-start.35 = (s32[2,1,3]{2,1,0:T(1,128)S(1)}, s32[2,1,3]{2,1,0:T(1,128)}, u32[]{:S(2)}) copy-start(s32[2,1,3]{2,1,0:T(1,128)} %param.27) | copy-start | bytes 76
  21.9 8.0 %copy-start.21 = (bf16[2,768]{1,0:T(2,128)(2,1)S(1)}, bf16[2,768]{1,0:T(2,128)(2,1)}, u32[]{:S(2)}) copy-start(bf16[2,768]{1,0:T(2,128)(2,1)} %param.47) | copy-start | bytes 9220
  21.9 8.0 %copy-start.34 = (bf16[2,192]{1,0:T(2,128)(2,1)S(1)}, bf16[2,192]{1,0:T(2,128)(2,1)}, u32[]{:S(2)}) copy-start(bf16[2,192]{1,0:T(2,128)(2,1)} %param.39) | copy-start | bytes 2308
  21.9 9.4 %copy-start.23 = (bf16[2,768]{1,0:T(2,128)(2,1)S(1)}, bf16[2,768]{1,0:T(2,128)(2,1)}, u32[]{:S(2)}) copy-start(bf16[2,768]{1,0:T(2,128)(2,1)} %param.28) | copy-start | bytes 9220
  21.9 9.4 %copy-start.24 = (bf16[2,768]{1,0:T(2,128)(2,1)S(1)}, bf16[2,768]{1,0:T(2,128)(2,1)}, u32[]{:S(2)}) copy-start(bf16[2,768]{1,0:T(2,128)(2,1)} %param.36) | copy-start | bytes 9220
  22.0 10.0 %copy-start.25 = (bf16[2,768]{1,0:T(2,128)(2,1)S(1)}, bf16[2,768]{1,0:T(2,128)(2,1)}, u32[]{:S(2)}) copy-start(bf16[2,768]{1,0:T(2,128)(2,1)} %param.29) | copy-start | bytes 9220
  22.0 10.0 %copy-start.26 = (bf16[2,768]{1,0:T(2,128)(2,1)S(1)}, bf16[2,768]{1,0:T(2,128)(2,1)}, u32[]{:S(2)}) copy-start(bf16[2,768]{1,0:T(2,128)(2,1)} %param.37) | copy-start | bytes 9220
  22.0 24.2 %all-to-all-start.1 = ((bf16[4,256,768]{2,1,0:T(8,128)(2,1)}), bf16[4,256,768]{2,1,0:T(8,128)(2,1)S(1)}, u32[]{:S(2)}, u32[]{:S(2)}) async-start(bf16[4,256,768]{2,1,0:T(8,128)(2,1)} %bitcast.14), calls=%async_computation.1 | async-start | bytes 3145728 | tf_op jit(solution)/shard_map/all_to_all | solution.py:546
  27.6 28.9 %collective-permute-start = (bf16[96,1536]{1,0:T(8,128)(2,1)}, bf16[96,1536]{1,0:T(8,128)(2,1)}, u32[]{:S(2)}, u32[]{:S(2)}) collective-permute-start(bf16[96,1536]{1,0:T(8,128)(2,1)} %get-tuple-element.301), channel_id=1, source_target_pairs={{0,2},{1,3},{2,0},{3,1},{4,6},{5,7},{6,4},{7,5},{8,10},{9,11},{10,... | collective-permute-start | bytes 884744 | tf_op jit(solution)/shard_map/ppermute | solution.py:527
  46.2 24.1 %all-to-all-start = ((bf16[4,259,768]{2,1,0:T(8,128)(2,1)}), bf16[4,259,768]{2,1,0:T(8,128)(2,1)S(1)}, u32[]{:S(2)}, u32[]{:S(2)}) async-start(bf16[4,259,768]{2,1,0:T(8,128)(2,1)} %bitcast.9), calls=%async_computation | async-start | bytes 3244032 | tf_op jit(solution)/shard_map/all_to_all | solution.py:545
  49.8 136.3 %all-gather.7.cloned.1.call-start = ((), (), s32[]{:S(2)}) async-start(), calls=%async_computation.11 | async-start | bytes 10027008 | tf_op jit(solution)/shard_map/all_gather | solution.py:530
  74.2 4.3 copy-start.2
  79.8 4.0 copy-start.27
  79.8 4.6 copy-start.28
  79.8 5.2 %copy-start.29 = (bf16[2,768]{1,0:T(2,128)(2,1)S(1)}, bf16[2,768]{1,0:T(2,128)(2,1)}, u32[]{:S(2)}) copy-start(bf16[2,768]{1,0:T(2,128)(2,1)} %param.49) | copy-start | bytes 9220
  79.8 5.8 %copy-start.30 = (bf16[2,768]{1,0:T(2,128)(2,1)S(1)}, bf16[2,768]{1,0:T(2,128)(2,1)}, u32[]{:S(2)}) copy-start(bf16[2,768]{1,0:T(2,128)(2,1)} %param.33) | copy-start | bytes 9220
  79.8 5.8 %copy-start.31 = (bf16[2,768]{1,0:T(2,128)(2,1)S(1)}, bf16[2,768]{1,0:T(2,128)(2,1)}, u32[]{:S(2)}) copy-start(bf16[2,768]{1,0:T(2,128)(2,1)} %param.34) | copy-start | bytes 9220
  79.8 6.4 %copy-start.32 = (bf16[2,768]{1,0:T(2,128)(2,1)S(1)}, bf16[2,768]{1,0:T(2,128)(2,1)}, u32[]{:S(2)}) copy-start(bf16[2,768]{1,0:T(2,128)(2,1)} %param.35) | copy-start | bytes 9220
  79.8 6.4 %copy-start.33 = (bf16[2,768]{1,0:T(2,128)(2,1)S(1)}, bf16[2,768]{1,0:T(2,128)(2,1)}, u32[]{:S(2)}) copy-start(bf16[2,768]{1,0:T(2,128)(2,1)} %param.43) | copy-start | bytes 9220
  79.9 23.8 %all-to-all-start.2 = ((bf16[4,256,768]{2,1,0:T(8,128)(2,1)}), bf16[4,256,768]{2,1,0:T(8,128)(2,1)S(1)}, u32[]{:S(2)}, u32[]{:S(2)}) async-start(bf16[4,256,768]{2,1,0:T(8,128)(2,1)} %bitcast.31), calls=%async_computation.2 | async-start | bytes 3145728 | tf_op jit(solution)/shard_map/all_to_all | solution.py:547
  83.6 272.8 %reduce-scatter.3.cloned.1.call-start = ((), (), s32[]{:S(2)}) async-start(), calls=%async_computation.8 | async-start | bytes 10027008 | tf_op jit(solution)/shard_map/reduce_scatter | solution.py:628
  229.6 192.2 %reduce-scatter.5.cloned.1.call-start = ((), (), s32[]{:S(2)}) async-start(), calls=%async_computation.9 | async-start | bytes 5013504 | tf_op jit(solution)/shard_map/reduce_scatter | solution.py:628
  323.5 4.7 copy-start.4
  326.5 5.5 %collective-permute-start.2 = (bf16[8,1,96,768]{3,2,0,1:T(8,128)(2,1)}, bf16[8,1,96,768]{3,2,0,1:T(8,128)(2,1)}, u32[]{:S(2)}, u32[]{:S(2)}) collective-permute-start(bf16[8,1,96,768]{3,2,0,1:T(8,128)(2,1)} %get-tuple-element.283), channel_id=1, source_target_pairs={{0,1},{1,0},{2,3},{3,2},{4,5},{5,4},{6,7},{7,6},{8,9},{9,8},{10,11... | collective-permute-start | bytes 3538952 | tf_op jit(solution)/shard_map/ppermute | solution.py:649
  332.0 24.4 %all-to-all-start.3 = ((bf16[4,256,768]{2,1,0:T(8,128)(2,1)}), bf16[4,256,768]{2,1,0:T(8,128)(2,1)S(1)}, u32[]{:S(2)}, u32[]{:S(2)}) async-start(bf16[4,256,768]{2,1,0:T(8,128)(2,1)} %bitcast.37), calls=%async_computation.4 | async-start | bytes 3145728 | tf_op jit(solution)/shard_map/all_to_all | solution.py:727
  338.0 18.4 %collective-permute-start.3 = (bf16[4,1,96,768]{3,2,1,0:T(8,128)(2,1)}, bf16[4,1,96,768]{3,2,1,0:T(8,128)(2,1)}, u32[]{:S(2)}, u32[]{:S(2)}) collective-permute-start(bf16[4,1,96,768]{3,2,1,0:T(8,128)(2,1)} %fusion.8), channel_id=1, source_target_pairs={{0,4},{4,0},{8,12},{12,8},{16,20},{20,16},{24,28},{28,24},{1,5},{5... | collective-permute-start | bytes 1769480 | tf_op jit(solution)/shard_map/ppermute | solution.py:649
  356.4 6.3 %copy-start.8 = (bf16[1,2,96,1536]{3,2,1,0:T(8,128)(2,1)S(1)}, bf16[1,2,96,1536]{3,2,1,0:T(8,128)(2,1)}, u32[]{:S(2)}) copy-start(bf16[1,2,96,1536]{3,2,1,0:T(8,128)(2,1)} %reduce-scatter.3.cloned.1.call-done) | copy-start | bytes 1769476
  358.7 22.0 %collective-permute-start.5 = (bf16[1,96,768]{2,1,0:T(8,128)(2,1)}, bf16[1,96,768]{2,1,0:T(8,128)(2,1)}, u32[]{:S(2)}, u32[]{:S(2)}) collective-permute-start(bf16[1,96,768]{2,1,0:T(8,128)(2,1)} %get-tuple-element.277), channel_id=1, source_target_pairs={{0,8},{4,12},{8,16},{12,20},{16,24},{20,28},{24,0},{28,4},{1,9},{5... | collective-permute-start | bytes 442376 | tf_op jit(solution)/shard_map/ppermute | solution.py:663
  358.9 21.7 %collective-permute-start.6 = (bf16[1,96,768]{2,1,0:T(8,128)(2,1)}, bf16[1,96,768]{2,1,0:T(8,128)(2,1)}, u32[]{:S(2)}, u32[]{:S(2)}) collective-permute-start(bf16[1,96,768]{2,1,0:T(8,128)(2,1)} %get-tuple-element.279), channel_id=1, source_target_pairs={{0,16},{4,20},{8,24},{12,28},{16,0},{20,4},{24,8},{28,12},{1,17},{... | collective-permute-start | bytes 442376 | tf_op jit(solution)/shard_map/ppermute | solution.py:663
  360.7 20.0 %collective-permute-start.7 = (bf16[1,96,768]{2,1,0:T(8,128)(2,1)}, bf16[1,96,768]{2,1,0:T(8,128)(2,1)}, u32[]{:S(2)}, u32[]{:S(2)}) collective-permute-start(bf16[1,96,768]{2,1,0:T(8,128)(2,1)} %get-tuple-element.278), channel_id=1, source_target_pairs={{0,24},{4,28},{8,0},{12,4},{16,8},{20,12},{24,16},{28,20},{1,25},{... | collective-permute-start | bytes 442376 | tf_op jit(solution)/shard_map/ppermute | solution.py:663
  362.8 19.9 %collective-permute-start.4 = (bf16[96,1536]{1,0:T(8,128)(2,1)S(1)}, bf16[96,1536]{1,0:T(8,128)(2,1)S(1)}, u32[]{:S(2)}, u32[]{:S(2)}) collective-permute-start(bf16[96,1536]{1,0:T(8,128)(2,1)S(1)} %slice_bitcast_fusion), channel_id=1, source_target_pairs={{0,2},{1,3},{2,0},{3,1},{4,6},{5,7},{6,4},{7,5},{8,10},{9,11},{10,... | collective-permute-start | bytes 884744 | tf_op jit(solution)/shard_map/ppermute | solution.py:667
  382.7 1.9 copy-start.14
  382.7 2.2 copy-start.5
  384.6 4.0 copy-start
  384.7 4.0 collective-permute-start.8
  388.7 1.3 copy-start.6
  390.0 31.8 %all-to-all-start.4 = ((bf16[4,256,768]{2,1,0:T(8,128)(2,1)}), bf16[4,256,768]{2,1,0:T(8,128)(2,1)S(1)}, u32[]{:S(2)}, u32[]{:S(2)}) async-start(bf16[4,256,768]{2,1,0:T(8,128)(2,1)} %bitcast.246), calls=%async_computation.5 | async-start | bytes 3145728 | tf_op jit(solution)/shard_map/all_to_all | solution.py:727
  393.6 1.3 copy-start.16
  394.9 26.9 %collective-permute-start.12 = (bf16[1,96,768]{2,1,0:T(8,128)(2,1)S(1)}, bf16[1,96,768]{2,1,0:T(8,128)(2,1)S(1)}, u32[]{:S(2)}, u32[]{:S(2)}) collective-permute-start(bf16[1,96,768]{2,1,0:T(8,128)(2,1)S(1)} %copy-done.16), channel_id=1, source_target_pairs={{0,2},{1,3},{2,0},{3,1},{4,6},{5,7},{6,4},{7,5},{8,10},{9,11},{10,... | collective-permute-start | bytes 442376 | tf_op jit(solution)/shard_map/ppermute | solution.py:667
  396.8 14.5 %copy-start.9 = (bf16[1,2,96,1536]{3,2,1,0:T(8,128)(2,1)S(1)}, bf16[1,2,96,1536]{3,2,1,0:T(8,128)(2,1)}, u32[]{:S(2)}) copy-start(bf16[1,2,96,1536]{3,2,1,0:T(8,128)(2,1)} %reduce-scatter.3.cloned.1.call-done) | copy-start | bytes 1769476
  396.8 14.5 %copy-start.15 = (bf16[96,1536]{1,0:T(8,128)(2,1)S(1)}, bf16[96,1536]{1,0:T(8,128)(2,1)}, u32[]{:S(2)}) copy-start(bf16[96,1536]{1,0:T(8,128)(2,1)} %copy-done.14) | copy-start | bytes 884740
  396.8 20.4 %collective-permute-start.11 = (bf16[4,1,96,768]{3,2,1,0:T(8,128)(2,1)}, bf16[4,1,96,768]{3,2,1,0:T(8,128)(2,1)S(1)}, u32[]{:S(2)}, u32[]{:S(2)}) collective-permute-start(bf16[4,1,96,768]{3,2,1,0:T(8,128)(2,1)} %bitcast.57), channel_id=1, source_target_pairs={{0,4},{4,0},{8,12},{12,8},{16,20},{20,16},{24,28},{28,24},{1,5},{5... | collective-permute-start | bytes 1769480 | tf_op jit(solution)/shard_map/ppermute | solution.py:753
  411.2 1.5 copy-start.11
  411.2 1.5 collective-permute-start.9
  412.7 4.4 collective-permute-start.10
  417.2 10.9 %copy-start.7 = (bf16[4,1,96,768]{3,2,1,0:T(8,128)(2,1)}, bf16[4,1,96,768]{3,2,1,0:T(8,128)(2,1)S(1)}, u32[]{:S(2)}) copy-start(bf16[4,1,96,768]{3,2,1,0:T(8,128)(2,1)S(1)} %collective-permute-done.11) | copy-start | bytes 1769476
  421.8 6.3 %copy-start.13 = (bf16[1,2,96,768]{3,2,1,0:T(8,128)(2,1)S(1)}, bf16[1,2,96,768]{3,2,1,0:T(8,128)(2,1)}, u32[]{:S(2)}) copy-start(bf16[1,2,96,768]{3,2,1,0:T(8,128)(2,1)} %reduce-scatter.5.cloned.1.call-done) | copy-start | bytes 884740
  421.8 8.2 %copy-start.3 = (bf16[1024,768]{1,0:T(8,128)(2,1)S(1)}, bf16[1024,768]{1,0:T(8,128)(2,1)}, u32[]{:S(2)}) copy-start(bf16[1024,768]{1,0:T(8,128)(2,1)} %get-tuple-element.165) | copy-start | bytes 4718596
  424.8 16.3 %collective-permute-start.15 = (bf16[120,768]{1,0:T(8,128)(2,1)}, bf16[120,768]{1,0:T(8,128)(2,1)}, u32[]{:S(2)}, u32[]{:S(2)}) collective-permute-start(bf16[120,768]{1,0:T(8,128)(2,1)} %get-tuple-element.335), channel_id=1, source_target_pairs={{0,24},{4,28},{8,0},{12,4},{16,8},{20,12},{24,16},{28,20},{1,25},{... | collective-permute-start | bytes 552968 | tf_op jit(solution)/shard_map/ppermute | solution.py:781
  426.8 16.0 %collective-permute-start.14 = (bf16[120,768]{1,0:T(8,128)(2,1)}, bf16[120,768]{1,0:T(8,128)(2,1)}, u32[]{:S(2)}, u32[]{:S(2)}) collective-permute-start(bf16[120,768]{1,0:T(8,128)(2,1)} %get-tuple-element.334), channel_id=1, source_target_pairs={{0,16},{4,20},{8,24},{12,28},{16,0},{20,4},{24,8},{28,12},{1,17},{... | collective-permute-start | bytes 552968 | tf_op jit(solution)/shard_map/ppermute | solution.py:781
  426.8 16.0 %collective-permute-start.13 = (bf16[120,768]{1,0:T(8,128)(2,1)}, bf16[120,768]{1,0:T(8,128)(2,1)}, u32[]{:S(2)}, u32[]{:S(2)}) collective-permute-start(bf16[120,768]{1,0:T(8,128)(2,1)} %get-tuple-element.333), channel_id=1, source_target_pairs={{0,8},{4,12},{8,16},{12,20},{16,24},{20,28},{24,0},{28,4},{1,9},{5... | collective-permute-start | bytes 552968 | tf_op jit(solution)/shard_map/ppermute | solution.py:781
  428.1 9.2 %collective-permute-start.17 = (bf16[96,768]{1,0:T(8,128)(2,1)S(1)}, bf16[96,768]{1,0:T(8,128)(2,1)}, u32[]{:S(2)}, u32[]{:S(2)}) collective-permute-start(bf16[96,768]{1,0:T(8,128)(2,1)S(1)} %slice_bitcast_fusion.1), channel_id=1, source_target_pairs={{0,2},{1,3},{2,0},{3,1},{4,6},{5,7},{6,4},{7,5},{8,10},{9,11},{10,... | collective-permute-start | bytes 442376 | tf_op jit(solution)/shard_map/ppermute | solution.py:667
  433.7 30.9 %all-to-all-start.5 = ((bf16[4,256,768]{2,1,0:T(8,128)(2,1)}), bf16[4,256,768]{2,1,0:T(8,128)(2,1)S(1)}, u32[]{:S(2)}, u32[]{:S(2)}) async-start(bf16[4,256,768]{2,1,0:T(8,128)(2,1)} %bitcast.248), calls=%async_computation.7 | async-start | bytes 3145728 | tf_op jit(solution)/shard_map/all_to_all | solution.py:727
  444.1 2.5 copy-start.10
  446.7 12.4 %collective-permute-start.16 = (f32[24,768]{1,0:T(8,128)S(1)}, f32[24,768]{1,0:T(8,128)}, u32[]{:S(2)}, u32[]{:S(2)}) collective-permute-start(f32[24,768]{1,0:T(8,128)S(1)} %fusion.105), channel_id=1, source_target_pairs={{0,2},{1,3},{2,0},{3,1},{4,6},{5,7},{6,4},{7,5},{8,10},{9,11},{10,... | collective-permute-start | bytes 221192 | tf_op jit(solution)/shard_map/ppermute | solution.py:667
Sparse Core Ops, SparseCore 0:
  20.7 82.8 all-gather.4
  106.5 79.5 all-gather.6
  229.7 109.4 reduce-scatter.2
  343.4 78.3 reduce-scatter.4

commit v4 on v3

--- a/solution.py
+++ b/solution.py
@@ -413,13 +413,36 @@
     self_back_part(dh_ref, w_ref, n_ref, dlow_ref, att_ref, dw_ref, dbias_ref, acc_ref)
 
 
-def self_back_last_kernel(dh_ref, w_ref, n_ref, dlow_ref, att_ref, x_ref, dmid_ref, before_ref, gain_ref,
-                          dw_ref, dbias_ref, own_ref, dg_ref, ds_ref, acc_ref):
-    j = pl.program_id(0)
+def self_weight_kernel(dh_ref, n_ref, dlow_ref, att_ref, dw_ref):
+    def weight(i, at, c):
+        dqkv = t_mm(n_ref[:, at], dh_ref[0])
+        do = t_mm(dlow_ref[:, at], att_ref[0])
+        put_rows(dw_ref, i, dqkv[:, : 4 * PAIR], slice(0, 4 * PAIR))
+        put_rows(dw_ref, i, dqkv[:, 4 * PAIR :] + do[:, :PAIR], slice(4 * PAIR, 5 * PAIR))
+        put_rows(dw_ref, i, do[:, PAIR:], slice(5 * PAIR, 6 * PAIR))
+
+    each(n_ref.shape[1], PART, weight)
+
+
+def self_rows_part(dh_ref, w_ref, dbias_ref, acc_ref):
+    rows = acc_ref.shape[0]
+    w = matrix(w_ref, 0, 5 * PAIR)
+    clear(acc_ref)
+
+    def one(i, at, total):
+        d = dh_ref[0, at, :]
+        acc_ref[at, :] += mm_t(d, w)
+        return total + col_sum(d.astype(F32))
+
+    dbias_ref[0, :, : 5 * PAIR] = each(rows, TALL, one, jnp.zeros((1, 5 * PAIR), F32))
+    dbias_ref[0, :, 5 * PAIR :] = jnp.zeros((1, PAIR), F32)
+
+
+def self_rows_last_kernel(dh_ref, w_ref, x_ref, dmid_ref, before_ref, gain_ref, dbias_ref, own_ref, dg_ref, ds_ref, acc_ref):
     rows, width = x_ref.shape
-    self_back_part(dh_ref, w_ref, n_ref, dlow_ref, att_ref, dw_ref, dbias_ref, acc_ref)
-
-    @pl.when(j == pl.num_programs(0) - 1)
+    self_rows_part(dh_ref, w_ref, dbias_ref, acc_ref)
+
+    @pl.when(pl.program_id(0) == pl.num_programs(0) - 1)
     def _():
         def last(i, at, sums):
             back, dg, ds = norm_back(acc_ref[at, :] + before_ref[at, :], x_ref[at, :].astype(F32), gain_ref[...])
@@ -715,19 +738,25 @@
     dw_part_spec = pl.BlockSpec((blocks, 1, 1, deep, 6 * PAIR), lambda j: (0, j, 0, 0, 0))
     bias_part = sds((batches, 1, 6 * PAIR), F32)
 
-    def self_back(t, dh, *more):
+    def self_back_first(t, dh):
         ins = steps(dh) + [(w_att, weight_block(w_att, 6 * PAIR, 0, t))] + given(n1, d_branch) + [(att, per_step(att, t))]
         outs = [(dw_part, dw_part_spec), (bias_part, per_step(bias_part))]
-        if more:
-            return call(self_back_last_kernel, "self_back_last", batches, ins + given(*more), outs + full(low, line, line),
-                        [pltpu.VMEM((rows, width), F32)], flops=1.5 * gemm, moved=rows * width * 30)
         return call(self_back_first_kernel, "self_back_first", batches, ins, outs + full(high), flops=1.5 * gemm, moved=rows * width * 24)
+
+    def self_weight(t, dh):
+        ins = steps(dh) + given(n1, d_branch) + [(att, per_step(att, t))]
+        return call(self_weight_kernel, "self_weight", batches, ins, [(dw_part, dw_part_spec)], flops=gemm, moved=rows * width * 16)[0]
+
+    def self_rows(t, dh, *more):
+        ins = steps(dh) + [(w_att, weight_block(w_att, 6 * PAIR, 0, t))] + given(*more)
+        return call(self_rows_last_kernel, "self_rows", batches, ins, [(bias_part, per_step(bias_part))] + full(low, line, line),
+                    [pltpu.VMEM((rows, width), F32)], flops=gemm / 2, moved=rows * width * 20)
 
     def home(a):
         return lax.all_to_all(a.reshape(members, local, width), "mp", 0, 0, tiled=True).reshape(2, batches, local, width)
 
     d_h1 = attend_back(hs, att, d_att, lse, 1)
-    dw_self1, d_selfb1, acc = self_back(1, d_h1)
+    dw_self1, d_selfb1, acc = self_back_first(1, d_h1)
     d_att, acc, dw_self1 = lax.optimization_barrier((d_att, acc, dw_self1))
     output = from_row(output, rows - first)
     if by_hand:
@@ -740,19 +769,27 @@
     their_ffn = to_partner(total_ffn[1])
     if by_hand:
         d_h0, got = lax.optimization_barrier((d_h0, self1[2]))
-        total1 = over_z(self1[:2] + [got])
-    dw_self0, d_selfb0, own, gg1, gs1 = self_back(0, d_h0, x, d_mid, acc, g1)
+        self1 = self1[:2] + [got]
+
+        def z_hop(s):
+            send = added([pick(t, (z_place + s) % lines, 0) for t in self1]).astype(BF)
+            return lax.ppermute(send, "dp", [(i, (i + 2 * s) % n_dp) for i in range(n_dp)])
+
+        near = z_hop(1)
+    dw_self0 = self_weight(0, d_h0)
     if by_hand:
-        own, dw_self0, gg1, their_ffn, total1 = lax.optimization_barrier((own, dw_self0, gg1, their_ffn, total1))
+        dw_self0, d_h0, near = lax.optimization_barrier((dw_self0, d_h0, near))
         self0 = over_cores(by_owner(dw_self0))
-        own = from_row(own, rows - first)
-        own, got, gg1 = lax.optimization_barrier((own, self0[1], gg1))
+        far = [z_hop(s) for s in range(2, lines)]
+    d_selfb0, own, gg1, gs1 = self_rows(0, d_h0, x, d_mid, acc, g1)
+    if by_hand:
+        own, gg1, their_ffn, got, *far = lax.optimization_barrier((own, gg1, their_ffn, self0[1], *far))
+        total1 = added([pick(t, z_place, 0) for t in self1] + [near] + far).astype(BF)
         self0 = [t.reshape((lines, 2) + t.shape[1:]) for t in (self0[0], got)]
         send = added([pick(t, 1 - x_place, 1) for t in self0]).astype(BF)
         own, send, d_hc = lax.optimization_barrier((own, send, d_hc))
         self0 = [pick(t, x_place, 1) for t in self0] + [lax.ppermute(send, "dp", x_pairs)]
-    else:
-        own = from_row(own, rows - first)
+    own = from_row(own, rows - first)
     got_own = home(own)
     other, ggy, gsy = side_back(d_hc)
     if by_hand:

time: 483 us -> 489 us (1.012)
    pallas_call x19 -> x20, Pallas kernels: 254 us -> 256 us  [call(): pl.pallas_call(kernel, grid=(steps,), in_specs=[s for _, s in ins], out_s...]
    unnamed x85 -> x83, local copies, waits for them, and re-layouts: 10.4 us -> 10 us
  transfers between devices with their start and end apart: 28 -> 28, of which waited for: 10 -> 13; matrix products, arithmetic and copies ran while one was open for 16% -> 16% of each run, Pallas kernels for 44% -> 44%
where the time goes in v4:
time: 489 us; the launch traced here: 480 us
  Pallas kernels  256 us (52%)
  waiting for transfers between devices  77.1 us (16%)
  other arithmetic  63.5 us (13%)
  starting transfers between devices  45.1 us (9%)
  local copies, waits for them, and re-layouts  20 us (4%)
  between operations  18.2 us (4%)
    pallas_call x20, Pallas kernels, call(): pl.pallas_call(kernel, grid=(steps,), in_specs=[s for _, s in ins], out_s...  256 us
    concatenate x6, other arithmetic, from_row(): return lax.dynamic_slice_in_dim(jnp.concatenate([a, a], 0), at, rows, 0)  22.5 us
    all_to_all x1, waiting for transfers between devices, body(): lax.all_to_all(cotangent.swapaxes(0, 1).reshape(members, local, width), '...  16.8 us
    all_gather x2, waiting for transfers between devices, gather(): lax.all_gather(pair, both, axis=0, axis_index_groups=groups)  16.4 us
    all_to_all x1, waiting for transfers between devices, body(): lax.all_to_all(by_view[::-1].reshape(members, local, width), 'mp', 0, 0,...  11.4 us
    all_to_all x3, starting transfers between devices, home(): lax.all_to_all(a.reshape(members, local, width), 'mp', 0, 0, tiled=True)  11.1 us
    unnamed x83, local copies, waits for them, and re-layouts  10 us
  transfers between devices with their start and end apart: 28, of which 13 were waited for; matrix products, arithmetic and copies ran while one was open for 16% of the time, Pallas kernels for 44%

profile of v4, /device:TPU:0, one launch (start us, length us, event | category | flops | bytes accessed | tf_op | source)
XLA Modules:
  0.0 480.2 jit_solution(8307895748121814624)
XLA Ops:
  7.3 1.5 fusion.102
  9.6 3.0 collective-permute-start.1
  12.6 7.0 %collective-permute-done.1 = bf16[96,1536]{1,0:T(8,128)(2,1)S(1)} collective-permute-done((bf16[96,1536]{1,0:T(8,128)(2,1)S(1)}, bf16[96,1536]{1,0:T(8,128)(2,1)S(1)}, u32[]{:S(2)}, u32[]{:S(2)}) %collective-permute-start.1) | collective-permute-done | bytes 294944 | tf_op jit(solution)/shard_map/ppermute | solution.py:550
  22.0 3.7 all-to-all-start.1
  25.7 1.9 fusion.18
  27.6 2.0 collective-permute-start
  34.8 11.4 %all-to-all-done.1 = bf16[4,256,768]{2,1,0:T(8,128)(2,1)S(1)} async-done(((bf16[4,256,768]{2,1,0:T(8,128)(2,1)}), bf16[4,256,768]{2,1,0:T(8,128)(2,1)S(1)}, u32[]{:S(2)}, u32[]{:S(2)}) %all-to-all-start.1) | async-done | bytes 1572896 | tf_op jit(solution)/shard_map/all_to_all | solution.py:569
  46.2 3.6 all-to-all-start
  53.4 3.1 fusion.12
  56.4 1.8 pad_maximum_fusion.2
  58.3 3.8 fusion.4.x_ref.y_ref
  62.0 4.1 norm.3.side_ref
  66.2 4.2 all-to-all-done
  70.5 3.8 fusion.5.x_ref.res_ref
  74.2 4.3 norm.2.n_ref
  79.8 3.7 all-to-all-start.2
  86.8 16.8 %all-to-all-done.2 = bf16[4,256,768]{2,1,0:T(8,128)(2,1)S(1)} async-done(((bf16[4,256,768]{2,1,0:T(8,128)(2,1)}), bf16[4,256,768]{2,1,0:T(8,128)(2,1)S(1)}, u32[]{:S(2)}, u32[]{:S(2)}) %all-to-all-start.2) | async-done | bytes 1572896 | tf_op jit(solution)/shard_map/all_to_all | solution.py:570
  103.6 3.7 fusion.3.dz_ref
  108.0 9.5 %self_in.1.heads_ref = bf16[4,1024,640]{2,1,0:T(8,128)(2,1)} custom-call(bf16[1024,768]{1,0:T(8,128)(2,1)} %norm.2.n_ref, bf16[8,2,2,96,1536]{4,3,2,1,0:T(8,128)(2,1)} %bitcast.229, f32[4,1,768]{2,1,0:T(1,128)} %get-tuple-element.332.bias_ref, f32[1024,128]{1,0:T(8,128)} %get-tuple-element.99.cos_ref, f32[1024,128]{1,0:T(8,128)} %get-tuple-element.100.sin_ref), custom_call_target="tpu_custom_call" | custom-call | flops 301989888 | bytes 786432 | tf_op jit(solution)/shard_map/self_in/pallas_call | solution.py:503
  117.5 14.5 %attend.2 = (bf16[4,1024,256]{2,1,0:T(8,128)(2,1)}, f32[4,1024,256]{2,1,0:T(8,128)}) custom-call(bf16[4,1024,640]{2,1,0:T(8,128)(2,1)} %self_in.1.heads_ref, bf16[1024,128]{1,0:T(8,128)(2,1)} %select_convert_fusion.qf_ref, bf16[1024,128]{1,0:T(8,128)(2,1)} %compare_convert_fusion.kf_ref), custom_call_target="tpu_custom_call" | custom-call | flops 402653184 | bytes 720896 | tf_op jit(solution)/shard_map/attend/pallas_call | solution.py:503
  132.0 6.1 %project.2 = (f32[1024,768]{1,0:T(8,128)}, bf16[1024,768]{1,0:T(8,128)(2,1)}) custom-call(bf16[4,1024,256]{2,1,0:T(8,128)(2,1)} %get-tuple-element.103.att_ref.o_ref, bf16[8,2,2,96,1536]{4,3,2,1,0:T(8,128)(2,1)} %bitcast.230, bf16[1024,768]{1,0:T(8,128)(2,1)} %fusion.5.x_ref.res_ref, f32[1,768]{1,0:T(1,128)} %get-tuple-element.353.bias_ref, ...), custom_call_target="tpu_custom_call" | custom-call | flops 100663296 | bytes 688128 | tf_op jit(solution)/shard_map/project/pallas_call | solution.py:503
  138.0 10.8 %cross_in.1.heads_ref = bf16[4,1024,640]{2,1,0:T(8,128)(2,1)} custom-call(bf16[1024,768]{1,0:T(8,128)(2,1)} %get-tuple-element.104.n_ref, bf16[1024,768]{1,0:T(8,128)(2,1)} %norm.3.side_ref, bf16[8,2,2,96,1536]{4,3,2,1,0:T(8,128)(2,1)} %bitcast.231, f32[4,1,768]{2,1,0:T(1,128)} %get-tuple-element.331.bias_ref, f32[1024,128]{1,0:T(8,128)} %get-tuple-element.99.cos_ref, ...), custom_call_target="tpu_custom_call" | custom-call | flops 301989888 | bytes 786432 | tf_op jit(solution)/shard_map/cross_in/pallas_call | solution.py:503
  148.8 14.5 %attend.3 = (bf16[4,1024,256]{2,1,0:T(8,128)(2,1)}, f32[4,1024,256]{2,1,0:T(8,128)}) custom-call(bf16[4,1024,640]{2,1,0:T(8,128)(2,1)} %cross_in.1.heads_ref, bf16[1024,128]{1,0:T(8,128)(2,1)} %select_convert_fusion.qf_ref, bf16[1024,128]{1,0:T(8,128)(2,1)} %compare_convert_fusion.kf_ref), custom_call_target="tpu_custom_call" | custom-call | flops 402653184 | bytes 720896 | tf_op jit(solution)/shard_map/attend/pallas_call | solution.py:503
  163.3 6.3 %project.3 = (f32[1024,768]{1,0:T(8,128)}, bf16[1024,768]{1,0:T(8,128)(2,1)}) custom-call(bf16[4,1024,256]{2,1,0:T(8,128)(2,1)} %get-tuple-element.106.att_ref.o_ref, bf16[8,2,2,96,1536]{4,3,2,1,0:T(8,128)(2,1)} %bitcast.232, f32[1024,768]{1,0:T(8,128)} %get-tuple-element.107.res_ref.mid_ref, f32[1,768]{1,0:T(1,128)} %get-tuple-element.356.bias_ref, ...), custom_call_target="tpu_custom_call" | custom-call | flops 100663296 | bytes 688128 | tf_op jit(solution)/shard_map/project/pallas_call | solution.py:503
  169.6 16.4 %all-gather.7.cloned.1.call-done = bf16[32,96,1536]{2,1,0:T(8,128)(2,1)} async-done(((bf16[2,96,1536]{2,1,0:T(8,128)(2,1)}), bf16[32,96,1536]{2,1,0:T(8,128)(2,1)}) %all-gather.7.cloned.1.call-update) | async-done | bytes 9437200 | tf_op jit(solution)/shard_map/all_gather | solution.py:553
  186.1 43.5 %ffn.1 = (bf16[1024,768]{1,0:T(8,128)(2,1)}, f32[1024,768]{1,0:T(8,128)}, bf16[1024,768]{1,0:T(8,128)(2,1)}, bf16[8,2,2,96,1536]{4,3,2,1,0:T(8,128)(2,1)}, f32[4...) custom-call(f32[1024,768]{1,0:T(8,128)} %get-tuple-element.108.mid_ref, ...), custom_call_target="tpu_custom_call" | custom-call | flops 1811939328 | bytes 2949120 | tf_op jit(solution)/shard_map/ffn/pallas_call | solution.py:503
  229.6 5.7 %project_back.2.do_ref = bf16[4,1024,256]{2,1,0:T(8,128)(2,1)} custom-call(bf16[1024,768]{1,0:T(8,128)(2,1)} %get-tuple-element.111.d_ref.dlow_ref, bf16[8,2,2,96,1536]{4,3,2,1,0:T(8,128)(2,1)} %bitcast.233), custom_call_target="tpu_custom_call" | custom-call | flops 100663296 | bytes 393216 | tf_op jit(solution)/shard_map/project_back/pallas_call | solution.py:503
  235.3 33.2 %attend_back.3.dh_ref = bf16[4,1024,640]{2,1,0:T(8,128)(2,1)} custom-call(bf16[4,1024,640]{2,1,0:T(8,128)(2,1)} %cross_in.1.heads_ref, bf16[4,1024,256]{2,1,0:T(8,128)(2,1)} %get-tuple-element.106.att_ref.o_ref, bf16[4,1024,256]{2,1,0:T(8,128)(2,1)} %project_back.2.do_ref, f32[4,1024,256]{2,1,0:T(8,128)} %get-tuple-element.112.lse_ref, ...), custom_call_target="tpu_custom_call" | custom-call | flops 1006632960 | bytes 1310720 | tf_op jit(solution)/shard_map/attend_back/pallas_call | solution.py:503
  268.5 20.0 %cross_back.1 = (bf16[8,2,2,96,768]{4,3,2,1,0:T(8,128)(2,1)}, f32[4,1,768]{2,1,0:T(1,128)}, f32[1024,768]{1,0:T(8,128)}, bf16[1024,768]{1,0:T(8,128)(2,1)}, f32[...) custom-call(bf16[4,1024,640]{2,1,0:T(8,128)(2,1)} %attend_back.3.dh_ref, bf16[8,2,2,96,1536]{4,3,2,1,0:T(8,128)(2,1)} %bitcast.234, ...), custom_call_target="tpu_custom_call" | custom-call | flops 603979776 | bytes 1474560 | tf_op jit(solution)/shard_map/cross_back/pallas_call | solution.py:503
  288.5 5.4 %project_back.3.do_ref = bf16[4,1024,256]{2,1,0:T(8,128)(2,1)} custom-call(bf16[1024,768]{1,0:T(8,128)(2,1)} %get-tuple-element.114.d_ref.dlow_ref, bf16[8,2,2,96,1536]{4,3,2,1,0:T(8,128)(2,1)} %bitcast.235), custom_call_target="tpu_custom_call" | custom-call | flops 100663296 | bytes 393216 | tf_op jit(solution)/shard_map/project_back/pallas_call | solution.py:503
  293.9 18.2 %attend_back.4.dh_ref = bf16[2,1024,640]{2,1,0:T(8,128)(2,1)} custom-call(bf16[4,1024,640]{2,1,0:T(8,128)(2,1)} %self_in.1.heads_ref, bf16[4,1024,256]{2,1,0:T(8,128)(2,1)} %get-tuple-element.103.att_ref.o_ref, bf16[4,1024,256]{2,1,0:T(8,128)(2,1)} %project_back.3.do_ref, f32[4,1024,256]{2,1,0:T(8,128)} %get-tuple-element.115.lse_ref, ...), custom_call_target="tpu_custom_call" | custom-call | flops 503316480 | bytes 655360 | tf_op jit(solution)/shard_map/attend_back/pallas_call | solution.py:503
  312.1 11.4 %self_back_first.1 = (bf16[8,2,1,96,768]{4,3,2,1,0:T(8,128)(2,1)}, f32[2,1,768]{2,1,0:T(1,128)}, f32[1024,768]{1,0:T(8,128)}) custom-call(bf16[2,1024,640]{2,1,0:T(8,128)(2,1)} %attend_back.4.dh_ref, bf16[8,2,2,96,1536]{4,3,2,1,0:T(8,128)(2,1)} %bitcast.236, bf16[1024,768]{1,0:T(8,128)(2,1)} %norm.2.n_ref, ...), custom_call_target="tpu_custom_call" | custom-call | flops 452984832 | bytes 1179648 | tf_op jit(solution)/shard_map/self_back_first/pallas_call | solution.py:503
  323.6 3.0 constant_dynamic-slice_fusion.6
  328.3 3.8 fusion.2
  332.0 4.0 all-to-all-start.3
  336.0 2.0 fusion.8
  338.4 18.0 %attend_back.5.dh_ref = bf16[2,1024,640]{2,1,0:T(8,128)(2,1)} custom-call(bf16[4,1024,640]{2,1,0:T(8,128)(2,1)} %self_in.1.heads_ref, bf16[4,1024,256]{2,1,0:T(8,128)(2,1)} %get-tuple-element.103.att_ref.o_ref, bf16[4,1024,256]{2,1,0:T(8,128)(2,1)} %project_back.3.do_ref, f32[4,1024,256]{2,1,0:T(8,128)} %get-tuple-element.115.lse_ref, ...), custom_call_target="tpu_custom_call" | custom-call | flops 503316480 | bytes 655360 | tf_op jit(solution)/shard_map/attend_back/pallas_call | solution.py:503
  356.5 2.2 fusion.30
  359.0 7.4 %self_weight.1 = bf16[8,2,1,96,768]{4,3,2,1,0:T(8,128)(2,1)} custom-call(bf16[2,1024,640]{2,1,0:T(8,128)(2,1)} %attend_back.5.dh_ref, bf16[1024,768]{1,0:T(8,128)(2,1)} %norm.2.n_ref, bf16[1024,768]{1,0:T(8,128)(2,1)} %get-tuple-element.114.d_ref.dlow_ref, bf16[4,1024,256]{2,1,0:T(8,128)(2,1)} %get-tuple-element.103.att_ref.o_ref), custom_call_target="tpu_custom_call" | custom-call | flops 301989888 | bytes 786432 | tf_op jit(solution)/shard_map/self_weight/pallas_call | solution.py:503
  366.5 2.8 constant_dynamic-slice_fusion.4
  369.5 1.9 collective-permute-start.5
  371.3 1.7 collective-permute-start.7
  373.0 2.1 collective-permute-start.8
  375.1 11.1 %self_rows.1 = (f32[2,1,768]{2,1,0:T(1,128)}, bf16[1024,768]{1,0:T(8,128)(2,1)}, f32[1,768]{1,0:T(1,128)}, f32[1,768]{1,0:T(1,128)}) custom-call(bf16[2,1024,640]{2,1,0:T(8,128)(2,1)} %attend_back.5.dh_ref, bf16[8,2,2,96,1536]{4,3,2,1,0:T(8,128)(2,1)} %bitcast.237, bf16[1024,768]{1,0:T(8,128)(2,1)} %fusion.5.x_ref.res_ref, ...), custom_call_target="tpu_custom_call" | custom-call | flops 150994944 | bytes 983040 | tf_op jit(solution)/shard_map/self_rows/pallas_call | solution.py:503
  386.2 2.4 collective-permute-done.7
  388.7 2.1 fusion.9
  390.8 3.8 fusion.1
  394.6 3.6 all-to-all-start.4
  400.8 2.0 collective-permute-start.12
  402.8 2.1 collective-permute-start.11
  405.0 10.9 %side_back.1 = (bf16[1024,768]{1,0:T(8,128)(2,1)}, f32[1,768]{1,0:T(1,128)}, f32[1,768]{1,0:T(1,128)}) custom-call(bf16[4,1024,640]{2,1,0:T(8,128)(2,1)} %attend_back.3.dh_ref, bf16[8,2,2,96,1536]{4,3,2,1,0:T(8,128)(2,1)} %bitcast.238, bf16[1024,768]{1,0:T(8,128)(2,1)} %fusion.4.x_ref.y_ref, f32[1,768]{1,0:T(1,128)} %get-tuple-element.350.gain_ref), custom_call_target="tpu_custom_call" | custom-call | flops 301989888 | bytes 786432 | tf_op jit(solution)/shard_map/side_back/pallas_call | solution.py:503
  415.8 1.5 collect.1
  420.2 3.1 collective-permute-done.10
  423.3 3.9 reduce-scatter.5.cloned.1.call-done
  427.2 1.5 fusion.25
  430.2 4.4 collective-permute-start.15
  434.6 1.7 collective-permute-start.14
  436.6 3.8 fusion
  440.3 3.6 all-to-all-start.5
  447.7 4.3 collective-permute-done.14
  452.0 1.4 convert_select_fusion.4
  457.8 1.7 copy.129
  459.6 6.0 %collective-permute-done.16 = f32[24,768]{1,0:T(8,128)} collective-permute-done((f32[24,768]{1,0:T(8,128)S(1)}, f32[24,768]{1,0:T(8,128)}, u32[]{:S(2)}, u32[]{:S(2)}) %collective-permute-start.16) | collective-permute-done | bytes 73760 | tf_op jit(solution)/shard_map/ppermute | solution.py:690
  471.5 1.9 copy.127
  (209 shorter events, 37.8 us)
Async XLA Ops:
  7.2 1.6 copy-start.12
  7.2 1.7 copy-start.16
  7.2 1.8 copy-start.17
  7.2 100.8 %all-gather.5.cloned.1.call-start = ((), (), s32[]{:S(2)}) async-start(), calls=%async_computation.10 | async-start | bytes 10027008 | tf_op jit(solution)/shard_map/all_gather | solution.py:553
  7.3 1.9 copy-start.18
  9.6 10.9 %copy-start.2 = (bf16[2,2,256,768]{3,2,1,0:T(8,128)(2,1)S(1)}, bf16[2,2,256,768]{3,2,1,0:T(8,128)(2,1)}, u32[]{:S(2)}) copy-start(bf16[2,2,256,768]{3,2,1,0:T(8,128)(2,1)} %param.25) | copy-start | bytes 4718596
  9.6 10.0 %collective-permute-start.1 = (bf16[96,1536]{1,0:T(8,128)(2,1)S(1)}, bf16[96,1536]{1,0:T(8,128)(2,1)S(1)}, u32[]{:S(2)}, u32[]{:S(2)}) collective-permute-start(bf16[96,1536]{1,0:T(8,128)(2,1)S(1)} %get-tuple-element.299), channel_id=1, source_target_pairs={{0,2},{1,3},{2,0},{3,1},{4,6},{5,7},{6,4},{7,5},{8,10},{9,11},{10,... | collective-permute-start | bytes 884744 | tf_op jit(solution)/shard_map/ppermute | solution.py:550
  21.9 7.7 %copy-start.21 = (bf16[2,3,192]{2,0,1:T(2,128)(2,1)S(1)}, bf16[2,3,192]{2,0,1:T(2,128)(2,1)}, u32[]{:S(2)}) copy-start(bf16[2,3,192]{2,0,1:T(2,128)(2,1)} %param.31) | copy-start | bytes 6916
  21.9 7.7 %copy-start.19 = (bf16[2,2,192]{2,1,0:T(2,128)(2,1)S(1)}, bf16[2,2,192]{2,1,0:T(2,128)(2,1)}, u32[]{:S(2)}) copy-start(bf16[2,2,192]{2,1,0:T(2,128)(2,1)} %param.41) | copy-start | bytes 4612
  21.9 7.7 %copy-start.34 = (s32[2,1,3]{2,1,0:T(1,128)S(1)}, s32[2,1,3]{2,1,0:T(1,128)}, u32[]{:S(2)}) copy-start(s32[2,1,3]{2,1,0:T(1,128)} %param.27) | copy-start | bytes 76
  21.9 8.0 %copy-start.20 = (bf16[2,768]{1,0:T(2,128)(2,1)S(1)}, bf16[2,768]{1,0:T(2,128)(2,1)}, u32[]{:S(2)}) copy-start(bf16[2,768]{1,0:T(2,128)(2,1)} %param.47) | copy-start | bytes 9220
  21.9 8.0 %copy-start.33 = (bf16[2,192]{1,0:T(2,128)(2,1)S(1)}, bf16[2,192]{1,0:T(2,128)(2,1)}, u32[]{:S(2)}) copy-start(bf16[2,192]{1,0:T(2,128)(2,1)} %param.39) | copy-start | bytes 2308
  21.9 9.4 %copy-start.22 = (bf16[2,768]{1,0:T(2,128)(2,1)S(1)}, bf16[2,768]{1,0:T(2,128)(2,1)}, u32[]{:S(2)}) copy-start(bf16[2,768]{1,0:T(2,128)(2,1)} %param.28) | copy-start | bytes 9220
  21.9 9.4 %copy-start.23 = (bf16[2,768]{1,0:T(2,128)(2,1)S(1)}, bf16[2,768]{1,0:T(2,128)(2,1)}, u32[]{:S(2)}) copy-start(bf16[2,768]{1,0:T(2,128)(2,1)} %param.36) | copy-start | bytes 9220
  22.0 10.0 %copy-start.24 = (bf16[2,768]{1,0:T(2,128)(2,1)S(1)}, bf16[2,768]{1,0:T(2,128)(2,1)}, u32[]{:S(2)}) copy-start(bf16[2,768]{1,0:T(2,128)(2,1)} %param.29) | copy-start | bytes 9220
  22.0 10.0 %copy-start.25 = (bf16[2,768]{1,0:T(2,128)(2,1)S(1)}, bf16[2,768]{1,0:T(2,128)(2,1)}, u32[]{:S(2)}) copy-start(bf16[2,768]{1,0:T(2,128)(2,1)} %param.37) | copy-start | bytes 9220
  22.0 24.2 %all-to-all-start.1 = ((bf16[4,256,768]{2,1,0:T(8,128)(2,1)}), bf16[4,256,768]{2,1,0:T(8,128)(2,1)S(1)}, u32[]{:S(2)}, u32[]{:S(2)}) async-start(bf16[4,256,768]{2,1,0:T(8,128)(2,1)} %bitcast.14), calls=%async_computation.1 | async-start | bytes 3145728 | tf_op jit(solution)/shard_map/all_to_all | solution.py:569
  27.6 28.9 %collective-permute-start = (bf16[96,1536]{1,0:T(8,128)(2,1)}, bf16[96,1536]{1,0:T(8,128)(2,1)}, u32[]{:S(2)}, u32[]{:S(2)}) collective-permute-start(bf16[96,1536]{1,0:T(8,128)(2,1)} %get-tuple-element.301), channel_id=1, source_target_pairs={{0,2},{1,3},{2,0},{3,1},{4,6},{5,7},{6,4},{7,5},{8,10},{9,11},{10,... | collective-permute-start | bytes 884744 | tf_op jit(solution)/shard_map/ppermute | solution.py:550
  46.2 24.1 %all-to-all-start = ((bf16[4,259,768]{2,1,0:T(8,128)(2,1)}), bf16[4,259,768]{2,1,0:T(8,128)(2,1)S(1)}, u32[]{:S(2)}, u32[]{:S(2)}) async-start(bf16[4,259,768]{2,1,0:T(8,128)(2,1)} %bitcast.9), calls=%async_computation | async-start | bytes 3244032 | tf_op jit(solution)/shard_map/all_to_all | solution.py:568
  49.8 136.3 %all-gather.7.cloned.1.call-start = ((), (), s32[]{:S(2)}) async-start(), calls=%async_computation.11 | async-start | bytes 10027008 | tf_op jit(solution)/shard_map/all_gather | solution.py:553
  74.2 4.3 copy-start.3
  79.8 4.0 copy-start.26
  79.8 4.6 copy-start.27
  79.8 5.2 %copy-start.28 = (bf16[2,768]{1,0:T(2,128)(2,1)S(1)}, bf16[2,768]{1,0:T(2,128)(2,1)}, u32[]{:S(2)}) copy-start(bf16[2,768]{1,0:T(2,128)(2,1)} %param.49) | copy-start | bytes 9220
  79.8 5.8 %copy-start.29 = (bf16[2,768]{1,0:T(2,128)(2,1)S(1)}, bf16[2,768]{1,0:T(2,128)(2,1)}, u32[]{:S(2)}) copy-start(bf16[2,768]{1,0:T(2,128)(2,1)} %param.33) | copy-start | bytes 9220
  79.8 5.8 %copy-start.30 = (bf16[2,768]{1,0:T(2,128)(2,1)S(1)}, bf16[2,768]{1,0:T(2,128)(2,1)}, u32[]{:S(2)}) copy-start(bf16[2,768]{1,0:T(2,128)(2,1)} %param.34) | copy-start | bytes 9220
  79.8 6.4 %copy-start.31 = (bf16[2,768]{1,0:T(2,128)(2,1)S(1)}, bf16[2,768]{1,0:T(2,128)(2,1)}, u32[]{:S(2)}) copy-start(bf16[2,768]{1,0:T(2,128)(2,1)} %param.35) | copy-start | bytes 9220
  79.8 6.4 %copy-start.32 = (bf16[2,768]{1,0:T(2,128)(2,1)S(1)}, bf16[2,768]{1,0:T(2,128)(2,1)}, u32[]{:S(2)}) copy-start(bf16[2,768]{1,0:T(2,128)(2,1)} %param.43) | copy-start | bytes 9220
  79.8 23.8 %all-to-all-start.2 = ((bf16[4,256,768]{2,1,0:T(8,128)(2,1)}), bf16[4,256,768]{2,1,0:T(8,128)(2,1)S(1)}, u32[]{:S(2)}, u32[]{:S(2)}) async-start(bf16[4,256,768]{2,1,0:T(8,128)(2,1)} %bitcast.31), calls=%async_computation.2 | async-start | bytes 3145728 | tf_op jit(solution)/shard_map/all_to_all | solution.py:570
  83.5 272.9 %reduce-scatter.3.cloned.1.call-start = ((), (), s32[]{:S(2)}) async-start(), calls=%async_computation.8 | async-start | bytes 10027008 | tf_op jit(solution)/shard_map/reduce_scatter | solution.py:651
  229.6 197.6 %reduce-scatter.5.cloned.1.call-start = ((), (), s32[]{:S(2)}) async-start(), calls=%async_computation.9 | async-start | bytes 5013504 | tf_op jit(solution)/shard_map/reduce_scatter | solution.py:651
  323.6 4.7 copy-start.5
  326.5 30.0 %copy-start = (bf16[8,1,1,96,768]{4,3,2,1,0:T(8,128)(2,1)}, bf16[8,1,1,96,768]{4,3,2,1,0:T(8,128)(2,1)S(1)}, u32[]{:S(2)}) copy-start(bf16[8,1,1,96,768]{4,3,2,1,0:T(8,128)(2,1)S(1)} %get-tuple-element.282) | copy-start | bytes 3538948
  326.5 5.5 %collective-permute-start.2 = (bf16[8,1,96,768]{3,2,0,1:T(8,128)(2,1)}, bf16[8,1,96,768]{3,2,0,1:T(8,128)(2,1)}, u32[]{:S(2)}, u32[]{:S(2)}) collective-permute-start(bf16[8,1,96,768]{3,2,0,1:T(8,128)(2,1)} %get-tuple-element.283), channel_id=1, source_target_pairs={{0,1},{1,0},{2,3},{3,2},{4,5},{5,4},{6,7},{7,6},{8,9},{9,8},{10,11... | collective-permute-start | bytes 3538952 | tf_op jit(solution)/shard_map/ppermute | solution.py:672
  332.0 24.4 %all-to-all-start.3 = ((bf16[4,256,768]{2,1,0:T(8,128)(2,1)}), bf16[4,256,768]{2,1,0:T(8,128)(2,1)S(1)}, u32[]{:S(2)}, u32[]{:S(2)}) async-start(bf16[4,256,768]{2,1,0:T(8,128)(2,1)} %bitcast.37), calls=%async_computation.4 | async-start | bytes 3145728 | tf_op jit(solution)/shard_map/all_to_all | solution.py:756
  338.0 18.4 %collective-permute-start.3 = (bf16[4,1,96,768]{3,2,1,0:T(8,128)(2,1)}, bf16[4,1,96,768]{3,2,1,0:T(8,128)(2,1)}, u32[]{:S(2)}, u32[]{:S(2)}) collective-permute-start(bf16[4,1,96,768]{3,2,1,0:T(8,128)(2,1)} %fusion.8), channel_id=1, source_target_pairs={{0,4},{4,0},{8,12},{12,8},{16,20},{20,16},{24,28},{28,24},{1,5},{5... | collective-permute-start | bytes 1769480 | tf_op jit(solution)/shard_map/ppermute | solution.py:672
  358.7 7.8 %collective-permute-start.4 = (bf16[1,96,768]{2,1,0:T(8,128)(2,1)S(1)}, bf16[1,96,768]{2,1,0:T(8,128)(2,1)}, u32[]{:S(2)}, u32[]{:S(2)}) collective-permute-start(bf16[1,96,768]{2,1,0:T(8,128)(2,1)S(1)} %get-tuple-element.279), channel_id=1, source_target_pairs={{0,8},{4,12},{8,16},{12,20},{16,24},{20,28},{24,0},{28,4},{1,9},{5... | collective-permute-start | bytes 442376 | tf_op jit(solution)/shard_map/ppermute | solution.py:776
  366.4 3.0 copy-start.8
  369.4 19.3 %copy-start.1 = (bf16[8,1,1,96,768]{4,3,2,1,0:T(8,128)(2,1)}, bf16[8,1,1,96,768]{4,3,2,1,0:T(8,128)(2,1)S(1)}, u32[]{:S(2)}) copy-start(bf16[8,1,1,96,768]{4,3,2,1,0:T(8,128)(2,1)S(1)} %get-tuple-element.280) | copy-start | bytes 3538948
  369.4 19.3 %collective-permute-start.6 = (bf16[8,1,96,768]{3,2,0,1:T(8,128)(2,1)}, bf16[8,1,96,768]{3,2,0,1:T(8,128)(2,1)}, u32[]{:S(2)}, u32[]{:S(2)}) collective-permute-start(bf16[8,1,96,768]{3,2,0,1:T(8,128)(2,1)} %get-tuple-element.281), channel_id=1, source_target_pairs={{0,1},{1,0},{2,3},{3,2},{4,5},{5,4},{6,7},{7,6},{8,9},{9,8},{10,11... | collective-permute-start | bytes 3538952 | tf_op jit(solution)/shard_map/ppermute | solution.py:672
  369.5 19.2 %collective-permute-start.5 = (bf16[96,1536]{1,0:T(8,128)(2,1)S(1)}, bf16[96,1536]{1,0:T(8,128)(2,1)S(1)}, u32[]{:S(2)}, u32[]{:S(2)}) collective-permute-start(bf16[96,1536]{1,0:T(8,128)(2,1)S(1)} %slice_bitcast_fusion), channel_id=1, source_target_pairs={{0,2},{1,3},{2,0},{3,1},{4,6},{5,7},{6,4},{7,5},{8,10},{9,11},{10,... | collective-permute-start | bytes 884744 | tf_op jit(solution)/shard_map/ppermute | solution.py:690
  371.3 17.2 %collective-permute-start.7 = (bf16[1,96,768]{2,1,0:T(8,128)(2,1)}, bf16[1,96,768]{2,1,0:T(8,128)(2,1)}, u32[]{:S(2)}, u32[]{:S(2)}) collective-permute-start(bf16[1,96,768]{2,1,0:T(8,128)(2,1)} %get-tuple-element.278), channel_id=1, source_target_pairs={{0,16},{4,20},{8,24},{12,28},{16,0},{20,4},{24,8},{28,12},{1,17},{... | collective-permute-start | bytes 442376 | tf_op jit(solution)/shard_map/ppermute | solution.py:776
  373.0 15.6 %collective-permute-start.8 = (bf16[1,96,768]{2,1,0:T(8,128)(2,1)}, bf16[1,96,768]{2,1,0:T(8,128)(2,1)}, u32[]{:S(2)}, u32[]{:S(2)}) collective-permute-start(bf16[1,96,768]{2,1,0:T(8,128)(2,1)} %get-tuple-element.277), channel_id=1, source_target_pairs={{0,24},{4,28},{8,0},{12,4},{16,8},{20,12},{24,16},{28,20},{1,25},{... | collective-permute-start | bytes 442376 | tf_op jit(solution)/shard_map/ppermute | solution.py:776
  386.2 4.6 copy-start.6
  388.7 5.9 %copy-start.14 = (bf16[96,1536]{1,0:T(8,128)(2,1)}, bf16[96,1536]{1,0:T(8,128)(2,1)S(1)}, u32[]{:S(2)}) copy-start(bf16[96,1536]{1,0:T(8,128)(2,1)S(1)} %collective-permute-done.5) | copy-start | bytes 884740
  394.6 32.7 %all-to-all-start.4 = ((bf16[4,256,768]{2,1,0:T(8,128)(2,1)}), bf16[4,256,768]{2,1,0:T(8,128)(2,1)S(1)}, u32[]{:S(2)}, u32[]{:S(2)}) async-start(bf16[4,256,768]{2,1,0:T(8,128)(2,1)} %bitcast.246), calls=%async_computation.5 | async-start | bytes 3145728 | tf_op jit(solution)/shard_map/all_to_all | solution.py:756
  400.8 26.4 %collective-permute-start.12 = (bf16[1,96,768]{2,1,0:T(8,128)(2,1)S(1)}, bf16[1,96,768]{2,1,0:T(8,128)(2,1)S(1)}, u32[]{:S(2)}, u32[]{:S(2)}) collective-permute-start(bf16[1,96,768]{2,1,0:T(8,128)(2,1)S(1)} %fusion.29), channel_id=1, source_target_pairs={{0,2},{1,3},{2,0},{3,1},{4,6},{5,7},{6,4},{7,5},{8,10},{9,11},{10,... | collective-permute-start | bytes 442376 | tf_op jit(solution)/shard_map/ppermute | solution.py:690
  402.8 14.6 %copy-start.9 = (bf16[1,2,96,1536]{3,2,1,0:T(8,128)(2,1)S(1)}, bf16[1,2,96,1536]{3,2,1,0:T(8,128)(2,1)}, u32[]{:S(2)}) copy-start(bf16[1,2,96,1536]{3,2,1,0:T(8,128)(2,1)} %reduce-scatter.3.cloned.1.call-done) | copy-start | bytes 1769476
  402.8 14.6 %copy-start.15 = (bf16[96,1536]{1,0:T(8,128)(2,1)S(1)}, bf16[96,1536]{1,0:T(8,128)(2,1)}, u32[]{:S(2)}) copy-start(bf16[96,1536]{1,0:T(8,128)(2,1)} %copy-done.14) | copy-start | bytes 884740
  402.8 20.5 %collective-permute-start.11 = (bf16[4,1,96,768]{3,2,1,0:T(8,128)(2,1)}, bf16[4,1,96,768]{3,2,1,0:T(8,128)(2,1)S(1)}, u32[]{:S(2)}, u32[]{:S(2)}) collective-permute-start(bf16[4,1,96,768]{3,2,1,0:T(8,128)(2,1)} %bitcast.55), channel_id=1, source_target_pairs={{0,4},{4,0},{8,12},{12,8},{16,20},{20,16},{24,28},{28,24},{1,5},{5... | collective-permute-start | bytes 1769480 | tf_op jit(solution)/shard_map/ppermute | solution.py:791
  417.4 1.5 copy-start.11
  417.4 1.5 collective-permute-start.9
  418.9 4.4 collective-permute-start.10
  423.3 13.0 %copy-start.7 = (bf16[4,1,96,768]{3,2,1,0:T(8,128)(2,1)}, bf16[4,1,96,768]{3,2,1,0:T(8,128)(2,1)S(1)}, u32[]{:S(2)}) copy-start(bf16[4,1,96,768]{3,2,1,0:T(8,128)(2,1)S(1)} %collective-permute-done.11) | copy-start | bytes 1769476
  427.2 9.1 %copy-start.13 = (bf16[1,2,96,768]{3,2,1,0:T(8,128)(2,1)S(1)}, bf16[1,2,96,768]{3,2,1,0:T(8,128)(2,1)}, u32[]{:S(2)}) copy-start(bf16[1,2,96,768]{3,2,1,0:T(8,128)(2,1)} %reduce-scatter.5.cloned.1.call-done) | copy-start | bytes 884740
  427.2 9.3 %copy-start.4 = (bf16[1024,768]{1,0:T(8,128)(2,1)S(1)}, bf16[1024,768]{1,0:T(8,128)(2,1)}, u32[]{:S(2)}) copy-start(bf16[1024,768]{1,0:T(8,128)(2,1)} %get-tuple-element.165) | copy-start | bytes 4718596
  430.2 17.4 %collective-permute-start.15 = (bf16[120,768]{1,0:T(8,128)(2,1)}, bf16[120,768]{1,0:T(8,128)(2,1)}, u32[]{:S(2)}, u32[]{:S(2)}) collective-permute-start(bf16[120,768]{1,0:T(8,128)(2,1)} %get-tuple-element.335), channel_id=1, source_target_pairs={{0,24},{4,28},{8,0},{12,4},{16,8},{20,12},{24,16},{28,20},{1,25},{... | collective-permute-start | bytes 552968 | tf_op jit(solution)/shard_map/ppermute | solution.py:818
  434.6 17.4 %collective-permute-start.14 = (bf16[120,768]{1,0:T(8,128)(2,1)}, bf16[120,768]{1,0:T(8,128)(2,1)}, u32[]{:S(2)}, u32[]{:S(2)}) collective-permute-start(bf16[120,768]{1,0:T(8,128)(2,1)} %get-tuple-element.334), channel_id=1, source_target_pairs={{0,16},{4,20},{8,24},{12,28},{16,0},{20,4},{24,8},{28,12},{1,17},{... | collective-permute-start | bytes 552968 | tf_op jit(solution)/shard_map/ppermute | solution.py:818
  436.3 15.7 %collective-permute-start.13 = (bf16[120,768]{1,0:T(8,128)(2,1)}, bf16[120,768]{1,0:T(8,128)(2,1)}, u32[]{:S(2)}, u32[]{:S(2)}) collective-permute-start(bf16[120,768]{1,0:T(8,128)(2,1)} %get-tuple-element.333), channel_id=1, source_target_pairs={{0,8},{4,12},{8,16},{12,20},{16,24},{20,28},{24,0},{28,4},{1,9},{5... | collective-permute-start | bytes 552968 | tf_op jit(solution)/shard_map/ppermute | solution.py:818
  436.3 7.6 %collective-permute-start.17 = (bf16[96,768]{1,0:T(8,128)(2,1)S(1)}, bf16[96,768]{1,0:T(8,128)(2,1)}, u32[]{:S(2)}, u32[]{:S(2)}) collective-permute-start(bf16[96,768]{1,0:T(8,128)(2,1)S(1)} %slice_bitcast_fusion.1), channel_id=1, source_target_pairs={{0,2},{1,3},{2,0},{3,1},{4,6},{5,7},{6,4},{7,5},{8,10},{9,11},{10,... | collective-permute-start | bytes 442376 | tf_op jit(solution)/shard_map/ppermute | solution.py:690
  440.3 30.9 %all-to-all-start.5 = ((bf16[4,256,768]{2,1,0:T(8,128)(2,1)}), bf16[4,256,768]{2,1,0:T(8,128)(2,1)S(1)}, u32[]{:S(2)}, u32[]{:S(2)}) async-start(bf16[4,256,768]{2,1,0:T(8,128)(2,1)} %bitcast.248), calls=%async_computation.7 | async-start | bytes 3145728 | tf_op jit(solution)/shard_map/all_to_all | solution.py:756
  453.4 2.5 copy-start.10
  455.9 9.7 %collective-permute-start.16 = (f32[24,768]{1,0:T(8,128)S(1)}, f32[24,768]{1,0:T(8,128)}, u32[]{:S(2)}, u32[]{:S(2)}) collective-permute-start(f32[24,768]{1,0:T(8,128)S(1)} %fusion.105), channel_id=1, source_target_pairs={{0,2},{1,3},{2,0},{3,1},{4,6},{5,7},{6,4},{7,5},{8,10},{9,11},{10,... | collective-permute-start | bytes 221192 | tf_op jit(solution)/shard_map/ppermute | solution.py:690
Sparse Core Ops, SparseCore 0:
  20.7 82.8 all-gather.4
  106.5 79.5 all-gather.6
  229.7 109.4 reduce-scatter.2
  343.4 83.7 reduce-scatter.4

commit v5 on v3

--- a/solution.py
+++ b/solution.py
@@ -767,12 +767,12 @@
         sum_ffn = both_views(total_ffn[0], their_ffn)
         up_wg, down_wg = sum_ffn[..., :fw], flip(sum_ffn[..., fw:])
         their1 = to_partner(total1)
-        flat = small + lax.ppermute(small, "dp", x_pairs)
+        flat = lax.reduce_precision(small + lax.ppermute(small, "dp", x_pairs), 8, 7)
+        flat = jnp.concatenate([flat, to_partner(flat.astype(BF)).astype(F32)], 0)
         flat, got, their1, got_own, other, up_wg, down_wg, total_cross = lax.optimization_barrier((flat, self0[2], their1, got_own, other, up_wg, down_wg, total_cross))
         other = from_row(other, rows - first)
         got_other = home(other)
         their_cross = to_partner(total_cross[1])
-        flat = lax.reduce_precision(flat, 8, 7)
         self0 = self0[:2] + [got]
         total0 = added([pick(t, z_place, 0) for t in self0])
         on_line = [flat]
@@ -783,7 +783,7 @@
             on_line.append(got[send.size // width :].astype(F32))
         on_line = jnp.stack(on_line, 0)
         flat = sum(pick(on_line, (z_place - p) % lines, 0) for p in range(lines))
-        flat_in = to_partner(flat)
+        flat, flat_in = flat[: small.shape[0]], flat[small.shape[0] :]
         sum_self = both_views(total0[0], their1[0])
     else:
         got_other = home(from_row(other, rows - first))

time: 483 us -> 483 us (level)
    ppermute x1, waiting for transfers between devices: 3.19 us -> 12.2 us  [body(): lax.ppermute(small, 'dp', x_pairs)]
    ppermute x4, waiting for transfers between devices: 7.73 us -> 0.9 us  [to_partner(): return lax.ppermute(a, 'mp', partner)]
  transfers between devices with their start and end apart: 28 -> 28, of which waited for: 10 -> 9; matrix products, arithmetic and copies ran while one was open for 16% -> 15% of each run, Pallas kernels for 44% -> 44%
where the time goes in v5:
time: 483 us; the launch traced here: 474 us
  Pallas kernels  254 us (53%)
  waiting for transfers between devices  75.1 us (16%)
  other arithmetic  60.9 us (13%)
  starting transfers between devices  46.4 us (10%)
  local copies, waits for them, and re-layouts  19.7 us (4%)
  between operations  18.3 us (4%)
    pallas_call x19, Pallas kernels, call(): pl.pallas_call(kernel, grid=(steps,), in_specs=[s for _, s in ins], out_s...  254 us
    concatenate x6, other arithmetic, from_row(): return lax.dynamic_slice_in_dim(jnp.concatenate([a, a], 0), at, rows, 0)  22.5 us
    all_to_all x1, waiting for transfers between devices, body(): lax.all_to_all(cotangent.swapaxes(0, 1).reshape(members, local, width), '...  16.8 us
    all_gather x2, waiting for transfers between devices, gather(): lax.all_gather(pair, both, axis=0, axis_index_groups=groups)  16.5 us
    ppermute x1, waiting for transfers between devices, body(): lax.ppermute(small, 'dp', x_pairs)  12.2 us
    all_to_all x1, waiting for transfers between devices, body(): lax.all_to_all(by_view[::-1].reshape(members, local, width), 'mp', 0, 0,...  11.4 us
    all_to_all x3, starting transfers between devices, home(): lax.all_to_all(a.reshape(members, local, width), 'mp', 0, 0, tiled=True)  11.1 us
    unnamed x85, local copies, waits for them, and re-layouts  10 us
  transfers between devices with their start and end apart: 28, of which 9 were waited for; matrix products, arithmetic and copies ran while one was open for 15% of the time, Pallas kernels for 44%

profile of v5, /device:TPU:0, one launch (start us, length us, event | category | flops | bytes accessed | tf_op | source)
XLA Modules:
  0.0 474.1 jit_solution(4635619191117649602)
XLA Ops:
  7.3 1.5 fusion.106
  9.6 3.0 collective-permute-start.1
  12.6 7.0 %collective-permute-done.1 = bf16[96,1536]{1,0:T(8,128)(2,1)S(1)} collective-permute-done((bf16[96,1536]{1,0:T(8,128)(2,1)S(1)}, bf16[96,1536]{1,0:T(8,128)(2,1)S(1)}, u32[]{:S(2)}, u32[]{:S(2)}) %collective-permute-start.1) | collective-permute-done | bytes 294944 | tf_op jit(solution)/shard_map/ppermute | solution.py:527
  20.7 1.2 rev.9
  22.0 3.7 all-to-all-start.1
  25.7 1.9 fusion.18
  27.6 2.0 collective-permute-start
  32.6 1.3 pad_maximum_fusion
  34.8 11.4 %all-to-all-done.1 = bf16[4,256,768]{2,1,0:T(8,128)(2,1)S(1)} async-done(((bf16[4,256,768]{2,1,0:T(8,128)(2,1)}), bf16[4,256,768]{2,1,0:T(8,128)(2,1)S(1)}, u32[]{:S(2)}, u32[]{:S(2)}) %all-to-all-start.1) | async-done | bytes 1572896 | tf_op jit(solution)/shard_map/all_to_all | solution.py:546
  46.2 3.6 all-to-all-start
  53.4 3.1 fusion.12
  56.4 1.8 pad_maximum_fusion.2
  58.3 3.8 fusion.4.x_ref.y_ref
  62.0 4.1 norm.3.side_ref
  66.2 4.2 all-to-all-done
  70.5 3.8 fusion.5.x_ref.res_ref
  74.2 4.3 norm.2.n_ref
  78.6 1.2 copy.123
  79.9 3.7 all-to-all-start.2
  86.8 16.8 %all-to-all-done.2 = bf16[4,256,768]{2,1,0:T(8,128)(2,1)S(1)} async-done(((bf16[4,256,768]{2,1,0:T(8,128)(2,1)}), bf16[4,256,768]{2,1,0:T(8,128)(2,1)S(1)}, u32[]{:S(2)}, u32[]{:S(2)}) %all-to-all-start.2) | async-done | bytes 1572896 | tf_op jit(solution)/shard_map/all_to_all | solution.py:547
  103.6 3.7 fusion.3.dz_ref
  108.0 9.5 %self_in.1.heads_ref = bf16[4,1024,640]{2,1,0:T(8,128)(2,1)} custom-call(bf16[1024,768]{1,0:T(8,128)(2,1)} %norm.2.n_ref, bf16[8,2,2,96,1536]{4,3,2,1,0:T(8,128)(2,1)} %bitcast.212, f32[4,1,768]{2,1,0:T(1,128)} %get-tuple-element.337.bias_ref, f32[1024,128]{1,0:T(8,128)} %get-tuple-element.99.cos_ref, f32[1024,128]{1,0:T(8,128)} %get-tuple-element.100.sin_ref), custom_call_target="tpu_custom_call" | custom-call | flops 301989888 | bytes 786432 | tf_op jit(solution)/shard_map/self_in/pallas_call | solution.py:480
  117.5 14.5 %attend.2 = (bf16[4,1024,256]{2,1,0:T(8,128)(2,1)}, f32[4,1024,256]{2,1,0:T(8,128)}) custom-call(bf16[4,1024,640]{2,1,0:T(8,128)(2,1)} %self_in.1.heads_ref, bf16[1024,128]{1,0:T(8,128)(2,1)} %select_convert_fusion.qf_ref, bf16[1024,128]{1,0:T(8,128)(2,1)} %compare_convert_fusion.kf_ref), custom_call_target="tpu_custom_call" | custom-call | flops 402653184 | bytes 720896 | tf_op jit(solution)/shard_map/attend/pallas_call | solution.py:480
  132.0 6.1 %project.2 = (f32[1024,768]{1,0:T(8,128)}, bf16[1024,768]{1,0:T(8,128)(2,1)}) custom-call(bf16[4,1024,256]{2,1,0:T(8,128)(2,1)} %get-tuple-element.103.att_ref.o_ref, bf16[8,2,2,96,1536]{4,3,2,1,0:T(8,128)(2,1)} %bitcast.213, bf16[1024,768]{1,0:T(8,128)(2,1)} %fusion.5.x_ref.res_ref, f32[1,768]{1,0:T(1,128)} %get-tuple-element.355.bias_ref, ...), custom_call_target="tpu_custom_call" | custom-call | flops 100663296 | bytes 688128 | tf_op jit(solution)/shard_map/project/pallas_call | solution.py:480
  138.0 10.8 %cross_in.1.heads_ref = bf16[4,1024,640]{2,1,0:T(8,128)(2,1)} custom-call(bf16[1024,768]{1,0:T(8,128)(2,1)} %get-tuple-element.104.n_ref, bf16[1024,768]{1,0:T(8,128)(2,1)} %norm.3.side_ref, bf16[8,2,2,96,1536]{4,3,2,1,0:T(8,128)(2,1)} %bitcast.214, f32[4,1,768]{2,1,0:T(1,128)} %get-tuple-element.336.bias_ref, f32[1024,128]{1,0:T(8,128)} %get-tuple-element.99.cos_ref, ...), custom_call_target="tpu_custom_call" | custom-call | flops 301989888 | bytes 786432 | tf_op jit(solution)/shard_map/cross_in/pallas_call | solution.py:480
  148.9 14.5 %attend.3 = (bf16[4,1024,256]{2,1,0:T(8,128)(2,1)}, f32[4,1024,256]{2,1,0:T(8,128)}) custom-call(bf16[4,1024,640]{2,1,0:T(8,128)(2,1)} %cross_in.1.heads_ref, bf16[1024,128]{1,0:T(8,128)(2,1)} %select_convert_fusion.qf_ref, bf16[1024,128]{1,0:T(8,128)(2,1)} %compare_convert_fusion.kf_ref), custom_call_target="tpu_custom_call" | custom-call | flops 402653184 | bytes 720896 | tf_op jit(solution)/shard_map/attend/pallas_call | solution.py:480
  163.3 6.3 %project.3 = (f32[1024,768]{1,0:T(8,128)}, bf16[1024,768]{1,0:T(8,128)(2,1)}) custom-call(bf16[4,1024,256]{2,1,0:T(8,128)(2,1)} %get-tuple-element.106.att_ref.o_ref, bf16[8,2,2,96,1536]{4,3,2,1,0:T(8,128)(2,1)} %bitcast.215, f32[1024,768]{1,0:T(8,128)} %get-tuple-element.107.res_ref.mid_ref, f32[1,768]{1,0:T(1,128)} %get-tuple-element.358.bias_ref, ...), custom_call_target="tpu_custom_call" | custom-call | flops 100663296 | bytes 688128 | tf_op jit(solution)/shard_map/project/pallas_call | solution.py:480
  169.6 16.5 %all-gather.7.cloned.1.call-done = bf16[32,96,1536]{2,1,0:T(8,128)(2,1)} async-done(((bf16[2,96,1536]{2,1,0:T(8,128)(2,1)}), bf16[32,96,1536]{2,1,0:T(8,128)(2,1)}) %all-gather.7.cloned.1.call-update) | async-done | bytes 9437200 | tf_op jit(solution)/shard_map/all_gather | solution.py:530
  186.1 43.5 %ffn.1 = (bf16[1024,768]{1,0:T(8,128)(2,1)}, f32[1024,768]{1,0:T(8,128)}, bf16[1024,768]{1,0:T(8,128)(2,1)}, bf16[8,2,2,96,1536]{4,3,2,1,0:T(8,128)(2,1)}, f32[4...) custom-call(f32[1024,768]{1,0:T(8,128)} %get-tuple-element.108.mid_ref, ...), custom_call_target="tpu_custom_call" | custom-call | flops 1811939328 | bytes 2949120 | tf_op jit(solution)/shard_map/ffn/pallas_call | solution.py:480
  229.6 5.7 %project_back.2.do_ref = bf16[4,1024,256]{2,1,0:T(8,128)(2,1)} custom-call(bf16[1024,768]{1,0:T(8,128)(2,1)} %get-tuple-element.111.d_ref.dlow_ref, bf16[8,2,2,96,1536]{4,3,2,1,0:T(8,128)(2,1)} %bitcast.216), custom_call_target="tpu_custom_call" | custom-call | flops 100663296 | bytes 393216 | tf_op jit(solution)/shard_map/project_back/pallas_call | solution.py:480
  235.3 33.2 %attend_back.3.dh_ref = bf16[4,1024,640]{2,1,0:T(8,128)(2,1)} custom-call(bf16[4,1024,640]{2,1,0:T(8,128)(2,1)} %cross_in.1.heads_ref, bf16[4,1024,256]{2,1,0:T(8,128)(2,1)} %get-tuple-element.106.att_ref.o_ref, bf16[4,1024,256]{2,1,0:T(8,128)(2,1)} %project_back.2.do_ref, f32[4,1024,256]{2,1,0:T(8,128)} %get-tuple-element.112.lse_ref, ...), custom_call_target="tpu_custom_call" | custom-call | flops 1006632960 | bytes 1310720 | tf_op jit(solution)/shard_map/attend_back/pallas_call | solution.py:480
  268.5 20.0 %cross_back.1 = (bf16[8,2,2,96,768]{4,3,2,1,0:T(8,128)(2,1)}, f32[4,1,768]{2,1,0:T(1,128)}, f32[1024,768]{1,0:T(8,128)}, bf16[1024,768]{1,0:T(8,128)(2,1)}, f32[...) custom-call(bf16[4,1024,640]{2,1,0:T(8,128)(2,1)} %attend_back.3.dh_ref, bf16[8,2,2,96,1536]{4,3,2,1,0:T(8,128)(2,1)} %bitcast.217, ...), custom_call_target="tpu_custom_call" | custom-call | flops 603979776 | bytes 1474560 | tf_op jit(solution)/shard_map/cross_back/pallas_call | solution.py:480
  288.5 5.4 %project_back.3.do_ref = bf16[4,1024,256]{2,1,0:T(8,128)(2,1)} custom-call(bf16[1024,768]{1,0:T(8,128)(2,1)} %get-tuple-element.114.d_ref.dlow_ref, bf16[8,2,2,96,1536]{4,3,2,1,0:T(8,128)(2,1)} %bitcast.218), custom_call_target="tpu_custom_call" | custom-call | flops 100663296 | bytes 393216 | tf_op jit(solution)/shard_map/project_back/pallas_call | solution.py:480
  293.9 18.3 %attend_back.4.dh_ref = bf16[2,1024,640]{2,1,0:T(8,128)(2,1)} custom-call(bf16[4,1024,640]{2,1,0:T(8,128)(2,1)} %self_in.1.heads_ref, bf16[4,1024,256]{2,1,0:T(8,128)(2,1)} %get-tuple-element.103.att_ref.o_ref, bf16[4,1024,256]{2,1,0:T(8,128)(2,1)} %project_back.3.do_ref, f32[4,1024,256]{2,1,0:T(8,128)} %get-tuple-element.115.lse_ref, ...), custom_call_target="tpu_custom_call" | custom-call | flops 503316480 | bytes 655360 | tf_op jit(solution)/shard_map/attend_back/pallas_call | solution.py:480
  312.1 11.4 %self_back_first.1 = (bf16[8,2,1,96,768]{4,3,2,1,0:T(8,128)(2,1)}, f32[2,1,768]{2,1,0:T(1,128)}, f32[1024,768]{1,0:T(8,128)}) custom-call(bf16[2,1024,640]{2,1,0:T(8,128)(2,1)} %attend_back.4.dh_ref, bf16[8,2,2,96,1536]{4,3,2,1,0:T(8,128)(2,1)} %bitcast.219, bf16[1024,768]{1,0:T(8,128)(2,1)} %norm.2.n_ref, ...), custom_call_target="tpu_custom_call" | custom-call | flops 452984832 | bytes 1179648 | tf_op jit(solution)/shard_map/self_back_first/pallas_call | solution.py:480
  323.6 2.9 constant_dynamic-slice_fusion.6
  328.2 3.8 fusion.2
  332.0 4.0 all-to-all-start.3
  336.0 2.0 fusion.8
  338.4 18.0 %attend_back.5.dh_ref = bf16[2,1024,640]{2,1,0:T(8,128)(2,1)} custom-call(bf16[4,1024,640]{2,1,0:T(8,128)(2,1)} %self_in.1.heads_ref, bf16[4,1024,256]{2,1,0:T(8,128)(2,1)} %get-tuple-element.103.att_ref.o_ref, bf16[4,1024,256]{2,1,0:T(8,128)(2,1)} %project_back.3.do_ref, f32[4,1024,256]{2,1,0:T(8,128)} %get-tuple-element.115.lse_ref, ...), custom_call_target="tpu_custom_call" | custom-call | flops 503316480 | bytes 655360 | tf_op jit(solution)/shard_map/attend_back/pallas_call | solution.py:480
  356.5 2.0 fusion.28
  358.8 1.7 collective-permute-start.6
  360.5 2.1 collective-permute-start.7
  363.2 2.0 collective-permute-start.4
  365.2 15.9 %self_back_last.1 = (bf16[8,2,1,96,768]{4,3,2,1,0:T(8,128)(2,1)}, f32[2,1,768]{2,1,0:T(1,128)}, bf16[1024,768]{1,0:T(8,128)(2,1)}, f32[1,768]{1,0:T(1,128)}, f32[1,768]{1,0:T(1,128)}) custom-call(bf16[2,1024,640]{2,1,0:T(8,128)(2,1)} %attend_back.5.dh_ref, bf16[8,2,2,96,1536]{4,3,2,1,0:T(8,128)(2,1)} %bitcast.220, bf16[1024,768]{1,0:T(8,128)(2,1)} %norm.2.n_ref, ...), custom_call_target="tpu_custom_call" | custom-call | flops 452984832 | bytes 1474560 | tf_op jit(solution)/shard_map/self_back_last/pallas_call | solution.py:480
  383.0 1.9 constant_dynamic-slice_fusion.3
  385.1 3.8 fusion.1
  390.3 3.6 all-to-all-start.4
  393.8 10.9 %side_back.1 = (bf16[1024,768]{1,0:T(8,128)(2,1)}, f32[1,768]{1,0:T(1,128)}, f32[1,768]{1,0:T(1,128)}) custom-call(bf16[4,1024,640]{2,1,0:T(8,128)(2,1)} %attend_back.3.dh_ref, bf16[8,2,2,96,1536]{4,3,2,1,0:T(8,128)(2,1)} %bitcast.221, bf16[1024,768]{1,0:T(8,128)(2,1)} %fusion.4.x_ref.y_ref, f32[1,768]{1,0:T(1,128)} %get-tuple-element.352.gain_ref), custom_call_target="tpu_custom_call" | custom-call | flops 301989888 | bytes 786432 | tf_op jit(solution)/shard_map/side_back/pallas_call | solution.py:480
  404.8 1.5 collect.1
  407.9 1.9 collective-permute-start.12
  411.1 1.7 collective-permute-start.13
  412.9 12.2 %collective-permute-done.10 = f32[24,768]{1,0:T(8,128)S(1)} collective-permute-done((f32[24,768]{1,0:T(8,128)S(1)}, f32[24,768]{1,0:T(8,128)S(1)}, u32[]{:S(2)}, u32[]{:S(2)}) %collective-permute-start.10) | collective-permute-done | bytes 73760 | tf_op jit(solution)/shard_map/ppermute | solution.py:770
  425.0 2.0 collective-permute-start.11
  429.2 1.6 fusion.25
  431.8 1.5 collective-permute-start.16
  433.5 2.1 collective-permute-start.14
  435.7 2.0 collective-permute-start.17
  437.7 3.8 fusion
  441.4 3.6 all-to-all-start.5
  449.7 2.4 collective-permute-done.15
  454.9 1.4 convert_select_fusion.4
  461.5 3.6 all-to-all-done.5
  465.4 1.9 copy.127
  (212 shorter events, 35.5 us)
Async XLA Ops:
  7.2 1.6 copy-start.14
  7.2 1.7 copy-start.17
  7.2 1.8 copy-start.18
  7.2 100.8 %all-gather.5.cloned.1.call-start = ((), (), s32[]{:S(2)}) async-start(), calls=%async_computation.10 | async-start | bytes 10027008 | tf_op jit(solution)/shard_map/all_gather | solution.py:530
  7.3 1.9 copy-start.19
  9.5 11.0 %copy-start.1 = (bf16[2,2,256,768]{3,2,1,0:T(8,128)(2,1)S(1)}, bf16[2,2,256,768]{3,2,1,0:T(8,128)(2,1)}, u32[]{:S(2)}) copy-start(bf16[2,2,256,768]{3,2,1,0:T(8,128)(2,1)} %param.25) | copy-start | bytes 4718596
  9.6 10.0 %collective-permute-start.1 = (bf16[96,1536]{1,0:T(8,128)(2,1)S(1)}, bf16[96,1536]{1,0:T(8,128)(2,1)S(1)}, u32[]{:S(2)}, u32[]{:S(2)}) collective-permute-start(bf16[96,1536]{1,0:T(8,128)(2,1)S(1)} %get-tuple-element.301), channel_id=1, source_target_pairs={{0,2},{1,3},{2,0},{3,1},{4,6},{5,7},{6,4},{7,5},{8,10},{9,11},{10,... | collective-permute-start | bytes 884744 | tf_op jit(solution)/shard_map/ppermute | solution.py:527
  21.9 7.7 %copy-start.22 = (bf16[2,3,192]{2,0,1:T(2,128)(2,1)S(1)}, bf16[2,3,192]{2,0,1:T(2,128)(2,1)}, u32[]{:S(2)}) copy-start(bf16[2,3,192]{2,0,1:T(2,128)(2,1)} %param.31) | copy-start | bytes 6916
  21.9 7.7 %copy-start.20 = (bf16[2,2,192]{2,1,0:T(2,128)(2,1)S(1)}, bf16[2,2,192]{2,1,0:T(2,128)(2,1)}, u32[]{:S(2)}) copy-start(bf16[2,2,192]{2,1,0:T(2,128)(2,1)} %param.41) | copy-start | bytes 4612
  21.9 7.7 %copy-start.35 = (s32[2,1,3]{2,1,0:T(1,128)S(1)}, s32[2,1,3]{2,1,0:T(1,128)}, u32[]{:S(2)}) copy-start(s32[2,1,3]{2,1,0:T(1,128)} %param.27) | copy-start | bytes 76
  21.9 8.0 %copy-start.21 = (bf16[2,768]{1,0:T(2,128)(2,1)S(1)}, bf16[2,768]{1,0:T(2,128)(2,1)}, u32[]{:S(2)}) copy-start(bf16[2,768]{1,0:T(2,128)(2,1)} %param.47) | copy-start | bytes 9220
  21.9 8.0 %copy-start.34 = (bf16[2,192]{1,0:T(2,128)(2,1)S(1)}, bf16[2,192]{1,0:T(2,128)(2,1)}, u32[]{:S(2)}) copy-start(bf16[2,192]{1,0:T(2,128)(2,1)} %param.39) | copy-start | bytes 2308
  21.9 9.4 %copy-start.23 = (bf16[2,768]{1,0:T(2,128)(2,1)S(1)}, bf16[2,768]{1,0:T(2,128)(2,1)}, u32[]{:S(2)}) copy-start(bf16[2,768]{1,0:T(2,128)(2,1)} %param.28) | copy-start | bytes 9220
  21.9 9.4 %copy-start.24 = (bf16[2,768]{1,0:T(2,128)(2,1)S(1)}, bf16[2,768]{1,0:T(2,128)(2,1)}, u32[]{:S(2)}) copy-start(bf16[2,768]{1,0:T(2,128)(2,1)} %param.36) | copy-start | bytes 9220
  22.0 10.0 %copy-start.25 = (bf16[2,768]{1,0:T(2,128)(2,1)S(1)}, bf16[2,768]{1,0:T(2,128)(2,1)}, u32[]{:S(2)}) copy-start(bf16[2,768]{1,0:T(2,128)(2,1)} %param.29) | copy-start | bytes 9220
  22.0 10.0 %copy-start.26 = (bf16[2,768]{1,0:T(2,128)(2,1)S(1)}, bf16[2,768]{1,0:T(2,128)(2,1)}, u32[]{:S(2)}) copy-start(bf16[2,768]{1,0:T(2,128)(2,1)} %param.37) | copy-start | bytes 9220
  22.0 24.2 %all-to-all-start.1 = ((bf16[4,256,768]{2,1,0:T(8,128)(2,1)}), bf16[4,256,768]{2,1,0:T(8,128)(2,1)S(1)}, u32[]{:S(2)}, u32[]{:S(2)}) async-start(bf16[4,256,768]{2,1,0:T(8,128)(2,1)} %bitcast.14), calls=%async_computation.1 | async-start | bytes 3145728 | tf_op jit(solution)/shard_map/all_to_all | solution.py:546
  27.6 28.9 %collective-permute-start = (bf16[96,1536]{1,0:T(8,128)(2,1)}, bf16[96,1536]{1,0:T(8,128)(2,1)}, u32[]{:S(2)}, u32[]{:S(2)}) collective-permute-start(bf16[96,1536]{1,0:T(8,128)(2,1)} %get-tuple-element.303), channel_id=1, source_target_pairs={{0,2},{1,3},{2,0},{3,1},{4,6},{5,7},{6,4},{7,5},{8,10},{9,11},{10,... | collective-permute-start | bytes 884744 | tf_op jit(solution)/shard_map/ppermute | solution.py:527
  46.2 24.1 %all-to-all-start = ((bf16[4,259,768]{2,1,0:T(8,128)(2,1)}), bf16[4,259,768]{2,1,0:T(8,128)(2,1)S(1)}, u32[]{:S(2)}, u32[]{:S(2)}) async-start(bf16[4,259,768]{2,1,0:T(8,128)(2,1)} %bitcast.9), calls=%async_computation | async-start | bytes 3244032 | tf_op jit(solution)/shard_map/all_to_all | solution.py:545
  49.8 136.3 %all-gather.7.cloned.1.call-start = ((), (), s32[]{:S(2)}) async-start(), calls=%async_computation.11 | async-start | bytes 10027008 | tf_op jit(solution)/shard_map/all_gather | solution.py:530
  74.2 4.3 copy-start.2
  79.8 4.0 copy-start.27
  79.8 4.6 copy-start.28
  79.8 5.2 %copy-start.29 = (bf16[2,768]{1,0:T(2,128)(2,1)S(1)}, bf16[2,768]{1,0:T(2,128)(2,1)}, u32[]{:S(2)}) copy-start(bf16[2,768]{1,0:T(2,128)(2,1)} %param.49) | copy-start | bytes 9220
  79.8 5.8 %copy-start.30 = (bf16[2,768]{1,0:T(2,128)(2,1)S(1)}, bf16[2,768]{1,0:T(2,128)(2,1)}, u32[]{:S(2)}) copy-start(bf16[2,768]{1,0:T(2,128)(2,1)} %param.33) | copy-start | bytes 9220
  79.8 5.8 %copy-start.31 = (bf16[2,768]{1,0:T(2,128)(2,1)S(1)}, bf16[2,768]{1,0:T(2,128)(2,1)}, u32[]{:S(2)}) copy-start(bf16[2,768]{1,0:T(2,128)(2,1)} %param.34) | copy-start | bytes 9220
  79.8 6.4 %copy-start.32 = (bf16[2,768]{1,0:T(2,128)(2,1)S(1)}, bf16[2,768]{1,0:T(2,128)(2,1)}, u32[]{:S(2)}) copy-start(bf16[2,768]{1,0:T(2,128)(2,1)} %param.35) | copy-start | bytes 9220
  79.8 6.4 %copy-start.33 = (bf16[2,768]{1,0:T(2,128)(2,1)S(1)}, bf16[2,768]{1,0:T(2,128)(2,1)}, u32[]{:S(2)}) copy-start(bf16[2,768]{1,0:T(2,128)(2,1)} %param.43) | copy-start | bytes 9220
  79.9 23.8 %all-to-all-start.2 = ((bf16[4,256,768]{2,1,0:T(8,128)(2,1)}), bf16[4,256,768]{2,1,0:T(8,128)(2,1)S(1)}, u32[]{:S(2)}, u32[]{:S(2)}) async-start(bf16[4,256,768]{2,1,0:T(8,128)(2,1)} %bitcast.31), calls=%async_computation.2 | async-start | bytes 3145728 | tf_op jit(solution)/shard_map/all_to_all | solution.py:547
  83.6 272.9 %reduce-scatter.3.cloned.1.call-start = ((), (), s32[]{:S(2)}) async-start(), calls=%async_computation.8 | async-start | bytes 10027008 | tf_op jit(solution)/shard_map/reduce_scatter | solution.py:628
  229.6 199.6 %reduce-scatter.5.cloned.1.call-start = ((), (), s32[]{:S(2)}) async-start(), calls=%async_computation.9 | async-start | bytes 5013504 | tf_op jit(solution)/shard_map/reduce_scatter | solution.py:628
  323.6 4.7 copy-start.4
  326.5 5.5 %collective-permute-start.2 = (bf16[8,1,96,768]{3,2,0,1:T(8,128)(2,1)}, bf16[8,1,96,768]{3,2,0,1:T(8,128)(2,1)}, u32[]{:S(2)}, u32[]{:S(2)}) collective-permute-start(bf16[8,1,96,768]{3,2,0,1:T(8,128)(2,1)} %get-tuple-element.285), channel_id=1, source_target_pairs={{0,1},{1,0},{2,3},{3,2},{4,5},{5,4},{6,7},{7,6},{8,9},{9,8},{10,11... | collective-permute-start | bytes 3538952 | tf_op jit(solution)/shard_map/ppermute | solution.py:649
  332.0 24.4 %all-to-all-start.3 = ((bf16[4,256,768]{2,1,0:T(8,128)(2,1)}), bf16[4,256,768]{2,1,0:T(8,128)(2,1)S(1)}, u32[]{:S(2)}, u32[]{:S(2)}) async-start(bf16[4,256,768]{2,1,0:T(8,128)(2,1)} %bitcast.37), calls=%async_computation.4 | async-start | bytes 3145728 | tf_op jit(solution)/shard_map/all_to_all | solution.py:727
  338.0 18.4 %collective-permute-start.3 = (bf16[4,1,96,768]{3,2,1,0:T(8,128)(2,1)}, bf16[4,1,96,768]{3,2,1,0:T(8,128)(2,1)S(1)}, u32[]{:S(2)}, u32[]{:S(2)}) collective-permute-start(bf16[4,1,96,768]{3,2,1,0:T(8,128)(2,1)} %fusion.8), channel_id=1, source_target_pairs={{0,4},{4,0},{8,12},{12,8},{16,20},{20,16},{24,28},{28,24},{1,5},{5... | collective-permute-start | bytes 1769480 | tf_op jit(solution)/shard_map/ppermute | solution.py:649
  356.4 6.1 %copy-start.10 = (bf16[1,2,96,1536]{3,2,1,0:T(8,128)(2,1)S(1)}, bf16[1,2,96,1536]{3,2,1,0:T(8,128)(2,1)}, u32[]{:S(2)}) copy-start(bf16[1,2,96,1536]{3,2,1,0:T(8,128)(2,1)} %reduce-scatter.3.cloned.1.call-done) | copy-start | bytes 1769476
  358.5 22.6 %collective-permute-start.5 = (bf16[1,96,768]{2,1,0:T(8,128)(2,1)}, bf16[1,96,768]{2,1,0:T(8,128)(2,1)S(1)}, u32[]{:S(2)}, u32[]{:S(2)}) collective-permute-start(bf16[1,96,768]{2,1,0:T(8,128)(2,1)} %get-tuple-element.279), channel_id=1, source_target_pairs={{0,8},{4,12},{8,16},{12,20},{16,24},{20,28},{24,0},{28,4},{1,9},{5... | collective-permute-start | bytes 442376 | tf_op jit(solution)/shard_map/ppermute | solution.py:663
  358.8 22.4 %collective-permute-start.6 = (bf16[1,96,768]{2,1,0:T(8,128)(2,1)}, bf16[1,96,768]{2,1,0:T(8,128)(2,1)}, u32[]{:S(2)}, u32[]{:S(2)}) collective-permute-start(bf16[1,96,768]{2,1,0:T(8,128)(2,1)} %get-tuple-element.281), channel_id=1, source_target_pairs={{0,16},{4,20},{8,24},{12,28},{16,0},{20,4},{24,8},{28,12},{1,17},{... | collective-permute-start | bytes 442376 | tf_op jit(solution)/shard_map/ppermute | solution.py:663
  360.5 21.3 %collective-permute-start.7 = (bf16[1,96,768]{2,1,0:T(8,128)(2,1)}, bf16[1,96,768]{2,1,0:T(8,128)(2,1)}, u32[]{:S(2)}, u32[]{:S(2)}) collective-permute-start(bf16[1,96,768]{2,1,0:T(8,128)(2,1)} %get-tuple-element.280), channel_id=1, source_target_pairs={{0,24},{4,28},{8,0},{12,4},{16,8},{20,12},{24,16},{28,20},{1,25},{... | collective-permute-start | bytes 442376 | tf_op jit(solution)/shard_map/ppermute | solution.py:663
  363.2 19.8 %collective-permute-start.4 = (bf16[96,1536]{1,0:T(8,128)(2,1)}, bf16[96,1536]{1,0:T(8,128)(2,1)}, u32[]{:S(2)}, u32[]{:S(2)}) collective-permute-start(bf16[96,1536]{1,0:T(8,128)(2,1)} %slice_bitcast_fusion), channel_id=1, source_target_pairs={{0,2},{1,3},{2,0},{3,1},{4,6},{5,7},{6,4},{7,5},{8,10},{9,11},{10,... | collective-permute-start | bytes 884744 | tf_op jit(solution)/shard_map/ppermute | solution.py:667
  381.1 0.7 copy-start.16
  383.0 2.1 copy-start.5
  384.9 4.0 copy-start
  384.9 3.9 collective-permute-start.8
  388.9 1.4 copy-start.6
  390.3 38.9 %all-to-all-start.4 = ((bf16[4,256,768]{2,1,0:T(8,128)(2,1)}), bf16[4,256,768]{2,1,0:T(8,128)(2,1)S(1)}, u32[]{:S(2)}, u32[]{:S(2)}) async-start(bf16[4,256,768]{2,1,0:T(8,128)(2,1)} %bitcast.229), calls=%async_computation.5 | async-start | bytes 3145728 | tf_op jit(solution)/shard_map/all_to_all | solution.py:727
  406.3 3.6 collective-permute-start.9
  406.7 1.3 copy-start.12
  406.7 3.2 copy-start.13
  406.7 3.4 copy-start.11
  407.9 21.2 %collective-permute-start.12 = (bf16[4,1,96,768]{3,2,1,0:T(8,128)(2,1)S(1)}, bf16[4,1,96,768]{3,2,1,0:T(8,128)(2,1)S(1)}, u32[]{:S(2)}, u32[]{:S(2)}) collective-permute-start(bf16[4,1,96,768]{3,2,1,0:T(8,128)(2,1)S(1)} %bitcast.248), channel_id=1, source_target_pairs={{0,4},{4,0},{8,12},{12,8},{16,20},{20,16},{24,28},{28,24},{1,5},{5... | collective-permute-start | bytes 1769480 | tf_op jit(solution)/shard_map/ppermute | solution.py:753
  409.9 15.1 %collective-permute-start.10 = (f32[24,768]{1,0:T(8,128)S(1)}, f32[24,768]{1,0:T(8,128)S(1)}, u32[]{:S(2)}, u32[]{:S(2)}) collective-permute-start(f32[24,768]{1,0:T(8,128)S(1)} %add.634), channel_id=1, source_target_pairs={{0,4},{4,0},{8,12},{12,8},{16,20},{20,16},{24,28},{28,24},{1,5},{5... | collective-permute-start | bytes 221192 | tf_op jit(solution)/shard_map/ppermute | solution.py:770
  411.1 18.0 %collective-permute-start.13 = (bf16[1,96,768]{2,1,0:T(8,128)(2,1)S(1)}, bf16[1,96,768]{2,1,0:T(8,128)(2,1)S(1)}, u32[]{:S(2)}, u32[]{:S(2)}) collective-permute-start(bf16[1,96,768]{2,1,0:T(8,128)(2,1)S(1)} %fusion.32), channel_id=1, source_target_pairs={{0,2},{1,3},{2,0},{3,1},{4,6},{5,7},{6,4},{7,5},{8,10},{9,11},{10,... | collective-permute-start | bytes 442376 | tf_op jit(solution)/shard_map/ppermute | solution.py:667
  425.0 4.0 collective-permute-start.11
  429.1 2.7 copy-start.9
  429.1 2.6 copy-start.7
  429.2 6.5 %copy-start.15 = (bf16[1,2,96,768]{3,2,1,0:T(8,128)(2,1)S(1)}, bf16[1,2,96,768]{3,2,1,0:T(8,128)(2,1)}, u32[]{:S(2)}) copy-start(bf16[1,2,96,768]{3,2,1,0:T(8,128)(2,1)} %reduce-scatter.5.cloned.1.call-done) | copy-start | bytes 884740
  429.2 8.5 %copy-start.3 = (bf16[1024,768]{1,0:T(8,128)(2,1)S(1)}, bf16[1024,768]{1,0:T(8,128)(2,1)}, u32[]{:S(2)}) copy-start(bf16[1024,768]{1,0:T(8,128)(2,1)} %get-tuple-element.165) | copy-start | bytes 4718596
  431.8 17.0 %collective-permute-start.16 = (bf16[144,768]{1,0:T(8,128)(2,1)}, bf16[144,768]{1,0:T(8,128)(2,1)}, u32[]{:S(2)}, u32[]{:S(2)}) collective-permute-start(bf16[144,768]{1,0:T(8,128)(2,1)} %get-tuple-element.323), channel_id=1, source_target_pairs={{0,24},{4,28},{8,0},{12,4},{16,8},{20,12},{24,16},{28,20},{1,25},{... | collective-permute-start | bytes 663560 | tf_op jit(solution)/shard_map/ppermute | solution.py:781
  433.3 18.9 %collective-permute-start.15 = (bf16[144,768]{1,0:T(8,128)(2,1)}, bf16[144,768]{1,0:T(8,128)(2,1)}, u32[]{:S(2)}, u32[]{:S(2)}) collective-permute-start(bf16[144,768]{1,0:T(8,128)(2,1)} %get-tuple-element.322), channel_id=1, source_target_pairs={{0,16},{4,20},{8,24},{12,28},{16,0},{20,4},{24,8},{28,12},{1,17},{... | collective-permute-start | bytes 663560 | tf_op jit(solution)/shard_map/ppermute | solution.py:781
  433.5 19.6 %collective-permute-start.14 = (bf16[144,768]{1,0:T(8,128)(2,1)}, bf16[144,768]{1,0:T(8,128)(2,1)}, u32[]{:S(2)}, u32[]{:S(2)}) collective-permute-start(bf16[144,768]{1,0:T(8,128)(2,1)} %get-tuple-element.321), channel_id=1, source_target_pairs={{0,8},{4,12},{8,16},{12,20},{16,24},{20,28},{24,0},{28,4},{1,9},{5... | collective-permute-start | bytes 663560 | tf_op jit(solution)/shard_map/ppermute | solution.py:781
  435.7 9.3 %collective-permute-start.17 = (bf16[96,768]{1,0:T(8,128)(2,1)S(1)}, bf16[96,768]{1,0:T(8,128)(2,1)}, u32[]{:S(2)}, u32[]{:S(2)}) collective-permute-start(bf16[96,768]{1,0:T(8,128)(2,1)S(1)} %slice_bitcast_fusion.1), channel_id=1, source_target_pairs={{0,2},{1,3},{2,0},{3,1},{4,6},{5,7},{6,4},{7,5},{8,10},{9,11},{10,... | collective-permute-start | bytes 442376 | tf_op jit(solution)/shard_map/ppermute | solution.py:667
  441.4 23.6 %all-to-all-start.5 = ((bf16[4,256,768]{2,1,0:T(8,128)(2,1)}), bf16[4,256,768]{2,1,0:T(8,128)(2,1)S(1)}, u32[]{:S(2)}, u32[]{:S(2)}) async-start(bf16[4,256,768]{2,1,0:T(8,128)(2,1)} %bitcast.231), calls=%async_computation.7 | async-start | bytes 3145728 | tf_op jit(solution)/shard_map/all_to_all | solution.py:727
  448.8 6.1 %copy-start.8 = (bf16[1,96,768]{2,1,0:T(8,128)(2,1)S(1)}, bf16[1,96,768]{2,1,0:T(8,128)(2,1)}, u32[]{:S(2)}) copy-start(bf16[1,96,768]{2,1,0:T(8,128)(2,1)} %copy-done.7) | copy-start | bytes 442372
Sparse Core Ops, SparseCore 0:
  20.7 82.8 all-gather.4
  106.5 79.5 all-gather.6
  229.7 109.4 reduce-scatter.2
  343.4 75.7 reduce-scatter.4
